TPU v7x, 32 devices: a whole 2x2x4 slice. The times are simulated.
32 devices in a mesh: rows: 16 (over z, y, core), seq: 2 (over x).
Axes of the slice: x: 2, y: 2, z: 4, core: 2. Of those that a mesh axis runs over, the one named last changes fastest.
Arguments:
- block_input: bfloat16 [16, 2048, 1024], P('rows', 'seq'), may hold values from -6 to 6
- lengths: int32 [16, 4], P('rows'), may hold values from 1 to 1024, 2048 in all within a row
- norm_gain: bfloat16 [1024], P('rows'), may hold values from 0.099609375 to 1.8984375
- norm_bias: bfloat16 [1024], P('rows'), may hold values from -2 to 2
- w_qkv: bfloat16 [1024, 3072], P('rows'), may hold values from -0.1875 to 0.1875
- w_attn_out: bfloat16 [1024, 1024], P('rows'), may hold values from -0.75 to 0.75
- w_fc_in: bfloat16 [1024, 4096], P('rows'), may hold values from -0.1875 to 0.1875
- b_fc_in: bfloat16 [4096], P('rows'), may hold values from -3 to 3
- w_fc_out: bfloat16 [4096, 1024], P('rows'), may hold values from -0.09375 to 0.09375
- b_fc_out: bfloat16 [1024], P('rows'), may hold values from -2 to 2
- cotangent: bfloat16 [16, 2048, 1024], P('rows', 'seq'), may hold values from -15 to 15
Outputs:
- block_output: bfloat16 [16, 2048, 1024], P('rows', 'seq')
- grad_input: float32 [16, 2048, 1024], P('rows', 'seq')
- grad_norm_gain: float32 [1024], P('rows')
- grad_norm_bias: float32 [1024], P('rows')
- grad_w_qkv: float32 [1024, 3072], P('rows')
- grad_w_attn_out: float32 [1024, 1024], P('rows')
- grad_w_fc_in: float32 [1024, 4096], P('rows')
- grad_b_fc_in: float32 [4096], P('rows')
- grad_w_fc_out: float32 [4096, 1024], P('rows')
- grad_b_fc_out: float32 [1024], P('rows')
Inputs may be any that keep to these rules, and one draw needn't show every extreme that they name: The 4 lengths of a row sum to 2048, and the longest protein of every row has exactly 1024 residues.
All inputs are finite; a program needn't handle non-finite values.
Results may differ from a plain program's by a relative error of at most 0.017.
Values may be sent and summed in bfloat16 or wider, within the bound.
A program may use at most 576 MiB of HBM per device.

v0:
```python
import jax
import jax.numpy as jnp
from jax import lax
from jax.sharding import PartitionSpec as P

HEADS = 16
ROT = 32


EPS = 1e-05
GELU_COEF = 0.7978845608028654


def passed_along(array, axis, by):
    count = lax.axis_size(axis)
    pairs = [(i, i + by) for i in range(count) if 0 <= i + by < count]
    return lax.ppermute(array, axis, pairs)


def normalize(values, norm_gain, norm_bias):
    row_mean = jnp.mean(values, axis=1, keepdims=True)
    centered = values - row_mean
    spread = jnp.mean(centered * centered, axis=1, keepdims=True)
    return centered * lax.rsqrt(spread + EPS) * norm_gain + norm_bias


def gelu_tanh(values):
    return (
        0.5 * values * (1.0 + jnp.tanh(GELU_COEF * (values + 0.044715 * values * values * values)))
    )


def layout(row_lengths, where_at):
    seg_ends = jnp.cumsum(row_lengths, dtype=jnp.int32)
    seg_starts = seg_ends - row_lengths
    segment = jnp.sum(
        (seg_ends[None, :] <= where_at[:, None]).astype(jnp.int32), axis=1, dtype=jnp.int32
    )
    chosen = segment[:, None] == jnp.arange(row_lengths.shape[0], dtype=jnp.int32)[None, :]
    seg_begin = jnp.sum(jnp.where(chosen, seg_starts[None, :], 0), axis=1, dtype=jnp.int32)
    return (segment, where_at - seg_begin)


def rotate(vectors, position):
    tokens = vectors.shape[0]
    head_count = vectors.shape[1]
    half_rot = ROT // 2
    freqs = 10000.0 ** (-2.0 * jnp.arange(half_rot, dtype=jnp.float32) / ROT)
    angles = position.astype(jnp.float32)[:, None] * freqs[None, :]
    cosine = jnp.cos(angles)[:, None, :]
    sine = jnp.sin(angles)[:, None, :]
    paired = vectors[:, :, :ROT].reshape(tokens, head_count, half_rot, 2)
    evens = paired[..., 0]
    odds = paired[..., 1]
    turned = jnp.stack([evens * cosine - odds * sine, odds * cosine + evens * sine], axis=-1)
    return jnp.concatenate([turned.reshape(tokens, head_count, ROT), vectors[:, :, ROT:]], axis=2)


def block_scores(query_block, key_block, allowed, score_scale):
    scores = (
        jnp.einsum("qhd,khd->hqk", query_block, key_block, preferred_element_type=jnp.float32)
        * score_scale
    )
    return jnp.where(allowed[None], scores, -1e30)


def reduce_mlp(terms):
    shares = (
        lax.psum_scatter(
            terms[0].astype(jnp.bfloat16), "rows", scatter_dimension=0, tiled=True
        ).astype(jnp.float32),
        lax.psum_scatter(
            terms[1].astype(jnp.bfloat16), "rows", scatter_dimension=0, tiled=True
        ).astype(jnp.float32),
        lax.psum_scatter(
            terms[2].astype(jnp.bfloat16), "rows", scatter_dimension=0, tiled=True
        ).astype(jnp.float32),
        lax.psum_scatter(
            terms[3].astype(jnp.bfloat16), "rows", scatter_dimension=0, tiled=True
        ).astype(jnp.float32),
    )
    return (
        lax.psum(shares[0].astype(jnp.bfloat16), "seq").astype(jnp.float32),
        lax.psum(shares[1].astype(jnp.bfloat16), "seq").astype(jnp.float32),
        lax.psum(shares[2].astype(jnp.bfloat16), "seq").astype(jnp.float32),
        lax.psum(shares[3].astype(jnp.bfloat16), "seq").astype(jnp.float32),
    )


def reduce_attn(terms):
    shares = (
        lax.psum_scatter(
            terms[0].astype(jnp.bfloat16), "rows", scatter_dimension=0, tiled=True
        ).astype(jnp.float32),
        lax.psum_scatter(
            terms[1].astype(jnp.bfloat16), "rows", scatter_dimension=0, tiled=True
        ).astype(jnp.float32),
        lax.psum_scatter(
            terms[2].astype(jnp.bfloat16), "rows", scatter_dimension=0, tiled=True
        ).astype(jnp.float32),
        lax.psum_scatter(
            terms[3].astype(jnp.bfloat16), "rows", scatter_dimension=0, tiled=True
        ).astype(jnp.float32),
    )
    return (
        lax.psum(shares[0].astype(jnp.bfloat16), "seq").astype(jnp.float32),
        lax.psum(shares[1].astype(jnp.bfloat16), "seq").astype(jnp.float32),
        lax.psum(shares[2].astype(jnp.bfloat16), "seq").astype(jnp.float32),
        lax.psum(shares[3].astype(jnp.bfloat16), "seq").astype(jnp.float32),
    )


def body(
    block_input,
    lengths,
    norm_gain,
    norm_bias,
    w_qkv,
    w_attn_out,
    w_fc_in,
    b_fc_in,
    w_fc_out,
    b_fc_out,
    cotangent,
):
    gain_all, bias_all, w_qkv_all, w_out_all = (
        lax.all_gather(norm_gain, "rows", axis=0, tiled=True),
        lax.all_gather(norm_bias, "rows", axis=0, tiled=True),
        lax.all_gather(w_qkv, "rows", axis=0, tiled=True),
        lax.all_gather(w_attn_out, "rows", axis=0, tiled=True),
    )
    w_in_all, b_in_all, w_back_all, b_back_all = (
        lax.all_gather(w_fc_in, "rows", axis=0, tiled=True),
        lax.all_gather(b_fc_in, "rows", axis=0, tiled=True),
        lax.all_gather(w_fc_out, "rows", axis=0, tiled=True),
        lax.all_gather(b_fc_out, "rows", axis=0, tiled=True),
    )
    model_width = gain_all.shape[0]
    head_dim = model_width // HEADS
    inputs = block_input[0].astype(jnp.float32)
    tokens = inputs.shape[0]
    first_index = lax.axis_index("seq") * tokens
    own_index = first_index + jnp.arange(tokens, dtype=jnp.int32)
    prior_index = own_index - tokens
    own_segment, own_position = layout(lengths[0], own_index)
    prior_segment, prior_position = layout(lengths[0], prior_index)
    normed_f, norm_pull = jax.vjp(
        normalize, inputs, gain_all.astype(jnp.float32), bias_all.astype(jnp.float32)
    )
    normed = normed_f.astype(jnp.bfloat16)
    mixed = jnp.dot(normed, w_qkv_all, preferred_element_type=jnp.float32)
    queries = rotate(mixed[:, :model_width].reshape(tokens, HEADS, head_dim), own_position).astype(
        jnp.bfloat16
    )
    keys_own = (
        rotate(
            mixed[:, model_width : 2 * model_width].reshape(tokens, HEADS, head_dim), own_position
        )
        .astype(jnp.bfloat16)
        .reshape(tokens, model_width)
    )
    values_own = mixed[:, 2 * model_width :].astype(jnp.bfloat16)
    prior_keys, prior_values = passed_along((keys_own, values_own), "seq", 1)
    pre = jnp.dot(normed, w_in_all, preferred_element_type=jnp.float32) + b_in_all.astype(
        jnp.float32
    )
    hidden_f, gelu_pull = jax.vjp(gelu_tanh, pre)
    hidden = hidden_f.astype(jnp.bfloat16)
    mlp_out = jnp.dot(hidden, w_back_all, preferred_element_type=jnp.float32) + b_back_all.astype(
        jnp.float32
    )
    keys_both = jnp.concatenate([prior_keys, keys_own], axis=0).reshape(2 * tokens, HEADS, head_dim)
    values_both = jnp.concatenate([prior_values, values_own], axis=0).reshape(
        2 * tokens, HEADS, head_dim
    )
    key_index = jnp.concatenate([prior_index, own_index])
    key_segment = jnp.concatenate([prior_segment, own_segment])
    block_rows = min(512, tokens)
    group_size = HEADS // 2
    score_scale = head_dim ** (-0.5)
    starts_list = list(range(0, tokens, block_rows))
    masks = []
    for begin_row in starts_list:
        q_index = own_index[begin_row : begin_row + block_rows]
        q_segment = own_segment[begin_row : begin_row + block_rows]
        masks.append(
            (q_segment[:, None] == key_segment[None, :])
            & (q_index[:, None] >= key_index[None, :])
            & (key_index[None, :] >= 0)
        )
    out_rows = []
    saved_lse = []
    for block_number, begin_row in enumerate(starts_list):
        head_pieces = []
        for head_low in range(0, HEADS, group_size):
            scores = block_scores(
                queries[begin_row : begin_row + block_rows, head_low : head_low + group_size],
                keys_both[:, head_low : head_low + group_size],
                masks[block_number],
                score_scale,
            )
            row_max = jnp.max(scores, axis=2, keepdims=True)
            exps = jnp.exp(scores - row_max)
            row_total = jnp.sum(exps, axis=2, keepdims=True)
            saved_lse.append(row_max + jnp.log(row_total))
            head_pieces.append(
                jnp.einsum(
                    "hqk,khd->qhd",
                    (exps / row_total).astype(jnp.bfloat16),
                    values_both[:, head_low : head_low + group_size],
                    preferred_element_type=jnp.float32,
                )
            )
        out_rows.append(jnp.concatenate(head_pieces, axis=1))
    attended = jnp.concatenate(out_rows, axis=0).reshape(tokens, model_width).astype(jnp.bfloat16)
    branch = jnp.dot(attended, w_out_all, preferred_element_type=jnp.float32)
    block_output = (inputs + branch + mlp_out).astype(jnp.bfloat16)[None]
    grad_out = cotangent[0]
    grad_w_back = jnp.dot(hidden.T, grad_out, preferred_element_type=jnp.float32)
    grad_b_back = jnp.sum(grad_out.astype(jnp.float32), axis=0)
    d_pre = gelu_pull(jnp.dot(grad_out, w_back_all.T, preferred_element_type=jnp.float32))[
        0
    ].astype(jnp.bfloat16)
    grad_w_in = jnp.dot(normed.T, d_pre, preferred_element_type=jnp.float32)
    grad_b_in = jnp.sum(d_pre.astype(jnp.float32), axis=0)
    d_normed = jnp.dot(d_pre, w_in_all.T, preferred_element_type=jnp.float32)
    mlp_grads = reduce_mlp((grad_w_in, grad_b_in, grad_w_back, grad_b_back))
    grad_w_out = jnp.dot(attended.T, grad_out, preferred_element_type=jnp.float32)
    d_attended = (
        jnp.dot(grad_out, w_out_all.T, preferred_element_type=jnp.float32)
        .astype(jnp.bfloat16)
        .reshape(tokens, HEADS, head_dim)
    )
    d_keys_both = jnp.zeros((2 * tokens, HEADS, head_dim), jnp.float32)
    d_values_both = jnp.zeros((2 * tokens, HEADS, head_dim), jnp.float32)
    d_query_rows = []
    lse_number = 0
    for block_number, begin_row in enumerate(starts_list):
        head_pieces = []
        for head_low in range(0, HEADS, group_size):
            query_part = queries[
                begin_row : begin_row + block_rows, head_low : head_low + group_size
            ]
            key_part = keys_both[:, head_low : head_low + group_size]
            value_part = values_both[:, head_low : head_low + group_size]
            d_out_block = d_attended[
                begin_row : begin_row + block_rows, head_low : head_low + group_size
            ]
            scores = block_scores(query_part, key_part, masks[block_number], score_scale)
            probs = jnp.exp(scores - saved_lse[lse_number])
            lse_number = lse_number + 1
            d_probs = jnp.einsum(
                "qhd,khd->hqk", d_out_block, value_part, preferred_element_type=jnp.float32
            )
            row_delta = jnp.sum(probs * d_probs, axis=2, keepdims=True)
            d_scores = (probs * (d_probs - row_delta)).astype(jnp.bfloat16)
            head_pieces.append(
                jnp.einsum("hqk,khd->qhd", d_scores, key_part, preferred_element_type=jnp.float32)
                * score_scale
            )
            d_keys_both = d_keys_both.at[:, head_low : head_low + group_size].add(
                jnp.einsum("hqk,qhd->khd", d_scores, query_part, preferred_element_type=jnp.float32)
                * score_scale
            )
            d_values_both = d_values_both.at[:, head_low : head_low + group_size].add(
                jnp.einsum(
                    "hqk,qhd->khd",
                    probs.astype(jnp.bfloat16),
                    d_out_block,
                    preferred_element_type=jnp.float32,
                )
            )
        d_query_rows.append(jnp.concatenate(head_pieces, axis=1))
    d_queries = jnp.concatenate(d_query_rows, axis=0)
    back_keys, back_values = (
        passed_along(
            d_keys_both[:tokens].reshape(tokens, model_width).astype(jnp.bfloat16), "seq", -1
        ).astype(jnp.float32),
        passed_along(
            d_values_both[:tokens].reshape(tokens, model_width).astype(jnp.bfloat16), "seq", -1
        ).astype(jnp.float32),
    )
    d_keys = d_keys_both[tokens:].reshape(tokens, model_width) + back_keys
    d_values = d_values_both[tokens:].reshape(tokens, model_width) + back_values
    d_mixed = jnp.concatenate(
        [
            rotate(d_queries, -own_position).reshape(tokens, model_width),
            rotate(d_keys.reshape(tokens, HEADS, head_dim), -own_position).reshape(
                tokens, model_width
            ),
            d_values,
        ],
        axis=1,
    ).astype(jnp.bfloat16)
    grad_w_qkv_local = jnp.dot(normed.T, d_mixed, preferred_element_type=jnp.float32)
    d_normed = d_normed + jnp.dot(d_mixed, w_qkv_all.T, preferred_element_type=jnp.float32)
    d_inputs, grad_gain_local, grad_bias_local = norm_pull(d_normed)
    grad_input = (d_inputs + grad_out.astype(jnp.float32))[None]
    attn_grads = reduce_attn((grad_gain_local, grad_bias_local, grad_w_qkv_local, grad_w_out))
    return (
        block_output,
        grad_input,
        attn_grads[0],
        attn_grads[1],
        attn_grads[2],
        attn_grads[3],
        mlp_grads[0],
        mlp_grads[1],
        mlp_grads[2],
        mlp_grads[3],
    )


def solution(mesh):
    in_specs = (
        P("rows", "seq", None),
        P("rows", None),
        P("rows"),
        P("rows"),
        P("rows", None),
        P("rows", None),
        P("rows", None),
        P("rows"),
        P("rows", None),
        P("rows"),
        P("rows", "seq", None),
    )
    out_specs = (
        P("rows", "seq", None),
        P("rows", "seq", None),
        P("rows"),
        P("rows"),
        P("rows", None),
        P("rows", None),
        P("rows", None),
        P("rows"),
        P("rows", None),
        P("rows"),
    )
    return jax.shard_map(body, mesh=mesh, in_specs=in_specs, out_specs=out_specs, check_vma=False)
```

profile of v0, /device:TPU:0, one launch (start us, length us, event | category | flops | bytes accessed | tf_op | source)
XLA Modules:
  0.0 1209.8 jit_solution(14482127710197912616)
XLA Ops:
  15.2 35.6 %all-reduce.8 = (bf16[1024]{0:T(1024)(128)(2,1)S(1)}, bf16[1024]{0:T(1024)(128)(2,1)S(1)}) all-reduce(bf16[1024]{0:T(1024)(128)(2,1)S(1)} %dynamic-update-slice.25, bf16[1024]{0:T(1024)(128)(2,1)S(1)} %dynamic-update-slice.24), channel_id=1, replica_groups=mesh['rows'=16,'seq'=2] {'rows'}, use_global_device_ids=true, to_apply=%add.1 | all-reduce | flops 2048 | bytes 8192
  55.5 19.3 %all-gather.6.cloned.1.call-done = bf16[1024,3072]{1,0:T(8,128)(2,1)} async-done(((bf16[64,3072]{1,0:T(8,128)(2,1)}), bf16[1024,3072]{1,0:T(8,128)(2,1)}) %all-gather.6.cloned.1.call-update) | async-done | bytes 6291472 | tf_op jit(solution)/shard_map/all_gather | solution.py:129
  74.8 9.0 fusion.135
  89.7 5.5 copy.47
  99.9 4.7 collective-permute-start
  117.1 5.3 fusion.77
  122.4 5.4 copy.44
  134.1 15.4 %collective-permute-done = bf16[1024,1024]{1,0:T(8,128)(2,1)} collective-permute-done((bf16[1024,1024]{1,0:T(8,128)(2,1)}, bf16[1024,1024]{1,0:T(8,128)(2,1)}, u32[]{:S(2)}, u32[]{:S(2)}) %collective-permute-start) | collective-permute-done | bytes 2097184 | tf_op jit(solution)/shard_map/ppermute | solution.py:17
  149.5 4.7 pad_maximum_fusion.4
  154.2 6.5 copy.43
  160.7 33.1 %collective-permute-done.1 = bf16[1024,1024]{0,1:T(8,128)(2,1)} collective-permute-done((bf16[1024,1024]{0,1:T(8,128)(2,1)}, bf16[1024,1024]{0,1:T(8,128)(2,1)}, u32[]{:S(2)}, u32[]{:S(2)}) %collective-permute-start.1) | collective-permute-done | bytes 2097184 | tf_op jit(solution)/shard_map/ppermute | solution.py:17
  193.8 16.1 %fusion.143 = (f32[8,512]{1,0:T(8,128)S(1)}, f32[8,512,2048]{2,1,0:T(8,128)}) fusion(bf16[1024,16,64]{0,2,1:T(8,128)(2,1)} %bitcast.14, bf16[1024,16,64]{0,2,1:T(8,128)(2,1)} %maximum_convert_fusion, bf16[1024,16,32]{0,2,1:T(8,128)(2,1)S(1)} %copy.50, bf16[1024,16,32]{0,2,1:T(8,128)(2,1)S(1)} %slice.506, pred[512,2048]{1,0:T(8,128)(4,1)} %get-tuple-element.140), kind=kOutput, calls=%fused_computation.223 | convolution fusion | flops 1104146432 | bytes 40910848 | tf_op jit(solution)/shard_map/qhd,khd->hqk/dot_general | solution.py:61
  209.8 15.8 %fusion.142 = (f32[8,512]{1,0:T(8,128)S(1)}, f32[8,512,2048]{2,1,0:T(8,128)}) fusion(bf16[512,8,64]{0,2,1:T(8,128)(2,1)S(1)} %pad_maximum_fusion.16, bf16[1024,16,64]{0,2,1:T(8,128)(2,1)} %bitcast.14, bf16[1024,16,64]{0,2,1:T(8,128)(2,1)} %maximum_convert_fusion, pred[512,2048]{1,0:T(8,128)(4,1)S(1)} %copy-done.24), kind=kOutput, calls=%fused_computation.222 | convolution fusion | flops 1103097856 | bytes 39337984 | tf_op jit(solution)/shard_map/qhd,khd->hqk/dot_general | solution.py:61
  225.7 14.5 %fusion.3 = f32[8,512]{1,0:T(8,128)S(1)} fusion(f32[8,512,2048]{2,1,0:T(8,128)} %get-tuple-element.156, f32[8,512]{1,0:T(8,128)S(1)} %get-tuple-element.155), kind=kLoop, calls=%fused_computation.27 | loop fusion | flops 16773120 | bytes 33587200 | tf_op jit(solution)/shard_map/reduce_sum | solution.py:204
  240.8 15.2 %fusion.97 = bf16[512,8,64]{0,2,1:T(8,128)(2,1)} fusion(bf16[2048,16,64]{0,2,1:T(8,128)(2,1)} %bitcast.172, f32[8,512,2048]{2,1,0:T(8,128)} %get-tuple-element.156, f32[8,512]{1,0:T(8,128)S(1)} %fusion.3, f32[8,512]{1,0:T(8,128)S(1)} %get-tuple-element.155), kind=kOutput, calls=%fused_computation.156 | convolution fusion | flops 1098907648 | bytes 38305792 | tf_op jit(solution)/shard_map/hqk,khd->qhd/dot_general | solution.py:207
  256.0 13.8 %fusion.2 = f32[8,512]{1,0:T(8,128)S(1)} fusion(f32[8,512,2048]{2,1,0:T(8,128)} %get-tuple-element.158, f32[8,512]{1,0:T(8,128)S(1)} %get-tuple-element.157), kind=kLoop, calls=%fused_computation.26 | loop fusion | flops 16773120 | bytes 33587200 | tf_op jit(solution)/shard_map/reduce_sum | solution.py:204
  269.8 15.1 %fusion.98 = bf16[512,8,64]{0,2,1:T(8,128)(2,1)} fusion(bf16[2048,16,64]{0,2,1:T(8,128)(2,1)} %bitcast.173, f32[8,512,2048]{2,1,0:T(8,128)} %get-tuple-element.158, f32[8,512]{1,0:T(8,128)S(1)} %fusion.2, f32[8,512]{1,0:T(8,128)S(1)} %get-tuple-element.157), kind=kOutput, calls=%fused_computation.157 | convolution fusion | flops 1098907648 | bytes 38305792 | tf_op jit(solution)/shard_map/hqk,khd->qhd/dot_general | solution.py:207
  284.9 15.7 %fusion.145 = (f32[8,512]{1,0:T(8,128)S(1)}, f32[8,512,2048]{2,1,0:T(8,128)}) fusion(bf16[1024,16,64]{0,2,1:T(8,128)(2,1)} %bitcast.14, bf16[1024,16,64]{0,2,1:T(8,128)(2,1)} %maximum_convert_fusion, bf16[1024,16,32]{0,2,1:T(8,128)(2,1)S(1)} %copy.50, bf16[1024,16,32]{0,2,1:T(8,128)(2,1)S(1)} %slice.506, pred[512,2048]{1,0:T(8,128)(4,1)} %get-tuple-element.139), kind=kOutput, calls=%fused_computation.225 | convolution fusion | flops 1104146432 | bytes 40910848 | tf_op jit(solution)/shard_map/qhd,khd->hqk/dot_general | solution.py:61
  300.6 15.7 %fusion.144 = (f32[8,512]{1,0:T(8,128)S(1)}, f32[8,512,2048]{2,1,0:T(8,128)}) fusion(bf16[1024,16,64]{0,2,1:T(8,128)(2,1)} %bitcast.14, bf16[1024,16,64]{0,2,1:T(8,128)(2,1)} %maximum_convert_fusion, bf16[1024,16,32]{0,2,1:T(8,128)(2,1)S(1)} %copy.50, bf16[1024,16,32]{0,2,1:T(8,128)(2,1)S(1)} %slice.506, pred[512,2048]{1,0:T(8,128)(4,1)} %get-tuple-element.139), kind=kOutput, calls=%fused_computation.224 | convolution fusion | flops 1104146432 | bytes 40910848 | tf_op jit(solution)/shard_map/qhd,khd->hqk/dot_general | solution.py:61
  316.3 22.7 %multiply_reduce_fusion.1 = (f32[8,512]{1,0:T(8,128)}, f32[8,512,2048]{2,1,0:T(8,128)}) fusion(f32[8,512,2048]{2,1,0:T(8,128)} %get-tuple-element.158, f32[8,512]{1,0:T(8,128)S(1)} %log_add_fusion.1, bf16[2048,16,64]{0,2,1:T(8,128)(2,1)S(1)} %bitcast.176, bf16[1024,16,64]{0,2,1:T(8,128)(2,1)S(1)} %bitcast.182), kind=kOutput, calls=%fused_computation.4 | convolution fusion | flops 1098903552 | bytes 69763072 | tf_op jit(solution)/shard_map/qhd,khd->hqk/dot_general | solution.py:252
  339.0 22.7 %multiply_reduce_fusion = (f32[8,512]{1,0:T(8,128)}, f32[8,512,2048]{2,1,0:T(8,128)}) fusion(f32[8,512,2048]{2,1,0:T(8,128)} %get-tuple-element.156, f32[8,512]{1,0:T(8,128)S(1)} %copy-done.27, bf16[2048,16,64]{0,2,1:T(8,128)(2,1)S(1)} %bitcast.177, bf16[1024,16,64]{0,2,1:T(8,128)(2,1)S(1)} %bitcast.183), kind=kOutput, calls=%fused_computation.1 | convolution fusion | flops 1098903552 | bytes 69763072 | tf_op jit(solution)/shard_map/qhd,khd->hqk/dot_general | solution.py:252
  361.7 13.7 %fusion = f32[8,512]{1,0:T(8,128)S(1)} fusion(f32[8,512,2048]{2,1,0:T(8,128)} %get-tuple-element.162, f32[8,512]{1,0:T(8,128)S(1)} %get-tuple-element.161), kind=kLoop, calls=%fused_computation.24 | loop fusion | flops 16773120 | bytes 33587200 | tf_op jit(solution)/shard_map/reduce_sum | solution.py:204
  375.4 13.5 %fusion.50 = f32[2048,8,64]{0,2,1:T(8,128)S(1)} fusion(f32[8,512,2048]{2,1,0:T(8,128)} %get-tuple-element.162, f32[8,512]{1,0:T(8,128)S(1)} %log_add_fusion.3, bf16[1024,16,64]{0,2,1:T(8,128)(2,1)S(1)} %bitcast.184), kind=kOutput, calls=%fused_computation.106 | convolution fusion | flops 1090519040 | bytes 38289408 | tf_op jit(solution)/shard_map/hqk,qhd->khd/dot_general | solution.py:266
  389.0 13.6 %fusion.1 = f32[8,512]{1,0:T(8,128)S(1)} fusion(f32[8,512,2048]{2,1,0:T(8,128)} %get-tuple-element.160, f32[8,512]{1,0:T(8,128)S(1)} %get-tuple-element.159), kind=kLoop, calls=%fused_computation.25 | loop fusion | flops 16773120 | bytes 33587200 | tf_op jit(solution)/shard_map/reduce_sum | solution.py:204
  402.6 15.3 %fusion.53 = f32[2048,8,64]{0,2,1:T(8,128)} fusion(f32[8,512,2048]{2,1,0:T(8,128)} %get-tuple-element.160, f32[8,512]{1,0:T(8,128)S(1)} %log_add_fusion.2, bf16[1024,16,64]{0,2,1:T(8,128)(2,1)S(1)} %bitcast.185), kind=kOutput, calls=%fused_computation.107 | convolution fusion | flops 1090519040 | bytes 38289408 | tf_op jit(solution)/shard_map/hqk,qhd->khd/dot_general | solution.py:266
  417.9 6.5 pad_maximum_fusion.1
  424.4 16.1 %fusion.48 = f32[2048,16,64]{0,2,1:T(8,128)} fusion(f32[2048,16,64]{0,2,1:T(8,128)} %pad_maximum_fusion.1, f32[2048,8,64]{0,2,1:T(8,128)S(1)} %fusion.50, f32[8,512,2048]{2,1,0:T(8,128)} %get-tuple-element.158, f32[8,512]{1,0:T(8,128)S(1)} %log_add_fusion.1, bf16[1024,16,64]{0,2,1:T(8,128)(2,1)} %bitcast.180), kind=kOutput, calls=%fused_computation.97 | convolution fusion | flops 1091567616 | bytes 42483712 | tf_op jit(solution)/shard_map/hqk,qhd->khd/dot_general | solution.py:266
  440.5 16.7 %fusion.45 = f32[2048,16,64]{0,2,1:T(8,128)} fusion(f32[2048,16,64]{0,2,1:T(8,128)} %fusion.48, f32[8,512,2048]{2,1,0:T(8,128)} %get-tuple-element.156, f32[8,512]{1,0:T(8,128)S(1)} %copy-done.27, bf16[1024,16,64]{0,2,1:T(8,128)(2,1)} %bitcast.181), kind=kOutput, calls=%fused_computation.86 | convolution fusion | flops 1091567616 | bytes 42483712 | tf_op jit(solution)/shard_map/hqk,qhd->khd/dot_general | solution.py:266
  461.1 4.9 slice.397
  466.0 22.5 %multiply_reduce_fusion.2 = (f32[8,512]{1,0:T(8,128)S(1)}, f32[8,512,2048]{2,1,0:T(8,128)}) fusion(f32[8,512,2048]{2,1,0:T(8,128)} %get-tuple-element.160, f32[8,512]{1,0:T(8,128)S(1)} %log_add_fusion.2, bf16[2048,16,64]{0,2,1:T(8,128)(2,1)S(1)} %bitcast.178, bf16[1024,16,64]{0,2,1:T(8,128)(2,1)S(1)} %bitcast.186), kind=kOutput, calls=%fused_computation.7 | convolution fusion | flops 1098903552 | bytes 69763072 | tf_op jit(solution)/shard_map/qhd,khd->hqk/dot_general | solution.py:252
  488.5 22.2 %multiply_reduce_fusion.3 = (f32[8,512]{1,0:T(8,128)S(1)}, f32[8,512,2048]{2,1,0:T(8,128)}) fusion(f32[8,512,2048]{2,1,0:T(8,128)} %get-tuple-element.162, f32[8,512]{1,0:T(8,128)S(1)} %log_add_fusion.3, bf16[2048,16,64]{0,2,1:T(8,128)(2,1)S(1)} %bitcast.179, bf16[1024,16,64]{0,2,1:T(8,128)(2,1)S(1)} %bitcast.187), kind=kOutput, calls=%fused_computation.10 | convolution fusion | flops 1098903552 | bytes 69763072 | tf_op jit(solution)/shard_map/qhd,khd->hqk/dot_general | solution.py:252
  510.6 27.8 %multiply_convert_fusion.1 = bf16[8,512,2048]{2,1,0:T(8,128)(2,1)} fusion(f32[8,512,2048]{2,1,0:T(8,128)} %get-tuple-element.168, f32[8,512,2048]{2,1,0:T(8,128)} %get-tuple-element.158, f32[8,512]{1,0:T(8,128)S(1)} %copy-done.41, f32[8,512]{1,0:T(8,128)S(1)} %log_add_fusion.1), kind=kLoop, calls=%fused_computation.3 | loop fusion | flops 33554432 | bytes 83918848 | tf_op jit(solution)/shard_map/convert_element_type | solution.py:256
  538.5 12.6 %fusion.95 = f32[512,8,64]{0,2,1:T(8,128)} fusion(bf16[8,512,2048]{2,1,0:T(8,128)(2,1)} %multiply_convert_fusion.1, bf16[1024,16,64]{0,2,1:T(8,128)(2,1)} %maximum_convert_fusion, bf16[1024,16,64]{0,2,1:T(8,128)(2,1)} %bitcast.14), kind=kOutput, calls=%fused_computation.154 | convolution fusion | flops 1082392576 | bytes 22020096 | tf_op jit(solution)/shard_map/hqk,khd->qhd/dot_general | solution.py:258
  551.1 28.0 %multiply_convert_fusion = bf16[8,512,2048]{2,1,0:T(8,128)(2,1)} fusion(f32[8,512,2048]{2,1,0:T(8,128)} %get-tuple-element.170, f32[8,512,2048]{2,1,0:T(8,128)} %get-tuple-element.156, f32[8,512]{1,0:T(8,128)S(1)} %copy-done.40, f32[8,512]{1,0:T(8,128)S(1)} %copy-done.27), kind=kLoop, calls=%fused_computation | loop fusion | flops 33554432 | bytes 83918848 | tf_op jit(solution)/shard_map/convert_element_type | solution.py:256
  579.1 12.6 %fusion.96 = f32[512,8,64]{0,2,1:T(8,128)} fusion(bf16[8,512,2048]{2,1,0:T(8,128)(2,1)} %multiply_convert_fusion, bf16[1024,16,64]{0,2,1:T(8,128)(2,1)} %maximum_convert_fusion, bf16[1024,16,64]{0,2,1:T(8,128)(2,1)} %bitcast.14), kind=kOutput, calls=%fused_computation.155 | convolution fusion | flops 1082392576 | bytes 22020096 | tf_op jit(solution)/shard_map/hqk,khd->qhd/dot_general | solution.py:258
  591.7 28.0 %multiply_convert_fusion.2 = bf16[8,512,2048]{2,1,0:T(8,128)(2,1)} fusion(f32[8,512,2048]{2,1,0:T(8,128)} %get-tuple-element.164, f32[8,512,2048]{2,1,0:T(8,128)} %get-tuple-element.160, f32[8,512]{1,0:T(8,128)S(1)} %get-tuple-element.163, f32[8,512]{1,0:T(8,128)S(1)} %log_add_fusion.2), kind=kLoop, calls=%fused_computation.6 | loop fusion | flops 33554432 | bytes 83918848 | tf_op jit(solution)/shard_map/convert_element_type | solution.py:256
  619.7 10.8 multiply_bitcast_fusion
  630.4 28.0 %multiply_convert_fusion.3 = bf16[8,512,2048]{2,1,0:T(8,128)(2,1)} fusion(f32[8,512,2048]{2,1,0:T(8,128)} %get-tuple-element.166, f32[8,512,2048]{2,1,0:T(8,128)} %get-tuple-element.162, f32[8,512]{1,0:T(8,128)S(1)} %get-tuple-element.165, f32[8,512]{1,0:T(8,128)S(1)} %log_add_fusion.3), kind=kLoop, calls=%fused_computation.9 | loop fusion | flops 33554432 | bytes 83918848 | tf_op jit(solution)/shard_map/convert_element_type | solution.py:256
  658.4 8.9 multiply_bitcast_fusion.1
  667.4 6.6 pad_maximum_fusion
  673.9 11.0 fusion.49
  685.0 7.3 fusion.46
  697.5 11.6 fusion.94
  709.1 15.5 %fusion.100 = bf16[512,8,64]{0,2,1:T(8,128)(2,1)} fusion(bf16[2048,16,64]{0,2,1:T(8,128)(2,1)} %bitcast.174, f32[8,512,2048]{2,1,0:T(8,128)} %get-tuple-element.162, f32[8,512]{1,0:T(8,128)S(1)} %copy-done.37, f32[8,512]{1,0:T(8,128)S(1)} %copy-done.33), kind=kOutput, calls=%fused_computation.159 | convolution fusion | flops 1098907648 | bytes 38305792 | tf_op jit(solution)/shard_map/hqk,khd->qhd/dot_general | solution.py:207
  724.7 15.0 %fusion.99 = bf16[512,8,64]{0,2,1:T(8,128)(2,1)} fusion(bf16[2048,16,64]{0,2,1:T(8,128)(2,1)} %bitcast.175, f32[8,512,2048]{2,1,0:T(8,128)} %get-tuple-element.160, f32[8,512]{1,0:T(8,128)S(1)} %copy-done.35, f32[8,512]{1,0:T(8,128)S(1)} %copy-done.31), kind=kOutput, calls=%fused_computation.158 | convolution fusion | flops 1098907648 | bytes 38305792 | tf_op jit(solution)/shard_map/hqk,khd->qhd/dot_general | solution.py:207
  739.7 12.7 %fusion.93 = f32[512,8,64]{0,2,1:T(8,128)} fusion(bf16[8,512,2048]{2,1,0:T(8,128)(2,1)} %multiply_convert_fusion.3, bf16[1024,16,64]{0,2,1:T(8,128)(2,1)} %maximum_convert_fusion, bf16[1024,16,64]{0,2,1:T(8,128)(2,1)} %bitcast.14), kind=kOutput, calls=%fused_computation.152 | convolution fusion | flops 1082392576 | bytes 22020096 | tf_op jit(solution)/shard_map/hqk,khd->qhd/dot_general | solution.py:258
  754.5 4.7 slice.390
  778.8 8.5 subtract_convert_fusion.1
  803.1 6.5 collective-permute-done.3
  813.8 12.3 %convolution_convert_fusion.2 = bf16[1024,3072]{1,0:T(8,128)(2,1)} fusion(bf16[1024,1024]{0,1:T(8,128)(2,1)} %fusion.47, bf16[1024,1024]{0,1:T(8,128)(2,1)} %bitcast.202, bf16[1024,1024]{0,1:T(8,128)(2,1)S(1)} %bitcast.200, bf16[1,1024,1024]{2,1,0:T(8,128)(2,1)S(1)} %copy-done.3, f32[1024]{0:T(1024)S(1)} %copy-done.49, f32[1024]{0:T(1024)S(1)} %copy-done.43, ...), kind=kOutput, calls=%fused_computation.61 | convolution fusion | flops 6470762496 | bytes 14696448 | tf_op jit(solution)/shard_map/dot_general | solution.py:295
  826.7 19.3 %all-gather = bf16[16,1,256]{2,1,0:T(2,128)(2,1)S(1)} all-gather(bf16[1,1,256]{2,1,0:T(2,128)(2,1)S(1)} %reshape.707), channel_id=1, replica_groups=mesh['rows'=16,'seq'=2] {'rows'}, dimensions={0}, use_global_device_ids=true | all-gather | bytes 8704 | tf_op jit(solution)/shard_map/all_gather | solution.py:134
  846.0 15.9 %fusion.133 = f32[1024,4096]{1,0:T(8,128)} fusion(bf16[1024,4096]{1,0:T(8,128)(2,1)} %all-gather.10.cloned.1.call-done, bf16[1,1024,1024]{2,1,0:T(8,128)(2,1)S(1)} %copy-done.3, f32[1024]{0:T(1024)S(1)} %copy-done.49, f32[1024]{0:T(1024)S(1)} %copy-done.43, f32[1024]{0:T(1024)S(1)} %copy-done.45, f32[1024]{0:T(1024)S(1)} %copy-done.39), kind=kOutput, calls=%fused_computation.215 | convolution fusion | flops 8596226048 | bytes 27279360 | tf_op jit(solution)/shard_map/dot_general | solution.py:164
  862.0 18.5 %convolution_convert_fusion = bf16[4096,1024]{1,0:T(8,128)(2,1)} fusion(bf16[1,1024,1024]{2,1,0:T(8,128)(2,1)S(1)} %copy-done.16, f32[1024,4096]{1,0:T(8,128)} %fusion.133, f32[4096]{0:T(1024)S(1)} %bitcast.205), kind=kOutput, calls=%fused_computation.57 | convolution fusion | flops 8636071936 | bytes 27279360 | tf_op jit(solution)/shard_map/dot_general | solution.py:219
  880.6 26.9 %fusion.146 = (bf16[4096]{0:T(1024)(128)(2,1)S(1)}, bf16[1024,4096]{1,0:T(8,128)(2,1)S(1)}) fusion(bf16[4096,1024]{1,0:T(8,128)(2,1)} %all-gather.12.cloned.1.call-done, bf16[1,1024,1024]{2,1,0:T(8,128)(2,1)} %param.37, f32[1024,4096]{1,0:T(8,128)} %fusion.133, f32[4096]{0:T(1024)S(1)} %bitcast.206), kind=kOutput, calls=%fused_computation.226 | convolution fusion | flops 8698982400 | bytes 35676160 | tf_op jit(solution)/shard_map/dot_general | solution.py:221
  910.7 12.2 %convolution_convert_fusion.1 = bf16[1024,4096]{1,0:T(8,128)(2,1)} fusion(bf16[1024,4096]{1,0:T(8,128)(2,1)S(1)} %get-tuple-element.173, bf16[1,1024,1024]{2,1,0:T(8,128)(2,1)S(1)} %copy-done.3, f32[1024]{0:T(1024)S(1)} %copy-done.49, f32[1024]{0:T(1024)S(1)} %copy-done.43, f32[1024]{0:T(1024)S(1)} %copy-done.45, f32[1024]{0:T(1024)S(1)} %copy-done.39), kind=kOutput, calls=%fused_computation.58 | convolution fusion | flops 8600420352 | bytes 18890752 | tf_op jit(solution)/shard_map/dot_general | solution.py:224
  933.2 13.3 %fusion.148 = f32[1024,1024]{1,0:T(8,128)} fusion(bf16[1024,4096]{1,0:T(8,128)(2,1)S(1)} %bitcast.211, bf16[1024,4096]{1,0:T(8,128)(2,1)} %all-gather.10.cloned.1.call-done), kind=kOutput, calls=%fused_computation.228 | convolution fusion | flops 8589934592 | bytes 20971520 | tf_op jit(solution)/shard_map/dot_general | solution.py:226
  946.5 12.6 %fusion.137 = (bf16[1024]{0:T(1024)(128)(2,1)S(1)}, f32[1024]{0:T(1024)S(1)}, f32[1024,1024]{1,0:T(8,128)S(1)}) fusion(f32[1024]{0:T(1024)S(1)} %copy-done.43, f32[1024]{0:T(1024)S(1)} %copy-done.39, bf16[1,1024,1024]{2,1,0:T(8,128)(2,1)S(1)} %copy-done.3, f32[1024,1024]{1,0:T(8,128)} %fusion.148, bf16[1024,3072]{1,0:T(8,128)(2,1)} %all-gather.6.cloned.1.call-done, ...), kind=kOutput, calls=%fused_computation.217 | convolution fusion | flops 6468663296 | bytes 23083008 | tf_op jit(solution)/shard_map/dot_general | solution.py:296
  963.6 61.5 %all-reduce.7 = (bf16[1024]{0:T(1024)(128)(2,1)S(1)}, bf16[1024]{0:T(1024)(128)(2,1)S(1)}, bf16[1024]{0:T(1024)(128)(2,1)S(1)}, bf16[4096]{0:T(1024)(128)(2,1)S(1)}, bf16[1024]{0:T(1024)(128)(2,1)S(1)}) all-reduce(bf16[1024]{0:T(1024)(128)(2,1)S(1)} %dynamic-update-slice.26, ...), channel_id=1, replica_groups=mesh['rows'=16,'seq'=2] {'rows'}, use_global_device_ids=true, to_apply=%add.2 | all-reduce | flops 8192 | bytes 32768
  1025.1 6.9 reduce-scatter.11.cloned.1.call-done
  1032.0 108.6 %reduce-scatter.9.cloned.1.call-done = bf16[64,4096]{1,0:T(8,128)(2,1)} async-done(((bf16[1024,4096]{1,0:T(8,128)(2,1)}), bf16[64,4096]{1,0:T(8,128)(2,1)}) %reduce-scatter.9.cloned.1.call-update) | async-done | bytes 524304 | tf_op jit(solution)/shard_map/reduce_scatter | solution.py:69
  1140.7 18.3 %fusion.61 = bf16[1,1024,1024]{2,1,0:T(8,128)(2,1)} fusion(f32[1024,1024]{1,0:T(8,128)} %fusion.147, bf16[1,1024,1024]{2,1,0:T(8,128)(2,1)S(1)} %copy-done.3, f32[1024]{0:T(1024)S(1)} %convert_element_type.204, bf16[4096,1024]{1,0:T(8,128)(2,1)} %all-gather.12.cloned.1.call-done, f32[1024,4096]{1,0:T(8,128)} %fusion.133, f32[4096]{0:T(1024)S(1)} %bitcast.207), kind=kOutput, calls=%fused_computation.115 | convolution fusion | flops 8637120512 | bytes 33574912 | tf_op jit(solution)/shard_map/dot_general | solution.py:169
  1159.2 5.0 all-reduce.9
  1166.3 5.1 add_bitcast_fusion
  1171.4 23.6 %all-reduce.13.cloned.1.call-done = (bf16[64,3072]{1,0:T(8,128)(2,1)}, bf16[64,1024]{1,0:T(8,128)(2,1)}, bf16[64,4096]{1,0:T(8,128)(2,1)}, bf16[256,1024]{1,0:T(8,128)(2,1)}) async-done(((bf16[64,3072]{1,0:T(8,128)(2,1)}, bf16[64,1024]{1,0:T(8,128)(2,1)}, bf16[64,4096]{1,0:T(8,128)(2,1)}, bf16[256,1024]{1,0:T(8,128)(2,1)}), (bf16[64,3072]{1,0:T(8,128)(2,1)}, bf16[64,1024]{1,0:T(8,128)(2,1)}, ...) | async-done | bytes 1572880 | tf_op jit(solution)/shard_map/psum | solution.py:108
  (237 shorter events, 119.8 us)
Async XLA Ops:
  7.2 45.6 %copy-start.2 = (bf16[1,1024,1024]{2,1,0:T(8,128)(2,1)S(1)}, bf16[1,1024,1024]{2,1,0:T(8,128)(2,1)}, u32[]{:S(2)}) copy-start(bf16[1,1024,1024]{2,1,0:T(8,128)(2,1)} %param.27) | copy-start | bytes 6291460
  7.2 67.6 %all-gather.6.cloned.1.call-start = ((), (), s32[]{:S(2)}) async-start(), calls=%async_computation.4 | async-start | bytes 6684672 | tf_op jit(solution)/shard_map/all_gather | solution.py:129
  7.9 109.2 %all-gather.8.cloned.1.call-start = ((), (), s32[]{:S(2)}) async-start(), calls=%async_computation.5 | async-start | bytes 2228224 | tf_op jit(solution)/shard_map/all_gather | solution.py:130
  8.7 837.3 %all-gather.10.cloned.1.call-start = ((), (), s32[]{:S(2)}) async-start(), calls=%async_computation.6 | async-start | bytes 8912896 | tf_op jit(solution)/shard_map/all_gather | solution.py:133
  9.4 871.2 %all-gather.12.cloned.1.call-start = ((), (), s32[]{:S(2)}) async-start(), calls=%async_computation.7 | async-start | bytes 8912896 | tf_op jit(solution)/shard_map/all_gather | solution.py:135
  10.0 1015.1 %reduce-scatter.7.cloned.1.call-start = ((), (), s32[]{:S(2)}) async-start(), calls=%async_computation.9 | async-start | bytes 2228224 | tf_op jit(solution)/shard_map/reduce_scatter | solution.py:101
  50.8 33.0 %copy-start.48 = (f32[1024]{0:T(1024)}, f32[1024]{0:T(1024)S(1)}, u32[]{:S(2)}) copy-start(f32[1024]{0:T(1024)S(1)} %convert_element_type.190) | copy-start | bytes 12292
  50.8 33.0 %copy-start.42 = (f32[1024]{0:T(1024)}, f32[1024]{0:T(1024)S(1)}, u32[]{:S(2)}) copy-start(f32[1024]{0:T(1024)S(1)} %convert_element_type.189) | copy-start | bytes 12292
  52.8 31.1 %copy-start.38 = (f32[1024]{0:T(1024)}, f32[1024]{0:T(1024)S(1)}, u32[]{:S(2)}) copy-start(f32[1024]{0:T(1024)S(1)} %broadcast_multiply_fusion) | copy-start | bytes 12292
  54.1 29.8 %copy-start.44 = (f32[1024]{0:T(1024)}, f32[1024]{0:T(1024)S(1)}, u32[]{:S(2)}) copy-start(f32[1024]{0:T(1024)S(1)} %fusion.112) | copy-start | bytes 12292
  99.9 49.6 %collective-permute-start = (bf16[1024,1024]{1,0:T(8,128)(2,1)}, bf16[1024,1024]{1,0:T(8,128)(2,1)}, u32[]{:S(2)}, u32[]{:S(2)}) collective-permute-start(bf16[1024,1024]{1,0:T(8,128)(2,1)} %slice.503), channel_id=1, source_target_pairs={{0,1},{2,3},{4,5},{6,7},{8,9},{10,11},{12,13},{14,15},{16,17},{18,... | collective-permute-start | bytes 6291464 | tf_op jit(solution)/shard_map/ppermute | solution.py:17
  105.1 12.0 copy-start.14
  107.3 86.5 %collective-permute-start.1 = (bf16[1024,1024]{0,1:T(8,128)(2,1)}, bf16[1024,1024]{0,1:T(8,128)(2,1)}, u32[]{:S(2)}, u32[]{:S(2)}) collective-permute-start(bf16[1024,1024]{0,1:T(8,128)(2,1)} %bitcast.13), channel_id=1, source_target_pairs={{0,1},{2,3},{4,5},{6,7},{8,9},{10,11},{12,13},{14,15},{16,17},{18,... | collective-permute-start | bytes 6291464 | tf_op jit(solution)/shard_map/ppermute | solution.py:17
  129.6 171.0 %copy-start.4 = (bf16[1024,16,32]{0,2,1:T(8,128)(2,1)}, bf16[1024,16,32]{0,2,1:T(8,128)(2,1)S(1)}, u32[]{:S(2)}) copy-start(bf16[1024,16,32]{0,2,1:T(8,128)(2,1)S(1)} %slice.506) | copy-start | bytes 3145732
  134.0 166.6 %copy-start.6 = (bf16[1024,16,32]{0,2,1:T(8,128)(2,1)}, bf16[1024,16,32]{0,2,1:T(8,128)(2,1)S(1)}, u32[]{:S(2)}) copy-start(bf16[1024,16,32]{0,2,1:T(8,128)(2,1)S(1)} %copy.50) | copy-start | bytes 3145732
  134.1 75.8 %copy-start.20 = (bf16[512,8,64]{0,2,1:T(8,128)(2,1)}, bf16[512,8,64]{0,2,1:T(8,128)(2,1)S(1)}, u32[]{:S(2)}) copy-start(bf16[512,8,64]{0,2,1:T(8,128)(2,1)S(1)} %pad_maximum_fusion.16) | copy-start | bytes 1572868
  193.8 16.1 %copy-start.24 = (pred[512,2048]{1,0:T(8,128)(4,1)S(1)}, pred[512,2048]{1,0:T(8,128)(4,1)}, u32[]{:S(2)}) copy-start(pred[512,2048]{1,0:T(8,128)(4,1)} %get-tuple-element.140) | copy-start | bytes 3145732
  300.6 74.8 %copy-start.32 = (f32[8,512]{1,0:T(8,128)}, f32[8,512]{1,0:T(8,128)S(1)}, u32[]{:S(2)}) copy-start(f32[8,512]{1,0:T(8,128)S(1)} %get-tuple-element.161) | copy-start | bytes 49156
  300.6 15.7 %copy-start = (bf16[2048,1024]{0,1:T(8,128)(2,1)S(1)}, bf16[2048,1024]{0,1:T(8,128)(2,1)}, u32[]{:S(2)}) copy-start(bf16[2048,1024]{0,1:T(8,128)(2,1)} %copy.43) | copy-start | bytes 12582916
  300.6 15.7 %copy-start.10 = (bf16[1024,1024]{0,1:T(8,128)(2,1)S(1)}, bf16[1024,1024]{0,1:T(8,128)(2,1)}, u32[]{:S(2)}) copy-start(bf16[1024,1024]{0,1:T(8,128)(2,1)} %fusion.77) | copy-start | bytes 6291460
  316.3 86.3 %copy-start.30 = (f32[8,512]{1,0:T(8,128)}, f32[8,512]{1,0:T(8,128)S(1)}, u32[]{:S(2)}) copy-start(f32[8,512]{1,0:T(8,128)S(1)} %get-tuple-element.159) | copy-start | bytes 49156
  316.3 22.7 %copy-start.27 = (f32[8,512]{1,0:T(8,128)S(1)}, f32[8,512]{1,0:T(8,128)}, u32[]{:S(2)}) copy-start(f32[8,512]{1,0:T(8,128)} %log_add_fusion) | copy-start | bytes 49156
  361.7 13.8 %copy-start.11 = (bf16[1024,1024]{0,1:T(8,128)(2,1)S(1)}, bf16[1024,1024]{0,1:T(8,128)(2,1)}, u32[]{:S(2)}) copy-start(bf16[1024,1024]{0,1:T(8,128)(2,1)} %fusion.77) | copy-start | bytes 6291460
  375.4 13.6 %copy-start.36 = (f32[8,512]{1,0:T(8,128)}, f32[8,512]{1,0:T(8,128)S(1)}, u32[]{:S(2)}) copy-start(f32[8,512]{1,0:T(8,128)S(1)} %fusion) | copy-start | bytes 49156
  402.6 15.4 %copy-start.34 = (f32[8,512]{1,0:T(8,128)}, f32[8,512]{1,0:T(8,128)S(1)}, u32[]{:S(2)}) copy-start(f32[8,512]{1,0:T(8,128)S(1)} %fusion.1) | copy-start | bytes 49156
  461.1 4.9 copy-start.1
  461.1 4.9 copy-start.12
  488.5 22.2 %copy-start.41 = (f32[8,512]{1,0:T(8,128)S(1)}, f32[8,512]{1,0:T(8,128)}, u32[]{:S(2)}) copy-start(f32[8,512]{1,0:T(8,128)} %get-tuple-element.167) | copy-start | bytes 49156
  538.5 12.6 %copy-start.40 = (f32[8,512]{1,0:T(8,128)S(1)}, f32[8,512]{1,0:T(8,128)}, u32[]{:S(2)}) copy-start(f32[8,512]{1,0:T(8,128)} %get-tuple-element.169) | copy-start | bytes 49156
  591.7 28.0 %copy-start.5 = (bf16[1024,16,32]{0,2,1:T(8,128)(2,1)S(1)}, bf16[1024,16,32]{0,2,1:T(8,128)(2,1)}, u32[]{:S(2)}) copy-start(bf16[1024,16,32]{0,2,1:T(8,128)(2,1)} %copy-done.4) | copy-start | bytes 3145732
  591.7 28.0 %copy-start.7 = (bf16[1024,16,32]{0,2,1:T(8,128)(2,1)S(1)}, bf16[1024,16,32]{0,2,1:T(8,128)(2,1)}, u32[]{:S(2)}) copy-start(bf16[1024,16,32]{0,2,1:T(8,128)(2,1)} %copy-done.6) | copy-start | bytes 3145732
  667.3 17.6 %slice-start = ((s8[16777216]{0:T(1024)(128)(4,1)}), s8[4194304]{0:T(1024)(128)(4,1)S(1)}, s32[]{:S(2)}) async-start(s8[16777216]{0:T(1024)(128)(4,1)} %bitcast.170), calls=%async_computation.13 | async-start | bytes 8388608
  667.4 17.6 %slice-start.1 = ((s8[16777216]{0:T(1024)(128)(4,1)}), s8[4194304]{0:T(1024)(128)(4,1)S(1)}, s32[]{:S(2)}) async-start(s8[16777216]{0:T(1024)(128)(4,1)} %bitcast.170), calls=%async_computation.14 | async-start | bytes 8388608
  673.9 11.0 slice-start.2
  673.9 11.0 slice-start.3
  673.9 11.0 copy-start.21
  696.1 13.0 %copy-start.33 = (f32[8,512]{1,0:T(8,128)S(1)}, f32[8,512]{1,0:T(8,128)}, u32[]{:S(2)}) copy-start(f32[8,512]{1,0:T(8,128)} %copy-done.32) | copy-start | bytes 49156
  696.1 13.0 %copy-start.37 = (f32[8,512]{1,0:T(8,128)S(1)}, f32[8,512]{1,0:T(8,128)}, u32[]{:S(2)}) copy-start(f32[8,512]{1,0:T(8,128)} %copy-done.36) | copy-start | bytes 49156
  696.1 74.7 %collective-permute-start.2 = (bf16[1024,1024]{0,1:T(8,128)(2,1)}, bf16[1024,1024]{0,1:T(8,128)(2,1)}, u32[]{:S(2)}, u32[]{:S(2)}) collective-permute-start(bf16[1024,1024]{0,1:T(8,128)(2,1)} %bitcast.34), channel_id=1, source_target_pairs={{1,0},{3,2},{5,4},{7,6},{9,8},{11,10},{13,12},{15,14},{17,16},{19,... | collective-permute-start | bytes 6291464 | tf_op jit(solution)/shard_map/ppermute | solution.py:17
  709.1 15.5 %copy-start.31 = (f32[8,512]{1,0:T(8,128)S(1)}, f32[8,512]{1,0:T(8,128)}, u32[]{:S(2)}) copy-start(f32[8,512]{1,0:T(8,128)} %copy-done.30) | copy-start | bytes 49156
  709.1 15.5 %copy-start.35 = (f32[8,512]{1,0:T(8,128)S(1)}, f32[8,512]{1,0:T(8,128)}, u32[]{:S(2)}) copy-start(f32[8,512]{1,0:T(8,128)} %copy-done.34) | copy-start | bytes 49156
  739.7 12.7 %copy-start.25 = (f32[512,8,64]{0,2,1:T(8,128)S(1)}, f32[512,8,64]{0,2,1:T(8,128)}, u32[]{:S(2)}) copy-start(f32[512,8,64]{0,2,1:T(8,128)} %fusion.95) | copy-start | bytes 3145732
  739.7 12.7 %copy-start.26 = (f32[512,8,64]{0,2,1:T(8,128)S(1)}, f32[512,8,64]{0,2,1:T(8,128)}, u32[]{:S(2)}) copy-start(f32[512,8,64]{0,2,1:T(8,128)} %fusion.96) | copy-start | bytes 3145732
  759.2 50.4 %collective-permute-start.3 = (bf16[1024,1024]{0,1:T(8,128)(2,1)}, bf16[1024,1024]{0,1:T(8,128)(2,1)}, u32[]{:S(2)}, u32[]{:S(2)}) collective-permute-start(bf16[1024,1024]{0,1:T(8,128)(2,1)} %bitcast.42), channel_id=1, source_target_pairs={{1,0},{3,2},{5,4},{7,6},{9,8},{11,10},{13,12},{15,14},{17,16},{19,... | collective-permute-start | bytes 6291464 | tf_op jit(solution)/shard_map/ppermute | solution.py:17
  762.9 4.1 copy-start.15
  770.8 254.3 %reduce-scatter.5.cloned.1.call-start = ((), (), s32[]{:S(2)}) async-start(), calls=%async_computation.8 | async-start | bytes 6684672 | tf_op jit(solution)/shard_map/reduce_scatter | solution.py:98
  797.9 11.7 copy-start.9
  799.5 14.2 %copy-start.22 = (bf16[1024,16,64]{0,2,1:T(8,128)(2,1)}, bf16[1024,16,64]{0,2,1:T(8,128)(2,1)S(1)}, u32[]{:S(2)}) copy-start(bf16[1024,16,64]{0,2,1:T(8,128)(2,1)S(1)} %pad_maximum_fusion.9) | copy-start | bytes 6291460
  803.1 10.6 copy-start.3
  803.1 10.6 copy-start.39
  803.1 10.6 copy-start.43
  803.1 10.6 copy-start.45
  803.1 10.6 copy-start.49
  826.0 206.0 %reduce-scatter.11.cloned.1.call-start = ((), (), s32[]{:S(2)}) async-start(), calls=%async_computation.11 | async-start | bytes 8912896 | tf_op jit(solution)/shard_map/reduce_scatter | solution.py:75
  846.0 16.0 %copy-start.16 = (bf16[1,1024,1024]{2,1,0:T(8,128)(2,1)S(1)}, bf16[1,1024,1024]{2,1,0:T(8,128)(2,1)}, u32[]{:S(2)}) copy-start(bf16[1,1024,1024]{2,1,0:T(8,128)(2,1)} %param.37) | copy-start | bytes 6291460
  880.5 260.1 %reduce-scatter.9.cloned.1.call-start = ((), (), s32[]{:S(2)}) async-start(), calls=%async_computation.10 | async-start | bytes 8912896 | tf_op jit(solution)/shard_map/reduce_scatter | solution.py:69
  907.5 3.3 copy-start.53
  923.0 3.6 copy-start.52
  923.0 3.9 copy-start.18
  923.0 272.0 %all-reduce.13.cloned.1.call-start = ((), (), s32[]{:S(2)}) async-start(), calls=%async_computation.12 | async-start | bytes 3145728 | tf_op jit(solution)/shard_map/psum | solution.py:108
  926.8 6.4 slice-start.4
  928.7 4.5 slice-start.5
  933.2 13.3 %copy-start.23 = (bf16[1024,16,64]{0,2,1:T(8,128)(2,1)S(1)}, bf16[1024,16,64]{0,2,1:T(8,128)(2,1)}, u32[]{:S(2)}) copy-start(bf16[1024,16,64]{0,2,1:T(8,128)(2,1)} %copy-done.22) | copy-start | bytes 6291460
  946.5 12.6 %copy-start.47 = (f32[1024]{0:T(1024)S(1)}, f32[1024]{0:T(1024)}, u32[]{:S(2)}) copy-start(f32[1024]{0:T(1024)} %copy-done.46) | copy-start | bytes 12292
  (9 other events, 14.9 us)
Sparse Core Ops, SparseCore 0:
  10.3 64.4 all-gather.5
  77.0 40.1 all-gather.7
  119.3 73.6 all-gather.9
  195.0 73.1 all-gather.11
  770.9 64.1 reduce-scatter.6
  839.4 84.2 reduce-scatter.4
  927.8 104.1 reduce-scatter.10
  1036.1 104.5 reduce-scatter.8
  1143.1 51.8 all-reduce.12
where the time goes:
time: 1220 us; the launch traced here: 1210 us
  matrix products  516 us (42%)
  other arithmetic  250 us (20%)
  waiting for transfers between devices  220 us (18%)
  blocking collectives  121 us (10%)
  local copies, waits for them, and re-layouts  74.7 us (6%)
  between operations  17.2 us (1%)
    convert_element_type x4, other arithmetic, body(): d_scores = (probs * (d_probs - row_delta)).astype(jnp.bfloat16)  112 us
    reduce_scatter x1, waiting for transfers between devices, reduce_mlp(): lax.psum_scatter(terms[0].astype(jnp.bfloat16), 'rows', scatter_dimension...  109 us
    unnamed x2, blocking collectives  97 us
    dot_general x4, matrix products, body(): jnp.einsum('qhd,khd->hqk', d_out_block, value_part, preferred_element_typ...  90 us
    dot_general x4, matrix products, block_scores(): jnp.einsum('qhd,khd->hqk', query_block, key_block, preferred_element_type...  63.2 us
    dot_general x4, matrix products, body(): jnp.einsum('hqk,qhd->khd', probs.astype(jnp.bfloat16), d_out_block, prefe...  61.7 us
    dot_general x4, matrix products, body(): jnp.einsum('hqk,khd->qhd', (exps / row_total).astype(jnp.bfloat16), value...  60.8 us
    reduce_sum x4, other arithmetic, body(): row_total = jnp.sum(exps, axis=2, keepdims=True)  55.6 us
  transfers between devices with their start and end apart: 13, of which 8 were waited for; matrix products, arithmetic and copies ran while one was open for 68% of the time, Pallas kernels for 0%

commit v1 on v0

v1 whole, which is shorter than its diff:
```python
import functools

import jax
import jax.numpy as jnp
import numpy as np
from jax import lax
from jax.experimental import pallas as pl
from jax.experimental.pallas import tpu as pltpu
from jax.sharding import PartitionSpec as P

HEADS = 16
HEAD = 64
ROT = 32
EPS = 1e-05
GELU_COEF = 0.7978845608028654

NEG = -1e30
BQ = 256

def dot_t(a, b):
    return lax.dot_general(a, b, (((1,), (1,)), ((), ())), preferred_element_type=jnp.float32)

def dot_n(a, b):
    return lax.dot_general(a, b, (((1,), (0,)), ((), ())), preferred_element_type=jnp.float32)

def dot_c(a, b):
    return lax.dot_general(a, b, (((0,), (0,)), ((), ())), preferred_element_type=jnp.float32)

def attention_kernel(pairs, tokens, lows, start_col, start_row, cos_ref, sin_ref, q_ref, k_ref, v_ref, do_ref,
                     out_ref, dq_ref, dk_ref, dv_ref, bias, bias_t, dk_acc, dv_acc, m_sc, l_sc, acc_sc, dq_sc):
    blocks = tokens // BQ
    span = blocks + 1
    lane = lax.broadcasted_iota(jnp.int32, (BQ, 128), 1)
    even = lane < 64

    @pl.when(pl.program_id(0) == 0)
    def _():
        for qb in range(blocks):
            start_c = start_col[qb * BQ:(qb + 1) * BQ, :]
            start_r = start_row[:, qb * BQ:(qb + 1) * BQ]
            q_c = tokens + qb * BQ + lax.broadcasted_iota(jnp.int32, (BQ, BQ), 0)
            q_r = tokens + qb * BQ + lax.broadcasted_iota(jnp.int32, (BQ, BQ), 1)

            def fill(kb, _):
                k_r = kb * BQ + lax.broadcasted_iota(jnp.int32, (BQ, BQ), 1)
                k_c = kb * BQ + lax.broadcasted_iota(jnp.int32, (BQ, BQ), 0)
                slot = qb * span + kb - qb
                bias[slot] = jnp.where((k_r >= start_c) & (k_r <= q_c), 0.0, NEG)
                bias_t[slot] = jnp.where((k_c >= start_r) & (k_c <= q_r), 0.0, NEG)
                return 0
            lax.fori_loop(lows[qb], blocks + qb + 1, fill, 0)

    dk_acc[...] = jnp.zeros_like(dk_acc)
    dv_acc[...] = jnp.zeros_like(dv_acc)
    heads = 2 * pairs

    def one_q(qb, _):
        q_rows = pl.ds(pl.multiple_of(qb * BQ, BQ), BQ)
        low = lows[qb]
        high = blocks + qb + 1
        q_h = []
        for p in range(pairs):
            q = q_ref[q_rows, p * 128:(p + 1) * 128]
            q_h += [jnp.where(even, q, 0), jnp.where(even, 0, q)]
        m_sc[...] = jnp.full_like(m_sc, NEG)
        l_sc[...] = jnp.zeros_like(l_sc)
        acc_sc[...] = jnp.zeros_like(acc_sc)

        def forward(kb, _):
            k_rows = pl.ds(pl.multiple_of(kb * BQ, BQ), BQ)
            b = bias[qb * span + kb - qb]
            for p in range(pairs):
                cols = slice(p * 128, (p + 1) * 128)
                k = k_ref[k_rows, cols]
                v = v_ref[k_rows, cols]
                outs, scales = [], []
                for h in (2 * p, 2 * p + 1):
                    s = dot_t(q_h[h], k) + b
                    m_old = m_sc[h]
                    m_new = jnp.maximum(m_old, jnp.max(s, axis=1, keepdims=True))
                    e = jnp.exp(s - m_new[:, :1])
                    a = jnp.exp(m_old - m_new)
                    l_sc[h] = a * l_sc[h] + jnp.sum(e, axis=1, keepdims=True)
                    m_sc[h] = m_new
                    outs.append(dot_n(e.astype(jnp.bfloat16), v))
                    scales.append(a)
                acc_sc[p] = acc_sc[p] * jnp.where(even, scales[0], scales[1]) + jnp.where(even, outs[0], outs[1])
            return 0
        lax.fori_loop(low, high, forward, 0)

        do_h, lse_r, delta_r = [], [], []
        for p in range(pairs):
            cols = slice(p * 128, (p + 1) * 128)
            o = acc_sc[p] / jnp.where(even, l_sc[2 * p], l_sc[2 * p + 1])
            out_ref[q_rows, cols] = o.astype(jnp.bfloat16)
            do = do_ref[q_rows, cols]
            prod = o * do.astype(jnp.float32)
            for h in (2 * p, 2 * p + 1):
                mine = even if h % 2 == 0 else ~even
                delta = jnp.sum(jnp.where(mine, prod, 0.0), axis=1, keepdims=True)
                lse = m_sc[h] + jnp.log(l_sc[h])
                both = jnp.where(even, lse, delta)
                turned = both.T
                lse_r.append(turned[0:1, :])
                delta_r.append(turned[64:65, :])
                do_h.append(jnp.where(mine, do, 0))
        dq_sc[...] = jnp.zeros_like(dq_sc)

        def backward(kb, _):
            k_rows = pl.ds(pl.multiple_of(kb * BQ, BQ), BQ)
            b = bias_t[qb * span + kb - qb]
            for p in range(pairs):
                cols = slice(p * 128, (p + 1) * 128)
                k = k_ref[k_rows, cols]
                v = v_ref[k_rows, cols]
                dqs, dks, dvs = [], None, None
                for h in (2 * p, 2 * p + 1):
                    s = dot_t(k, q_h[h]) + b
                    prob = jnp.exp(s - lse_r[h])
                    dp = dot_t(v, do_h[h])
                    ds = (prob * (dp - delta_r[h])).astype(jnp.bfloat16)
                    dv = dot_n(prob.astype(jnp.bfloat16), do_h[h])
                    dk = dot_n(ds, q_h[h])
                    dvs = dv if dvs is None else dvs + dv
                    dks = dk if dks is None else dks + dk
                    dqs.append(dot_c(ds, k))
                dv_acc[k_rows, cols] += dvs
                dk_acc[k_rows, cols] += dks
                dq_sc[p] += jnp.where(even, dqs[0], dqs[1])
            return 0
        lax.fori_loop(low, high, backward, 0)
        own_rows = pl.ds(pl.multiple_of(tokens + qb * BQ, BQ), BQ)
        for p in range(pairs):
            dq_ref[q_rows, p * 128:(p + 1) * 128] = unrotate(
                dq_sc[p] * 0.125, cos_ref[own_rows, :], sin_ref[own_rows, :]).astype(jnp.bfloat16)
        return 0
    lax.fori_loop(0, blocks, one_q, 0)

    def finish(kb, _):
        rows = pl.ds(pl.multiple_of(kb * BQ, BQ), BQ)
        for p in range(pairs):
            cols = slice(p * 128, (p + 1) * 128)
            dk_ref[rows, cols] = unrotate(dk_acc[rows, cols], cos_ref[rows, :], sin_ref[rows, :]).astype(jnp.bfloat16)
            dv_ref[rows, cols] = dv_acc[rows, cols].astype(jnp.bfloat16)
        return 0
    lax.fori_loop(0, 2 * blocks, finish, 0)

def swap_pairs(x):
    odd = lax.broadcasted_iota(jnp.int32, x.shape, 1) % 2 == 1
    n = x.shape[1]
    return jnp.where(odd, pltpu.roll(x, 1, 1), pltpu.roll(x, n - 1, 1))

def rotate(x, cosine, sine):
    return x * cosine + swap_pairs(x) * sine

def unrotate(x, cosine, sine):
    return x * cosine - swap_pairs(x) * sine

def attention(lows, starts, cosine, sine, mixed, d_out):
    tokens, width = d_out.shape
    pairs = 2
    wide = 128 * pairs
    groups = width // wide
    blocks = tokens // BQ
    whole = lambda shape: pl.BlockSpec(shape, lambda g, lows: (0,) * len(shape))
    own = pl.BlockSpec((tokens, wide), lambda g, lows: (0, g))
    both = pl.BlockSpec((2 * tokens, wide), lambda g, lows: (0, g))
    q_spec = pl.BlockSpec((tokens, wide), lambda g, lows: (1, g))
    k_spec = pl.BlockSpec((2 * tokens, wide), lambda g, lows: (0, groups + g))
    v_spec = pl.BlockSpec((2 * tokens, wide), lambda g, lows: (0, 2 * groups + g))
    bf, f32 = jnp.bfloat16, jnp.float32
    slots = blocks * (blocks + 1)
    one, two = jax.ShapeDtypeStruct((tokens, width), bf), jax.ShapeDtypeStruct((2 * tokens, width), bf)
    return pl.pallas_call(
        functools.partial(attention_kernel, pairs, tokens),
        out_shape=[one, one, two, two],
        grid_spec=pltpu.PrefetchScalarGridSpec(
            num_scalar_prefetch=1,
            grid=(groups,),
            in_specs=[whole((tokens, 1)), whole((1, tokens)), whole((2 * tokens, 128)), whole((2 * tokens, 128)),
                      q_spec, k_spec, v_spec, own],
            out_specs=[own, own, both, both],
            scratch_shapes=[pltpu.VMEM((slots, BQ, BQ), f32), pltpu.VMEM((slots, BQ, BQ), f32),
                            pltpu.VMEM((2 * tokens, wide), f32), pltpu.VMEM((2 * tokens, wide), f32),
                            pltpu.VMEM((2 * pairs, BQ, 128), f32), pltpu.VMEM((2 * pairs, BQ, 128), f32),
                            pltpu.VMEM((pairs, BQ, 128), f32), pltpu.VMEM((pairs, BQ, 128), f32)],
        ),
        compiler_params=pltpu.CompilerParams(vmem_limit_bytes=56 * 2**20),
        cost_estimate=pl.CostEstimate(flops=60 * 10**9, bytes_accessed=30 * 2**20, transcendentals=0),
        name="attention",
    )(lows, starts[:, None], starts[None, :], cosine, sine, mixed, mixed, mixed, d_out)


def qkv_kernel(cols, normed_ref, w_ref, cos_ref, sin_ref, out_ref):
    block = pl.program_id(1)
    mixed = dot_n(normed_ref[...], w_ref[...])

    @pl.when(block < 2 * cols)
    def _():
        scale = jnp.where(block < cols, 0.125, 1.0)
        cosine = cos_ref[...] * scale
        sine = sin_ref[...] * scale
        for i in range(mixed.shape[1] // 128):
            lanes = slice(i * 128, (i + 1) * 128)
            out_ref[:, lanes] = rotate(mixed[:, lanes], cosine, sine).astype(jnp.bfloat16)

    @pl.when(block >= 2 * cols)
    def _():
        out_ref[...] = mixed.astype(jnp.bfloat16)


def project(normed, w_qkv, cosine, sine):
    rows, width = normed.shape
    wide, tall = 512, 1024
    cols = width // wide
    return pl.pallas_call(
        functools.partial(qkv_kernel, cols),
        out_shape=jax.ShapeDtypeStruct((rows, 3 * width), jnp.bfloat16),
        grid=(rows // tall, 3 * cols),
        in_specs=[
            pl.BlockSpec((tall, width), lambda i, j: (i, 0)),
            pl.BlockSpec((width, wide), lambda i, j: (0, j)),
            pl.BlockSpec((tall, 128), lambda i, j: (i, 0)),
            pl.BlockSpec((tall, 128), lambda i, j: (i, 0)),
        ],
        out_specs=pl.BlockSpec((tall, wide), lambda i, j: (i, j)),
        compiler_params=pltpu.CompilerParams(vmem_limit_bytes=48 * 2**20),
        cost_estimate=pl.CostEstimate(flops=12 * 10**9, bytes_accessed=24 * 2**20, transcendentals=0),
        name="project",
    )(normed, w_qkv, cosine, sine)


def rope_tables(position):
    lane = np.arange(128) % HEAD
    freqs = np.where(lane < ROT, 10000.0 ** (-2.0 * (lane // 2) / ROT), 0.0).astype(np.float32)
    sign = np.where(lane % 2 == 0, -1.0, 1.0).astype(np.float32)
    angles = position.astype(jnp.float32)[:, None] * freqs[None, :]
    return jnp.cos(angles), jnp.sin(angles) * sign[None, :]


def layer_norm_stats(values):
    mean = jnp.mean(values, axis=1, keepdims=True)
    centered = values - mean
    spread = jnp.mean(centered * centered, axis=1, keepdims=True)
    scale = lax.rsqrt(spread + EPS)
    return centered * scale, scale


def body(block_input, lengths, norm_gain, norm_bias, w_qkv, w_attn_out, w_fc_in, b_fc_in, w_fc_out, b_fc_out, cotangent):
    f32, bf = jnp.float32, jnp.bfloat16
    gather = lambda w: lax.all_gather(w, "rows", axis=0, tiled=True)
    seqs = lax.axis_size("seq")
    prior_input = lax.ppermute(block_input[0], "seq", [(i, i + 1) for i in range(seqs - 1)])
    gain, bias = gather(norm_gain).astype(f32), gather(norm_bias).astype(f32)
    w_qkv_all, w_out_all = gather(w_qkv), gather(w_attn_out)
    w_in_all, b_in_all, w_back_all, b_back_all = gather(w_fc_in), gather(b_fc_in), gather(w_fc_out), gather(b_fc_out)
    inputs = block_input[0].astype(f32)
    tokens, width = inputs.shape
    own_lengths = lengths[0]
    count = own_lengths.shape[0]
    first = lax.axis_index("seq") * tokens
    index = first - tokens + jnp.arange(2 * tokens, dtype=jnp.int32)
    order = np.arange(count)
    ends = jnp.sum(jnp.where(order[None, :] <= order[:, None], own_lengths[None, :], 0), axis=1)
    begin = jnp.sum(jnp.where(ends[None, :] <= index[:, None], own_lengths[None, :], 0), axis=1)
    cosine, sine = rope_tables(index - begin)
    starts = (begin - first + tokens)[tokens:]
    lows = starts[::BQ] // BQ

    unit, scale = layer_norm_stats(inputs)
    normed = (unit * gain + bias).astype(bf)
    prior_unit, _ = layer_norm_stats(prior_input.astype(f32))
    normed_both = jnp.concatenate([(prior_unit * gain + bias).astype(bf), normed], axis=0)
    mixed = project(normed_both, w_qkv_all, cosine, sine)
    grad_out = cotangent[0]
    d_attended = jnp.dot(grad_out, w_out_all.T, preferred_element_type=f32).astype(bf)
    attended, d_q, d_k, d_v = attention(lows, starts, cosine, sine, mixed, d_attended)

    d_normed_both = jnp.dot(d_k, w_qkv_all[:, width:2 * width].T, preferred_element_type=f32) + jnp.dot(
        d_v, w_qkv_all[:, 2 * width:].T, preferred_element_type=f32)
    back = lax.ppermute(d_normed_both[:tokens].astype(bf), "seq", [(i + 1, i) for i in range(seqs - 1)])
    grad_w_qkv = jnp.concatenate([
        jnp.dot(normed.T, d_q, preferred_element_type=f32).astype(bf),
        jnp.dot(normed_both.T, d_k, preferred_element_type=f32).astype(bf),
        jnp.dot(normed_both.T, d_v, preferred_element_type=f32).astype(bf)], axis=1)
    grad_w_out = jnp.dot(attended.T, grad_out, preferred_element_type=f32).astype(bf)

    pre = jnp.dot(normed, w_in_all, preferred_element_type=f32) + b_in_all.astype(f32)
    turn = jnp.tanh(GELU_COEF * (pre + 0.044715 * pre * pre * pre))
    hidden = (0.5 * pre * (1.0 + turn)).astype(bf)
    slope = 0.5 * (1.0 + turn) + 0.5 * pre * (1.0 - turn * turn) * (GELU_COEF * (1.0 + 3 * 0.044715 * pre * pre))
    d_pre = (jnp.dot(grad_out, w_back_all.T, preferred_element_type=f32) * slope).astype(bf)
    grad_w_back = jnp.dot(hidden.T, grad_out, preferred_element_type=f32).astype(bf)
    grad_w_in = jnp.dot(normed.T, d_pre, preferred_element_type=f32).astype(bf)
    grad_b_back = jnp.sum(grad_out.astype(f32), axis=0)
    grad_b_in = jnp.sum(d_pre.astype(f32), axis=0)
    d_normed = jnp.dot(d_pre, w_in_all.T, preferred_element_type=f32)
    d_normed = d_normed + jnp.dot(d_q, w_qkv_all[:, :width].T, preferred_element_type=f32)
    d_normed = d_normed + d_normed_both[tokens:] + back.astype(f32)

    block_output = (inputs + jnp.dot(attended, w_out_all, preferred_element_type=f32)
                    + jnp.dot(hidden, w_back_all, preferred_element_type=f32) + b_back_all.astype(f32)).astype(bf)
    grad_gain = jnp.sum(d_normed * unit, axis=0)
    grad_bias = jnp.sum(d_normed, axis=0)
    d_unit = d_normed * gain
    d_input = (d_unit - jnp.mean(d_unit, axis=1, keepdims=True)
               - unit * jnp.mean(d_unit * unit, axis=1, keepdims=True)) * scale
    grad_input = d_input + grad_out.astype(f32)

    def reduce(term):
        share = lax.psum_scatter(term.astype(bf), "rows", scatter_dimension=0, tiled=True)
        return lax.psum(share, "seq").astype(f32)

    return (block_output[None], grad_input[None], reduce(grad_gain), reduce(grad_bias), reduce(grad_w_qkv),
            reduce(grad_w_out), reduce(grad_w_in), reduce(grad_b_in), reduce(grad_w_back), reduce(grad_b_back))


def solution(mesh):
    vector, matrix, tokens = P("rows"), P("rows", None), P("rows", "seq", None)
    in_specs = (tokens, matrix, vector, vector, matrix, matrix, matrix, vector, matrix, vector, tokens)
    out_specs = (tokens, tokens, vector, vector, matrix, matrix, matrix, vector, matrix, vector)
    return jax.shard_map(body, mesh=mesh, in_specs=in_specs, out_specs=out_specs, check_vma=False)
```

time: 1220 us -> 809 us (0.66)
  matrix products: 516 us -> 161 us
  other arithmetic: 250 us -> 45.8 us
  Pallas kernels: 0 us -> 139 us
  local copies, waits for them, and re-layouts: 74.7 us -> 25.5 us
  waiting for transfers between devices: 220 us -> 262 us
  blocking collectives: 121 us -> 141 us
    dot_general x36 -> x15, matrix products: 516 us -> 161 us  [the longest x1 25.6 us: body(): jnp.dot(grad_out, w_back_all.T, preferred_element_type=f32) * slope]
    pallas_call x0 -> x2, Pallas kernels: none -> 139 us  [the longest x1 110 us: attention(): pl.pallas_call(functools.partial(attention_kernel, pairs, tokens), out_sh...]
    convert_element_type x18 -> x13, other arithmetic: 123 us -> 10.9 us  [the longest x7 7.93 us: reduce(): return lax.psum(share, 'seq').astype(f32)]
    reduce_sum x10 -> x7, other arithmetic: 62.8 us -> 9.52 us  [the longest x2 4.63 us: layer_norm_stats(): mean = jnp.mean(values, axis=1, keepdims=True)]
    slice x20 -> x2, local copies, waits for them, and re-layouts: 46.2 us -> 1.73 us  [the longest x1 1.64 us: body(): d_normed_both[:tokens].astype(bf)]
    another operation x10 -> x0, other arithmetic: 23.2 us -> none
    all_gather x1, blocking collectives: 19.3 us -> 40.1 us  [body(): gather = lambda w: lax.all_gather(w, 'rows', axis=0, tiled=True)]
    ppermute x4 -> x2, waiting for transfers between devices: 55 us -> 75.4 us  [the longest x1 75.4 us: body(): lax.ppermute(d_normed_both[:tokens].astype(bf), 'seq', [(i + 1, i) for i...]
  transfers between devices with their start and end apart: 13 -> 11, of which waited for: 8 -> 5; matrix products, arithmetic and copies ran while one was open for 68% -> 27% of each run, Pallas kernels for 0% -> 17%
where the time goes in v1:
time: 809 us; the launch traced here: 799 us
  waiting for transfers between devices  262 us (32%)
  matrix products  161 us (20%)
  blocking collectives  141 us (17%)
  Pallas kernels  139 us (17%)
  other arithmetic  45.8 us (6%)
  local copies, waits for them, and re-layouts  25.5 us (3%)
  between operations  16.5 us (2%)
    reduce_scatter x3, waiting for transfers between devices, reduce(): lax.psum_scatter(term.astype(bf), 'rows', scatter_dimension=0, tiled=True)  116 us
    pallas_call x1, Pallas kernels, attention(): pl.pallas_call(functools.partial(attention_kernel, pairs, tokens), out_sh...  110 us
    unnamed x2, blocking collectives  95.7 us
    ppermute x1, waiting for transfers between devices, body(): lax.ppermute(d_normed_both[:tokens].astype(bf), 'seq', [(i + 1, i) for i...  75.4 us
    all_gather x1, blocking collectives, body(): gather = lambda w: lax.all_gather(w, 'rows', axis=0, tiled=True)  40.1 us
    all_gather x4, waiting for transfers between devices, body(): gather = lambda w: lax.all_gather(w, 'rows', axis=0, tiled=True)  35.9 us
    psum x1, waiting for transfers between devices, reduce(): return lax.psum(share, 'seq').astype(f32)  32.8 us
    pallas_call x1, Pallas kernels, project(): pl.pallas_call(functools.partial(qkv_kernel, cols), out_shape=jax.ShapeDt...  29.4 us
  transfers between devices with their start and end apart: 11, of which 5 were waited for; matrix products, arithmetic and copies ran while one was open for 27% of the time, Pallas kernels for 17%

profile of v1, /device:TPU:0, one launch (start us, length us, event | category | flops | bytes accessed | tf_op | source)
XLA Modules:
  0.0 799.5 jit_solution(11042537723297190814)
XLA Ops:
  7.3 0.7 all-gather.8.cloned.1.call-update
  8.0 0.7 all-gather.6.cloned.1.call-update
  8.7 0.7 all-gather.10.cloned.1.call-update
  9.5 0.5 all-gather.12.cloned.1.call-update
  10.1 6.2 collective-permute-start
  16.2 1.3 fusion.53
  18.2 0.8 dynamic-update-slice
  19.1 0.8 dynamic-update-slice.1
  19.9 33.4 %all-reduce.8 = (bf16[1024]{0:T(1024)(128)(2,1)S(1)}, bf16[1024]{0:T(1024)(128)(2,1)S(1)}) all-reduce(bf16[1024]{0:T(1024)(128)(2,1)S(1)} %dynamic-update-slice.1, bf16[1024]{0:T(1024)(128)(2,1)S(1)} %dynamic-update-slice), channel_id=1, replica_groups=mesh['rows'=16,'seq'=2] {'rows'}, use_global_device_ids=true, to_apply=%add.1 | all-reduce | flops 2048 | bytes 8192
  53.3 0.8 select_reduce_fusion.1
  54.1 0.7 select_reduce_fusion
  55.0 1.0 copy.29.start_col
  56.0 1.9 convert_reduce_fusion
  58.0 0.5 and_select_fusion.lows
  58.5 0.7 fusion.24
  59.3 3.7 fusion.51
  63.0 2.7 convert_reduce_fusion.1
  65.7 2.3 fusion.25
  68.1 2.9 fusion.28
  71.0 1.3 copy-done.5
  72.3 0.7 copy-done.7
  73.0 2.5 pad_maximum_fusion.1.normed_ref
  75.5 5.9 fusion.45.do_ref
  81.4 35.8 %all-gather.6.cloned.1.call-done.w_ref = bf16[1024,3072]{1,0:T(8,128)(2,1)} async-done(((bf16[64,3072]{1,0:T(8,128)(2,1)}), bf16[1024,3072]{1,0:T(8,128)(2,1)}) %all-gather.6.cloned.1.call-update) | async-done | bytes 6291472 | tf_op jit(solution)/shard_map/all_gather | solution.py:251
  117.2 29.4 %project.1.q_ref.k_ref.v_ref = bf16[2048,3072]{1,0:T(8,128)(2,1)} custom-call(bf16[2048,1024]{1,0:T(8,128)(2,1)} %pad_maximum_fusion.1.normed_ref, bf16[1024,3072]{1,0:T(8,128)(2,1)} %all-gather.6.cloned.1.call-done.w_ref, f32[2048,128]{1,0:T(8,128)S(1)} %get-tuple-element.78.cos_ref, f32[2048,128]{1,0:T(8,128)S(1)} %get-tuple-element.77.sin_ref), custom_call_target="tpu_custom_call" | custom-call | flops 12000000000 | bytes 25165824 | tf_op jit(solution)/shard_map/project/pallas_call | solution.py:216
  146.7 110.0 %attention.1 = (bf16[1024,1024]{1,0:T(8,128)(2,1)}, bf16[1024,1024]{1,0:T(8,128)(2,1)}, bf16[2048,1024]{1,0:T(8,128)(2,1)}, bf16[2048,1024]{1,0:T(8,128)(2,1)}) custom-call(s32[4]{0:T(128)} %and_select_fusion.lows, s32[1024,1]{1,0:T(8,128)} %copy.29.start_col, s32[1,1024]{1,0:T(1,128)} %bitcast.56, f32[2048,128]{1,0:T(8,128)} %copy-done.1, ...), custom_call_target="tpu_custom_call" | custom-call | flops 60000002048 | bytes 31457280 | tf_op jit(solution)/shard_map/attention/pallas_call | solution.py:174
  256.7 4.1 convolution_convert_fusion.4
  260.9 4.8 convolution_convert_fusion.3
  265.7 4.8 convolution_convert_fusion.2
  270.5 13.5 %pad_maximum_fusion = bf16[1024,3072]{0,1:T(8,128)(2,1)} fusion(bf16[1024,1024]{0,1:T(8,128)(2,1)S(1)} %convolution_convert_fusion.2, bf16[1024,1024]{0,1:T(8,128)(2,1)S(1)} %convolution_convert_fusion.3, bf16[1024,1024]{0,1:T(8,128)(2,1)S(1)} %convolution_convert_fusion.4), kind=kLoop, calls=%fused_computation.13 | loop fusion | flops 18874368 | bytes 12582912 | tf_op jit(solution)/shard_map/concatenate | solution.py:282
  284.1 8.7 %copy.31 = bf16[1024,3072]{1,0:T(8,128)(2,1)} copy(bf16[1024,3072]{0,1:T(8,128)(2,1)} %pad_maximum_fusion) | data formatting | bytes 12582912
  292.8 0.6 copy-done.21
  293.4 40.1 %all-gather = bf16[16,1,256]{2,1,0:T(2,128)(2,1)S(1)} all-gather(bf16[1,1,256]{2,1,0:T(2,128)(2,1)S(1)} %reshape.76), channel_id=1, replica_groups=mesh['rows'=16,'seq'=2] {'rows'}, dimensions={0}, use_global_device_ids=true | all-gather | bytes 8704 | tf_op jit(solution)/shard_map/all_gather | solution.py:251
  333.6 5.9 fusion.48
  339.6 14.8 %fusion.56 = f32[1024,4096]{1,0:T(8,128)} fusion(bf16[1024,1024]{1,0:T(8,128)(2,1)S(1)} %copy-done.6, bf16[1024,4096]{1,0:T(8,128)(2,1)} %all-gather.10.cloned.1.call-done), kind=kOutput, calls=%fused_computation.88 | convolution fusion | flops 8589934592 | bytes 27262976 | tf_op jit(solution)/shard_map/dot_general | solution.py:288
  354.4 18.4 %convolution_convert_fusion = bf16[4096,1024]{1,0:T(8,128)(2,1)} fusion(bf16[1,1024,1024]{2,1,0:T(8,128)(2,1)S(1)} %copy-done.9, f32[1024,4096]{1,0:T(8,128)} %fusion.56, f32[4096]{0:T(1024)S(1)} %bitcast.57), kind=kOutput, calls=%fused_computation.11 | convolution fusion | flops 8636071936 | bytes 27279360 | tf_op jit(solution)/shard_map/dot_general | solution.py:293
  372.9 25.6 %fusion.54 = (bf16[4096]{0:T(1024)(128)(2,1)S(1)}, bf16[1024,4096]{1,0:T(8,128)(2,1)}) fusion(f32[1024,4096]{1,0:T(8,128)} %fusion.56, f32[4096]{0:T(1024)S(1)} %bitcast.58, bf16[4096,1024]{1,0:T(8,128)(2,1)} %all-gather.12.cloned.1.call-done, bf16[1,1024,1024]{2,1,0:T(8,128)(2,1)} %param.24), kind=kOutput, calls=%fused_computation.86 | convolution fusion | flops 8678010880 | bytes 35676160 | tf_op jit(solution)/shard_map/dot_general | solution.py:292
  398.5 14.9 %convolution_convert_fusion.1 = bf16[1024,4096]{1,0:T(8,128)(2,1)} fusion(bf16[1024,1024]{1,0:T(8,128)(2,1)S(1)} %copy-done.6, bf16[1024,4096]{1,0:T(8,128)(2,1)} %get-tuple-element.85), kind=kOutput, calls=%fused_computation.12 | convolution fusion | flops 8594128896 | bytes 18874368 | tf_op jit(solution)/shard_map/dot_general | solution.py:294
  413.5 7.2 fusion.35
  420.8 6.3 convolution_add_fusion
  427.0 3.2 copy-done.11
  430.2 1.6 slice.48
  431.9 1.3 collective-permute-start.1
  434.9 0.4 dynamic-update-slice.2
  435.3 6.8 fusion.55
  442.0 4.1 fusion.37
  446.2 75.4 %collective-permute-done.1 = bf16[1024,1024]{1,0:T(8,128)(2,1)} collective-permute-done((bf16[1024,1024]{1,0:T(8,128)(2,1)}, bf16[1024,1024]{1,0:T(8,128)(2,1)}, u32[]{:S(2)}, u32[]{:S(2)}) %collective-permute-start.1) | collective-permute-done | bytes 2097184 | tf_op jit(solution)/shard_map/ppermute | solution.py:281
  521.6 19.5 %fusion.23 = (bf16[1024]{0:T(1024)(128)(2,1)S(1)}, f32[1024]{0:T(1024)S(1)}, f32[1024]{0:T(1024)S(1)}, bf16[1024]{0:T(1024)(128)(2,1)S(1)}, f32[1024,1024]{1,0:T(8,128)}) fusion(f32[1024]{0:T(1024)S(1)} %copy-done.17, f32[1024]{0:T(1024)S(1)} %copy-done.13, bf16[1,1024,1024]{2,1,0:T(8,128)(2,1)S(1)} %copy-done.4, f32[1024]{0:T(1024)S(1)} %copy-done.15, ...), kind=kOutput, calls=%fused_computation.34 | convolution fusion | flops 8604610560 | bytes 33579008 | tf_op jit(solution)/shard_map/dot_general | solution.py:297
  541.0 62.2 %all-reduce.7 = (bf16[1024]{0:T(1024)(128)(2,1)S(1)}, bf16[1024]{0:T(1024)(128)(2,1)S(1)}, bf16[1024]{0:T(1024)(128)(2,1)S(1)}, bf16[4096]{0:T(1024)(128)(2,1)S(1)}, bf16[1024]{0:T(1024)(128)(2,1)S(1)}) all-reduce(bf16[1024]{0:T(1024)(128)(2,1)S(1)} %dynamic-update-slice.2, ...), channel_id=1, replica_groups=mesh['rows'=16,'seq'=2] {'rows'}, use_global_device_ids=true, to_apply=%add.2 | all-reduce | flops 8192 | bytes 32768
  603.3 2.2 copy.32
  605.5 7.1 reduce-scatter.11.cloned.1.call-done
  612.5 108.6 %reduce-scatter.9.cloned.1.call-done = bf16[64,4096]{1,0:T(8,128)(2,1)} async-done(((bf16[1024,4096]{1,0:T(8,128)(2,1)}), bf16[64,4096]{1,0:T(8,128)(2,1)}) %reduce-scatter.9.cloned.1.call-update) | async-done | bytes 524304 | tf_op jit(solution)/shard_map/reduce_scatter | solution.py:311
  721.1 18.3 %fusion.33 = bf16[1,1024,1024]{2,1,0:T(8,128)(2,1)} fusion(f32[1024,1024]{1,0:T(8,128)} %fusion.55, f32[1024]{0:T(1024)S(1)} %convert_element_type.112, bf16[4096,1024]{1,0:T(8,128)(2,1)} %all-gather.12.cloned.1.call-done, bf16[1,1024,1024]{2,1,0:T(8,128)(2,1)S(1)} %copy-done.4, f32[1024,4096]{1,0:T(8,128)} %fusion.56, f32[4096]{0:T(1024)S(1)} %bitcast.59), kind=kOutput, calls=%fused_computation.49 | convolution fusion | flops 8637120512 | bytes 33574912 | tf_op jit(solution)/shard_map/dot_general | solution.py:302
  739.7 5.0 all-reduce.9
  744.7 0.5 convert_element_type.118
  745.2 0.5 convert_element_type.120
  745.7 0.5 convert_element_type.132
  746.2 0.6 convert_element_type.129
  746.8 5.1 fusion.22
  751.9 32.8 %all-reduce.13.cloned.1.call-done = (bf16[64,3072]{0,1:T(8,128)(2,1)}, bf16[64,1024]{1,0:T(8,128)(2,1)}, bf16[64,4096]{1,0:T(8,128)(2,1)}, bf16[256,1024]{1,0:T(8,128)(2,1)}) async-done(((bf16[64,3072]{0,1:T(8,128)(2,1)}, bf16[64,1024]{1,0:T(8,128)(2,1)}, bf16[64,4096]{1,0:T(8,128)(2,1)}, bf16[256,1024]{1,0:T(8,128)(2,1)}), (bf16[64,3072]{0,1:T(8,128)(2,1)}, bf16[64,1024]{1,0:T(8,128)(2,1)}, ...) | async-done | bytes 1572880 | tf_op jit(solution)/shard_map/psum | solution.py:312
  784.6 2.3 copy.30
  786.9 1.6 convert_element_type.126
  788.5 2.1 convert_element_type.128
  790.6 2.1 convert_element_type.131
  (92 shorter events, 1.4 us)
Async XLA Ops:
  7.2 52.1 %copy-start.19 = (f32[128]{0:T(128)S(1)}, f32[128]{0:T(128)}, u32[]{:S(2)}) copy-start(f32[128]{0:T(128)} %constant.64) | copy-start | bytes 1540
  7.2 52.1 %copy-start.20 = (f32[128]{0:T(128)S(1)}, f32[128]{0:T(128)}, u32[]{:S(2)}) copy-start(f32[128]{0:T(128)} %constant.63) | copy-start | bytes 1540
  7.2 51.3 %copy-start.2 = (bf16[1,1024,1024]{2,1,0:T(8,128)(2,1)S(1)}, bf16[1,1024,1024]{2,1,0:T(8,128)(2,1)}, u32[]{:S(2)}) copy-start(bf16[1,1024,1024]{2,1,0:T(8,128)(2,1)} %param.14) | copy-start | bytes 6291460
  7.2 68.3 %all-gather.8.cloned.1.call-start = ((), (), s32[]{:S(2)}) async-start(), calls=%async_computation.5 | async-start | bytes 2228224 | tf_op jit(solution)/shard_map/all_gather | solution.py:251
  7.9 109.3 %all-gather.6.cloned.1.call-start = ((), (), s32[]{:S(2)}) async-start(), calls=%async_computation.4 | async-start | bytes 6684672 | tf_op jit(solution)/shard_map/all_gather | solution.py:251
  8.7 330.9 %all-gather.10.cloned.1.call-start = ((), (), s32[]{:S(2)}) async-start(), calls=%async_computation.6 | async-start | bytes 8912896 | tf_op jit(solution)/shard_map/all_gather | solution.py:251
  9.4 363.5 %all-gather.12.cloned.1.call-start = ((), (), s32[]{:S(2)}) async-start(), calls=%async_computation.7 | async-start | bytes 8912896 | tf_op jit(solution)/shard_map/all_gather | solution.py:251
  10.0 593.3 %reduce-scatter.13.cloned.1.call-start = ((), (), s32[]{:S(2)}) async-start(), calls=%async_computation.11 | async-start | bytes 6684672
  10.1 53.0 %collective-permute-start = (bf16[1024,1024]{1,0:T(8,128)(2,1)}, bf16[1024,1024]{1,0:T(8,128)(2,1)}, u32[]{:S(2)}, u32[]{:S(2)}) collective-permute-start(bf16[1024,1024]{1,0:T(8,128)(2,1)} %bitcast.54), channel_id=1, source_target_pairs={{0,1},{2,3},{4,5},{6,7},{8,9},{10,11},{12,13},{14,15},{16,17},{18,... | collective-permute-start | bytes 6291464 | tf_op jit(solution)/shard_map/ppermute | solution.py:253
  53.3 14.7 %copy-start.14 = (f32[1024]{0:T(1024)}, f32[1024]{0:T(1024)S(1)}, u32[]{:S(2)}) copy-start(f32[1024]{0:T(1024)S(1)} %convert_element_type.105) | copy-start | bytes 12292
  54.9 10.8 %copy-start.18 = (s32[1024]{0:T(1024)}, s32[1024]{0:T(1024)S(1)}, u32[]{:S(2)}) copy-start(s32[1024]{0:T(1024)S(1)} %fusion.52) | copy-start | bytes 12292
  58.5 9.5 %copy-start.12 = (f32[1024]{0:T(1024)}, f32[1024]{0:T(1024)S(1)}, u32[]{:S(2)}) copy-start(f32[1024]{0:T(1024)S(1)} %broadcast_multiply_fusion.2) | copy-start | bytes 12292
  58.5 9.5 %copy-start.3 = (bf16[1,1024,1024]{2,1,0:T(8,128)(2,1)S(1)}, bf16[1,1024,1024]{2,1,0:T(8,128)(2,1)}, u32[]{:S(2)}) copy-start(bf16[1,1024,1024]{2,1,0:T(8,128)(2,1)} %param.14) | copy-start | bytes 6291460
  59.2 11.8 %copy-start.16 = (f32[1024]{0:T(1024)}, f32[1024]{0:T(1024)S(1)}, u32[]{:S(2)}) copy-start(f32[1024]{0:T(1024)S(1)} %add_rsqrt_fusion) | copy-start | bytes 12292
  63.0 54.3 %copy-start = (f32[2048,128]{1,0:T(8,128)}, f32[2048,128]{1,0:T(8,128)S(1)}, u32[]{:S(2)}) copy-start(f32[2048,128]{1,0:T(8,128)S(1)} %get-tuple-element.77.sin_ref) | copy-start | bytes 3145732
  63.0 54.3 %copy-start.1 = (f32[2048,128]{1,0:T(8,128)}, f32[2048,128]{1,0:T(8,128)S(1)}, u32[]{:S(2)}) copy-start(f32[2048,128]{1,0:T(8,128)S(1)} %get-tuple-element.78.cos_ref) | copy-start | bytes 3145732
  71.0 1.3 copy-start.5
  71.0 2.0 copy-start.7
  146.7 110.0 %copy-start.6 = (bf16[1024,1024]{1,0:T(8,128)(2,1)S(1)}, bf16[1024,1024]{1,0:T(8,128)(2,1)}, u32[]{:S(2)}) copy-start(bf16[1024,1024]{1,0:T(8,128)(2,1)} %copy-done.5) | copy-start | bytes 6291460
  256.7 4.2 copy-start.8
  256.7 4.2 copy-start.26
  260.9 4.8 copy-start.24
  292.8 0.7 copy-start.21
  292.8 312.7 %reduce-scatter.7.cloned.1.call-start = ((), (), s32[]{:S(2)}) async-start(), calls=%async_computation.8 | async-start | bytes 2228224 | tf_op jit(solution)/shard_map/reduce_scatter | solution.py:311
  339.5 273.0 %reduce-scatter.11.cloned.1.call-start = ((), (), s32[]{:S(2)}) async-start(), calls=%async_computation.10 | async-start | bytes 8912896 | tf_op jit(solution)/shard_map/reduce_scatter | solution.py:311
  339.6 14.8 %copy-start.9 = (bf16[1,1024,1024]{2,1,0:T(8,128)(2,1)S(1)}, bf16[1,1024,1024]{2,1,0:T(8,128)(2,1)}, u32[]{:S(2)}) copy-start(bf16[1,1024,1024]{2,1,0:T(8,128)(2,1)} %param.24) | copy-start | bytes 6291460
  372.9 348.3 %reduce-scatter.9.cloned.1.call-start = ((), (), s32[]{:S(2)}) async-start(), calls=%async_computation.9 | async-start | bytes 8912896 | tf_op jit(solution)/shard_map/reduce_scatter | solution.py:311
  413.5 371.1 %all-reduce.13.cloned.1.call-start = ((), (), s32[]{:S(2)}) async-start(), calls=%async_computation.12 | async-start | bytes 3932160 | tf_op jit(solution)/shard_map/psum | solution.py:312
  413.5 7.2 copy-start.25
  427.0 3.2 copy-start.11
  430.2 4.2 copy-start.10
  430.2 4.6 copy-start.22
  431.9 89.7 %collective-permute-start.1 = (bf16[1024,1024]{1,0:T(8,128)(2,1)}, bf16[1024,1024]{1,0:T(8,128)(2,1)}, u32[]{:S(2)}, u32[]{:S(2)}) collective-permute-start(bf16[1024,1024]{1,0:T(8,128)(2,1)} %slice.48), channel_id=1, source_target_pairs={{1,0},{3,2},{5,4},{7,6},{9,8},{11,10},{13,12},{15,14},{17,16},{19,... | collective-permute-start | bytes 6291464 | tf_op jit(solution)/shard_map/ppermute | solution.py:281
  435.3 6.8 copy-start.23
  442.0 79.5 %copy-start.4 = (bf16[1,1024,1024]{2,1,0:T(8,128)(2,1)S(1)}, bf16[1,1024,1024]{2,1,0:T(8,128)(2,1)}, u32[]{:S(2)}) copy-start(bf16[1,1024,1024]{2,1,0:T(8,128)(2,1)} %param.14) | copy-start | bytes 6291460
  442.0 79.5 %copy-start.13 = (f32[1024]{0:T(1024)S(1)}, f32[1024]{0:T(1024)}, u32[]{:S(2)}) copy-start(f32[1024]{0:T(1024)} %copy-done.12) | copy-start | bytes 12292
  442.0 79.5 %copy-start.15 = (f32[1024]{0:T(1024)S(1)}, f32[1024]{0:T(1024)}, u32[]{:S(2)}) copy-start(f32[1024]{0:T(1024)} %copy-done.14) | copy-start | bytes 12292
  442.0 79.5 %copy-start.17 = (f32[1024]{0:T(1024)S(1)}, f32[1024]{0:T(1024)}, u32[]{:S(2)}) copy-start(f32[1024]{0:T(1024)} %copy-done.16) | copy-start | bytes 12292
Sparse Core Ops, SparseCore 0:
  10.2 44.0 all-gather.7
  56.6 60.5 all-gather.5
  119.4 73.4 all-gather.9
  195.0 73.2 all-gather.11
  292.9 146.6 reduce-scatter.12
  443.7 60.6 reduce-scatter.6
  508.5 104.0 reduce-scatter.10
  616.6 104.4 reduce-scatter.8
  724.2 60.4 all-reduce.12

commit v2 on v1

--- a/solution.py
+++ b/solution.py
@@ -246,10 +246,354 @@
     return centered * scale, scale
 
 
+MESH = pl.DeviceIdType.MESH
+RING = 12
+SLOTS = 4
+
+
+def reduce_kernel(dims, g_qkv, g_out, normed, normed_t, grad, grad_t, x_ref, w_in, w_back, b_in, base_out, base_dn,
+                  vec_in, o_qkv, o_out, o_in, o_back, o_vec, block_out, d_normed,
+                  buf, core_recv, chip, x_recv, y_recv, part, z_recv, fin, fin_recv, res, acc_out, hidden, d_pre, win_buf, wback_buf,
+                  vec, vec_recv, load_sem, acc_sem, w_sem, send_sem, recv_sem, zsend_sem, zrecv_sem, vsend_sem, vrecv_sem):
+    rows, seqs, q_rows, edge, tokens, width, ff = dims
+    bf, f32 = jnp.bfloat16, jnp.float32
+    levels = rows // 4
+    region = q_rows - edge
+    r, s = lax.axis_index("rows"), lax.axis_index("seq")
+    core, y, z = lax.rem(r, 2), lax.rem(r // 2, 2), r // 4
+    odd = lax.rem(s, 2)
+    core_id = {"rows": r + 1 - 2 * core}
+    y_id = {"rows": r + 2 - 4 * y}
+    flip = lambda bit: {"seq": s + bit - 2 * bit * lax.rem(s // bit, 2)}
+    z_of = lambda d: lax.rem(z + d, levels)
+    z_id = lambda d: {"rows": z_of(d) * 4 + lax.rem(r, 4)}
+    bits = []
+    while 2 ** (len(bits) + 1) < seqs:
+        bits.append(2 ** (len(bits) + 1))
+    finals = bits + [1]
+
+    barrier = pltpu.get_barrier_semaphore()
+    partners = [core_id, y_id] + [z_id(d) for d in range(1, levels)] + [flip(b) for b in finals]
+    for partner in partners:
+        pl.semaphore_signal(barrier, inc=1, device_id=partner, device_id_type=MESH)
+    pl.semaphore_wait(barrier, len(partners))
+
+    piece = q_rows // 4
+    n_qkv, n_out, n_in, n_back = 3 * width // 512, width // 512, ff // 512, width // 128
+    n_first = n_qkv + n_out
+    n_mlp = n_first + n_in
+    total = n_mlp + n_back
+    own_rows = pl.ds(pl.multiple_of(odd * edge, edge), region)
+    c_mine = pl.ds(pl.multiple_of(odd * (q_rows - edge), edge), edge)
+    c_other = pl.ds(pl.multiple_of((1 - odd) * (q_rows - edge), edge), edge)
+
+    def remote(src, dst, stage, slot, target):
+        return pltpu.make_async_remote_copy(src, dst, send_sem.at[stage, slot], recv_sem.at[stage, slot],
+                                            device_id=target, device_id_type=MESH)
+
+    def core_copy(k):
+        return remote(buf.at[lax.rem(k, RING), :, 1 - core], core_recv.at[lax.rem(k, SLOTS)], 0, lax.rem(k, SLOTS), core_id)
+
+    def x_copy(k):
+        t = lax.rem(k, SLOTS)
+        return remote(chip.at[t, :, :, c_other], x_recv.at[t], 1, t, flip(1))
+
+    def y_copy(k):
+        t = lax.rem(k, SLOTS)
+        return remote(chip.at[t, :, 1 - y, own_rows], y_recv.at[t], 2, t, y_id)
+
+    def z_copy(k, d):
+        t = lax.rem(k, SLOTS)
+        return pltpu.make_async_remote_copy(part.at[t, z_of(d)], z_recv.at[t, d - 1], zsend_sem.at[d - 1, t],
+                                            zrecv_sem.at[d - 1, t], device_id=z_id(d), device_id_type=MESH)
+
+    def fin_copy(k, i):
+        t = lax.rem(k, SLOTS)
+        return remote(fin.at[t, i], fin_recv.at[t, i], 3 + i, t, flip(finals[i]))
+
+    def load_copies(source, col, k):
+        slot = lax.rem(k, RING)
+        return [pltpu.make_async_copy(source.at[:, :, :, pl.ds(pl.multiple_of(col + 128 * j, 128), 128)],
+                                      buf.at[slot, :, :, pl.ds(j * piece, piece)], load_sem.at[j]) for j in range(4)]
+
+    def load(k):
+        @pl.when(k < n_qkv)
+        def _():
+            for copy in load_copies(g_qkv, k * 512, k):
+                copy.start()
+
+        @pl.when((k >= n_qkv) & (k < n_first))
+        def _():
+            for copy in load_copies(g_out, (k - n_qkv) * 512, k):
+                copy.start()
+
+    def weights(j):
+        t = lax.rem(j, 2)
+        cols = pl.ds(pl.multiple_of(j * 512, 512), 512)
+        return [pltpu.make_async_copy(w_in.at[:, cols], win_buf.at[t], w_sem.at[0, t]),
+                pltpu.make_async_copy(w_back.at[cols, :], wback_buf.at[t], w_sem.at[1, t])]
+
+    starts = [pltpu.make_async_copy(base_out, acc_out, acc_sem.at[0]), pltpu.make_async_copy(base_dn, d_normed, acc_sem.at[1])]
+    for copy in weights(0) + starts:
+        copy.start()
+    load(0)
+
+    def mlp(j):
+        @pl.when(j == 0)
+        def _():
+            for copy in starts:
+                copy.wait()
+        for copy in weights(j):
+            copy.wait()
+
+        @pl.when(j + 1 < n_in)
+        def _():
+            for copy in weights(j + 1):
+                copy.start()
+        t = lax.rem(j, 2)
+        cols = pl.ds(pl.multiple_of(j * 512, 512), 512)
+        tall = 512
+        bias = b_in[:, cols]
+
+        def rows_step(i, sums):
+            block = pl.ds(pl.multiple_of(i * tall, tall), tall)
+            pre = dot_n(normed[block, :], win_buf[t]) + bias
+            up = dot_t(grad[block, :], wback_buf[t])
+            square = pre * pre
+            turn = jnp.tanh(pre * (GELU_COEF + (GELU_COEF * 0.044715) * square))
+            half = 0.5 + 0.5 * turn
+            hid = (pre * half).astype(bf)
+            slope = half + (0.5 * pre) * (1.0 - turn * turn) * (GELU_COEF + (3 * 0.044715 * GELU_COEF) * square)
+            down = (up * slope).astype(bf)
+            hidden[block, cols] = hid
+            d_pre[block, :] = down
+            acc_out[block, :] += dot_n(hid, wback_buf[t])
+            d_normed[block, :] += dot_t(down, win_buf[t])
+            return sums + jnp.sum(down.astype(f32), axis=0, keepdims=True)
+        sums = lax.fori_loop(0, tokens // tall, rows_step, jnp.zeros((1, 512), f32))
+        vec[pl.ds(3 + j // 2, 1), pl.ds(pl.multiple_of(lax.rem(j, 2) * 512, 512), 512)] = sums
+        slot = lax.rem(n_first + j, RING)
+        per = 8
+        big = per * width // rows
+
+        def grads_step(i, _):
+            value = dot_n(normed_t[pl.ds(pl.multiple_of(i * big, big), big), :], d_pre[...]).astype(bf)
+            for m in range(per):
+                for a in range(4):
+                    buf[slot, i * (per // 2) + m // 2, m % 2, a * piece:(a + 1) * piece, :] = (
+                        value[m * piece:(m + 1) * piece, a * 128:(a + 1) * 128])
+            return 0
+        lax.fori_loop(0, rows // per, grads_step, 0)
+
+    def finish_tokens():
+        gain = vec_in[0:1, :]
+        bias = vec_in[1:2, :]
+        back = jnp.zeros((1, width), f32)
+        tall = 256
+        def step(i, sums):
+            gain, bias, back = sums
+            block = pl.ds(pl.multiple_of(i * tall, tall), tall)
+            block_out[block, :] = acc_out[block, :].astype(bf)
+            values = x_ref[block, :].astype(f32)
+            centered = values - jnp.mean(values, axis=1, keepdims=True)
+            unit = centered * lax.rsqrt(jnp.mean(centered * centered, axis=1, keepdims=True) + EPS)
+            d = d_normed[block, :]
+            return (gain + jnp.sum(d * unit, axis=0, keepdims=True), bias + jnp.sum(d, axis=0, keepdims=True),
+                    back + jnp.sum(grad[block, :].astype(f32), axis=0, keepdims=True))
+        gain, bias, back = lax.fori_loop(0, tokens // tall, step, (gain, bias, back))
+        vec[0:1, :] = gain
+        vec[1:2, :] = bias
+        vec[2:3, :] = back
+        vec[7:8, :] = jnp.zeros((1, width), f32)
+
+    def back_grads(j):
+        value = dot_n(grad_t[pl.ds(pl.multiple_of(j * 128, 128), 128), :], hidden[...]).astype(bf)
+        slot = lax.rem(n_mlp + j, RING)
+        parts = q_rows // 128
+        for d in range(rows):
+            for a in range(parts):
+                buf[slot, d // 2, d % 2, a * 128:(a + 1) * 128, :] = value[:, (d * parts + a) * 128:(d * parts + a + 1) * 128]
+
+    def vec_copy(i, target):
+        return pltpu.make_async_remote_copy(vec, vec_recv.at[i], vsend_sem.at[i], vrecv_sem.at[i],
+                                            device_id=target, device_id_type=MESH)
+    vec_stages = [[(0, core_id)], [(1, y_id)], [(2 + d - 1, z_id(d)) for d in range(1, levels)]]
+    vec_stages += [[(1 + levels + i, flip(b))] for i, b in enumerate(finals)]
+
+    def store(k):
+        def place(out, col):
+            for j in range(4):
+                out[:, pl.ds(pl.multiple_of(col + 128 * j, 128), 128)] = res[j * piece:(j + 1) * piece, :]
+
+        @pl.when(k < n_qkv)
+        def _():
+            place(o_qkv, k * 512)
+
+        @pl.when((k >= n_qkv) & (k < n_first))
+        def _():
+            place(o_out, (k - n_qkv) * 512)
+
+        @pl.when((k >= n_first) & (k < n_mlp))
+        def _():
+            place(o_in, (k - n_first) * 512)
+
+        @pl.when(k >= n_mlp)
+        def _():
+            for a in range(q_rows // 128):
+                o_back[a * 128:(a + 1) * 128, pl.ds(pl.multiple_of((k - n_mlp) * 128, 128), 128)] = (
+                    res[a * 128:(a + 1) * 128, :].T)
+
+    def stage(lag, it, body):
+        k = it - lag
+
+        @pl.when((k >= 0) & (k < total))
+        def _():
+            body(k, lax.rem(k, SLOTS))
+
+    def send_first(k, t):
+        @pl.when(k < n_first)
+        def _():
+            for copy in load_copies(g_qkv, 0, k):
+                copy.wait()
+        load(k + 1)
+        core_copy(k).start()
+
+    def core_add(k, t):
+        core_copy(k).wait()
+        slot = lax.rem(k, RING)
+        for i in range(rows // 2):
+            chip[t, i // 2, i % 2] = buf[slot, i, core] + core_recv[t, i]
+        x_copy(k).start()
+
+    def x_add(k, t):
+        x_copy(k).wait()
+        for i in range(rows // 2):
+            chip[t, i // 2, i % 2, c_mine] = chip[t, i // 2, i % 2, c_mine] + x_recv[t, i // 2, i % 2]
+        y_copy(k).start()
+
+    def y_add(k, t):
+        y_copy(k).wait()
+        for i in range(levels):
+            part[t, i] = chip[t, i, y, own_rows] + y_recv[t, i]
+        for d in range(1, levels):
+            z_copy(k, d).start()
+
+    def z_add(k, t):
+        for d in range(1, levels):
+            z_copy(k, d).wait()
+        value = part[t, z].astype(f32)
+        for d in range(1, levels):
+            value = value + z_recv[t, d - 1].astype(f32)
+        fin[t, 0] = value.astype(bf)
+        fin_copy(k, 0).start()
+
+    def fin_add(i):
+        def body(k, t):
+            fin_copy(k, i).wait()
+            fin[t, i + 1] = fin[t, i] + fin_recv[t, i]
+            fin_copy(k, i + 1).start()
+        return body
+
+    def last(k, t):
+        i = len(finals) - 1
+        fin_copy(k, i).wait()
+        middle = q_rows - 2 * edge
+        at = lambda start, size: pl.ds(pl.multiple_of(start, edge), size)
+        res[c_mine, :] = fin[t, i, at(odd * middle, edge)].astype(f32)
+        res[c_other, :] = fin_recv[t, i, at((1 - odd) * middle, edge)].astype(f32)
+        res[edge:q_rows - edge, :] = (fin[t, i, at((1 - odd) * edge, middle)].astype(f32)
+                                      + fin_recv[t, i, at(odd * edge, middle)].astype(f32))
+        store(k)
+
+    pipeline = [send_first, core_add, x_add, y_add, z_add] + [fin_add(i) for i in range(len(bits))] + [last]
+
+    def step(it, _):
+        for lag, body in enumerate(pipeline):
+            stage(lag, it, body)
+
+        @pl.when(it < n_in)
+        def _():
+            mlp(it)
+
+        @pl.when(it == n_in)
+        def _():
+            finish_tokens()
+            for i, target in vec_stages[0]:
+                vec_copy(i, target).start()
+        for number, stages in enumerate(vec_stages):
+            @pl.when(it == n_in + 1 + number)
+            def _():
+                for i, target in stages:
+                    vec_copy(i, target).wait()
+                value = vec[...]
+                for i, target in stages:
+                    value = value + vec_recv[i]
+                if number + 1 < len(vec_stages):
+                    vec[...] = value
+                    for i, target in vec_stages[number + 1]:
+                        vec_copy(i, target).start()
+                else:
+                    o_vec[...] = value
+
+        @pl.when((it >= n_in) & (it < n_in + n_back))
+        def _():
+            back_grads(it - n_in)
+        return 0
+    lax.fori_loop(0, total + len(pipeline) - 1, step, 0)
+
+
+def reduce_all(rows, seqs, g_qkv, g_out, normed, normed_t, grad, grad_t, x, w_in, w_back, b_in, base_out, base_dn, vec_in):
+    tokens, width = normed.shape
+    ff = w_in.shape[1]
+    share = width // rows
+    q_rows = 4 * share
+    edge = q_rows // 4
+    levels = rows // 4
+    region = q_rows - edge
+    finals = max(1, (seqs - 1).bit_length())
+    bf, f32 = jnp.bfloat16, jnp.float32
+    vmem, hbm = pl.BlockSpec(memory_space=pltpu.VMEM), pl.BlockSpec(memory_space=pl.ANY)
+    dma = pltpu.SemaphoreType.DMA
+    return pl.pallas_call(
+        functools.partial(reduce_kernel, (rows, seqs, q_rows, edge, tokens, width, ff)),
+        out_shape=[jax.ShapeDtypeStruct((share, 3 * width), f32), jax.ShapeDtypeStruct((share, width), f32),
+                   jax.ShapeDtypeStruct((share, ff), f32), jax.ShapeDtypeStruct((ff // rows, width), f32),
+                   jax.ShapeDtypeStruct((8, width), f32), jax.ShapeDtypeStruct((tokens, width), bf),
+                   jax.ShapeDtypeStruct((tokens, width), f32)],
+        in_specs=[hbm, hbm, vmem, vmem, vmem, vmem, vmem, hbm, hbm, vmem, hbm, hbm, vmem],
+        out_specs=[vmem] * 7,
+        scratch_shapes=[
+            pltpu.VMEM((RING, rows // 2, 2, q_rows, 128), bf),
+            pltpu.VMEM((SLOTS, rows // 2, q_rows, 128), bf),
+            pltpu.VMEM((SLOTS, levels, 2, q_rows, 128), bf),
+            pltpu.VMEM((SLOTS, levels, 2, edge, 128), bf),
+            pltpu.VMEM((SLOTS, levels, region, 128), bf),
+            pltpu.VMEM((SLOTS, levels, region, 128), bf),
+            pltpu.VMEM((SLOTS, levels - 1, region, 128), bf),
+            pltpu.VMEM((SLOTS, finals, region, 128), bf),
+            pltpu.VMEM((SLOTS, finals, region, 128), bf),
+            pltpu.VMEM((q_rows, 128), f32),
+            pltpu.VMEM((tokens, width), f32),
+            pltpu.VMEM((tokens, ff), bf),
+            pltpu.VMEM((tokens, 512), bf),
+            pltpu.VMEM((2, width, 512), bf),
+            pltpu.VMEM((2, 512, width), bf),
+            pltpu.VMEM((8, width), f32),
+            pltpu.VMEM((1 + levels + finals, 8, width), f32),
+            dma((4,)), dma((2,)), dma((2, 2)), dma((3 + finals, SLOTS)), dma((3 + finals, SLOTS)),
+            dma((levels - 1, SLOTS)), dma((levels - 1, SLOTS)), dma((1 + levels + finals,)), dma((1 + levels + finals,)),
+        ],
+        compiler_params=pltpu.CompilerParams(collective_id=1, has_side_effects=True, vmem_limit_bytes=62 * 2**20),
+        cost_estimate=pl.CostEstimate(flops=100 * 10**9, bytes_accessed=100 * 2**20, transcendentals=0),
+        name="reduce",
+    )(g_qkv.reshape(rows // 2, 2, share, 3 * width), g_out.reshape(rows // 2, 2, share, width), normed, normed_t, grad, grad_t, x,
+      w_in, w_back, b_in, base_out, base_dn, vec_in)
+
+
 def body(block_input, lengths, norm_gain, norm_bias, w_qkv, w_attn_out, w_fc_in, b_fc_in, w_fc_out, b_fc_out, cotangent):
     f32, bf = jnp.float32, jnp.bfloat16
     gather = lambda w: lax.all_gather(w, "rows", axis=0, tiled=True)
-    seqs = lax.axis_size("seq")
+    rows, seqs = lax.axis_size("rows"), lax.axis_size("seq")
     prior_input = lax.ppermute(block_input[0], "seq", [(i, i + 1) for i in range(seqs - 1)])
     gain, bias = gather(norm_gain).astype(f32), gather(norm_bias).astype(f32)
     w_qkv_all, w_out_all = gather(w_qkv), gather(w_attn_out)
@@ -278,41 +622,31 @@
 
     d_normed_both = jnp.dot(d_k, w_qkv_all[:, width:2 * width].T, preferred_element_type=f32) + jnp.dot(
         d_v, w_qkv_all[:, 2 * width:].T, preferred_element_type=f32)
-    back = lax.ppermute(d_normed_both[:tokens].astype(bf), "seq", [(i + 1, i) for i in range(seqs - 1)])
+    d_prior = d_normed_both[:tokens]
+    back = lax.ppermute(d_prior.astype(bf), "seq", [(i + 1, i) for i in range(seqs - 1)])
+    vec_in = jnp.stack([jnp.sum(d_prior * prior_unit, axis=0), jnp.sum(d_prior, axis=0)])
     grad_w_qkv = jnp.concatenate([
         jnp.dot(normed.T, d_q, preferred_element_type=f32).astype(bf),
         jnp.dot(normed_both.T, d_k, preferred_element_type=f32).astype(bf),
         jnp.dot(normed_both.T, d_v, preferred_element_type=f32).astype(bf)], axis=1)
     grad_w_out = jnp.dot(attended.T, grad_out, preferred_element_type=f32).astype(bf)
-
-    pre = jnp.dot(normed, w_in_all, preferred_element_type=f32) + b_in_all.astype(f32)
-    turn = jnp.tanh(GELU_COEF * (pre + 0.044715 * pre * pre * pre))
-    hidden = (0.5 * pre * (1.0 + turn)).astype(bf)
-    slope = 0.5 * (1.0 + turn) + 0.5 * pre * (1.0 - turn * turn) * (GELU_COEF * (1.0 + 3 * 0.044715 * pre * pre))
-    d_pre = (jnp.dot(grad_out, w_back_all.T, preferred_element_type=f32) * slope).astype(bf)
-    grad_w_back = jnp.dot(hidden.T, grad_out, preferred_element_type=f32).astype(bf)
-    grad_w_in = jnp.dot(normed.T, d_pre, preferred_element_type=f32).astype(bf)
-    grad_b_back = jnp.sum(grad_out.astype(f32), axis=0)
-    grad_b_in = jnp.sum(d_pre.astype(f32), axis=0)
-    d_normed = jnp.dot(d_pre, w_in_all.T, preferred_element_type=f32)
-    d_normed = d_normed + jnp.dot(d_q, w_qkv_all[:, :width].T, preferred_element_type=f32)
-    d_normed = d_normed + d_normed_both[tokens:] + back.astype(f32)
-
-    block_output = (inputs + jnp.dot(attended, w_out_all, preferred_element_type=f32)
-                    + jnp.dot(hidden, w_back_all, preferred_element_type=f32) + b_back_all.astype(f32)).astype(bf)
-    grad_gain = jnp.sum(d_normed * unit, axis=0)
-    grad_bias = jnp.sum(d_normed, axis=0)
+    base_dn = d_normed_both[tokens:] + jnp.dot(d_q, w_qkv_all[:, :width].T, preferred_element_type=f32)
+    base_out = inputs + jnp.dot(attended, w_out_all, preferred_element_type=f32) + b_back_all.astype(f32)
+
+    g_qkv, g_out, g_in, g_back, vec, block_output, d_normed = reduce_all(
+        rows, seqs, grad_w_qkv, grad_w_out, normed, normed.T, grad_out, grad_out.T, block_input[0], w_in_all, w_back_all,
+        b_in_all.astype(f32)[None], base_out, base_dn, vec_in)
+
+    d_normed = d_normed + back.astype(f32)
     d_unit = d_normed * gain
     d_input = (d_unit - jnp.mean(d_unit, axis=1, keepdims=True)
                - unit * jnp.mean(d_unit * unit, axis=1, keepdims=True)) * scale
     grad_input = d_input + grad_out.astype(f32)
-
-    def reduce(term):
-        share = lax.psum_scatter(term.astype(bf), "rows", scatter_dimension=0, tiled=True)
-        return lax.psum(share, "seq").astype(f32)
-
-    return (block_output[None], grad_input[None], reduce(grad_gain), reduce(grad_bias), reduce(grad_w_qkv),
-            reduce(grad_w_out), reduce(grad_w_in), reduce(grad_b_in), reduce(grad_w_back), reduce(grad_b_back))
+    share, wide = width // rows, 4 * width // rows
+    r = lax.axis_index("rows")
+    own = lambda vector, size: lax.dynamic_slice_in_dim(vector, r * size, size)
+    return (block_output[None], grad_input[None], own(vec[0], share), own(vec[1], share), g_qkv, g_out, g_in,
+            own(vec[3:7].reshape(4 * width), wide), g_back, own(vec[2], share))
 
 
 def solution(mesh):

time: 809 us -> 593 us (0.73)
  waiting for transfers between devices: 262 us -> 11.3 us
  Pallas kernels: 139 us -> 371 us
  matrix products: 161 us -> 47.6 us
  blocking collectives: 141 us -> 51 us
    pallas_call x0 -> x1, Pallas kernels: none -> 232 us  [reduce_all(): pl.pallas_call(functools.partial(reduce_kernel, (rows, seqs, q_rows, edge...]
    reduce_scatter x3 -> x0, waiting for transfers between devices: 116 us -> none  [reduce(): lax.psum_scatter(term.astype(bf), 'rows', scatter_dimension=0, tiled=True)]
    dot_general x6 -> x0, matrix products: 112 us -> none  [the longest x1 25.6 us: body(): jnp.dot(grad_out, w_back_all.T, preferred_element_type=f32) * slope]
    ppermute x1, waiting for transfers between devices: 75.4 us -> 0.01 us  [body(): lax.ppermute(d_prior.astype(bf), 'seq', [(i + 1, i) for i in range(seqs -...]
    unnamed x2 -> x1, blocking collectives: 95.7 us -> 33.8 us
    psum x1 -> x0, waiting for transfers between devices: 32.8 us -> none  [reduce(): return lax.psum(share, 'seq').astype(f32)]
    all_gather x4, waiting for transfers between devices: 35.9 us -> 9.22 us  [body(): gather = lambda w: lax.all_gather(w, 'rows', axis=0, tiled=True)]
    all_gather x1, blocking collectives: 40.1 us -> 17.2 us  [body(): gather = lambda w: lax.all_gather(w, 'rows', axis=0, tiled=True)]
  transfers between devices with their start and end apart: 11 -> 6, of which waited for: 5 -> 1; matrix products, arithmetic and copies ran while one was open for 27% -> 19% of each run, Pallas kernels for 17% -> 64%
where the time goes in v2:
time: 593 us; the launch traced here: 584 us
  Pallas kernels  371 us (63%)
  blocking collectives  51 us (9%)
  other arithmetic  47.6 us (8%)
  matrix products  47.6 us (8%)
  local copies, waits for them, and re-layouts  32.5 us (5%)
  between operations  15 us (3%)
  waiting for transfers between devices  11.3 us (2%)
  starting transfers between devices  7.87 us (1%)
    pallas_call x1, Pallas kernels, reduce_all(): pl.pallas_call(functools.partial(reduce_kernel, (rows, seqs, q_rows, edge...  232 us
    pallas_call x1, Pallas kernels, attention(): pl.pallas_call(functools.partial(attention_kernel, pairs, tokens), out_sh...  110 us
    unnamed x1, blocking collectives  33.8 us
    pallas_call x1, Pallas kernels, project(): pl.pallas_call(functools.partial(qkv_kernel, cols), out_shape=jax.ShapeDt...  29.4 us
    all_gather x1, blocking collectives, body(): gather = lambda w: lax.all_gather(w, 'rows', axis=0, tiled=True)  17.2 us
    concatenate x1, other arithmetic, body(): jnp.concatenate([jnp.dot(normed.T, d_q, preferred_element_type=f32).astyp...  13.1 us
  transfers between devices with their start and end apart: 6, of which 1 were waited for; matrix products, arithmetic and copies ran while one was open for 19% of the time, Pallas kernels for 64%

profile of v2, /device:TPU:0, one launch (start us, length us, event | category | flops | bytes accessed | tf_op | source)
XLA Modules:
  0.0 583.9 jit_solution(12342676858510142771)
XLA Ops:
  7.2 0.0 all-gather.8.cloned.1.call-start
  7.2 0.7 all-gather.8.cloned.1.call-update
  7.9 0.0 all-gather.6.cloned.1.call-start
  8.0 0.7 all-gather.6.cloned.1.call-update
  8.7 0.0 all-gather.10.cloned.1.call-start
  8.7 0.7 all-gather.10.cloned.1.call-update
  9.4 0.0 all-gather.12.cloned.1.call-start
  9.5 6.2 %collective-permute-start = (bf16[1024,1024]{1,0:T(8,128)(2,1)}, bf16[1024,1024]{1,0:T(8,128)(2,1)}, u32[]{:S(2)}, u32[]{:S(2)}) collective-permute-start(bf16[1024,1024]{1,0:T(8,128)(2,1)} %bitcast.51), channel_id=1, source_target_pairs={{0,1},{2,3},{4,5},{6,7},{8,9},{10,11},{12,13},{14,15},{16,17},{18,... | collective-permute-start | bytes 6291464 | tf_op jit(solution)/shard_map/ppermute | solution.py:597
  15.6 0.0 all-gather.12.cloned.1.call-update
  15.7 1.2 dynamic-slice.3
  17.6 0.8 dynamic-update-slice
  18.4 0.8 dynamic-update-slice.1
  19.3 0.8 dynamic-update-slice.2
  20.1 33.8 %all-reduce.3 = (bf16[1024]{0:T(1024)(128)(2,1)S(1)}, bf16[1024]{0:T(1024)(128)(2,1)S(1)}, bf16[1024]{0:T(1024)(128)(2,1)S(1)}) all-reduce(bf16[1024]{0:T(1024)(128)(2,1)S(1)} %dynamic-update-slice.1, bf16[1024]{0:T(1024)(128)(2,1)S(1)} %dynamic-update-slice, ...), channel_id=1, replica_groups=mesh['rows'=16,'seq'=2] {'rows'}, use_global_device_ids=true, to_apply=%add.1 | all-reduce | flops 3072 | bytes 12288
  54.0 0.8 select_reduce_fusion.1
  54.8 0.7 select_reduce_fusion
  55.6 0.1 slice.34
  55.7 1.0 copy.35.start_col
  56.7 4.0 copy.38.grad_t
  60.7 17.2 %all-gather = bf16[16,1,256]{2,1,0:T(2,128)(2,1)S(1)} all-gather(bf16[1,1,256]{2,1,0:T(2,128)(2,1)S(1)} %reshape.91), channel_id=1, replica_groups=mesh['rows'=16,'seq'=2] {'rows'}, dimensions={0}, use_global_device_ids=true | all-gather | bytes 8704 | tf_op jit(solution)/shard_map/all_gather | solution.py:595
  77.9 0.6 convert.1.b_in
  78.5 0.3 convert_reduce_fusion
  78.9 0.5 and_select_fusion.lows
  79.4 0.7 fusion.19
  80.1 3.7 fusion.30
  83.9 3.1 convert_reduce_fusion.1
  87.0 2.3 fusion.20
  89.3 4.4 fusion.10
  93.7 3.9 copy.37.normed_t
  97.7 4.7 pad_maximum_fusion.1.normed_ref
  102.4 5.9 %convolution_convert_fusion.4.do_ref = bf16[1024,1024]{1,0:T(8,128)(2,1)} fusion(bf16[1024,1024]{1,0:T(8,128)(2,1)} %all-gather.8.cloned.1.call-done, bf16[1,1024,1024]{2,1,0:T(8,128)(2,1)} %param.24), kind=kOutput, calls=%fused_computation.43 | convolution fusion | flops 2148532224 | bytes 6291456 | tf_op jit(solution)/shard_map/dot_general | solution.py:620
  108.3 9.2 %all-gather.6.cloned.1.call-done.w_ref = bf16[1024,3072]{1,0:T(8,128)(2,1)} async-done(((bf16[64,3072]{1,0:T(8,128)(2,1)}), bf16[1024,3072]{1,0:T(8,128)(2,1)}) %all-gather.6.cloned.1.call-update) | async-done | bytes 6291472 | tf_op jit(solution)/shard_map/all_gather | solution.py:595
  117.5 29.4 %project.1.q_ref.k_ref.v_ref = bf16[2048,3072]{1,0:T(8,128)(2,1)} custom-call(bf16[2048,1024]{1,0:T(8,128)(2,1)} %pad_maximum_fusion.1.normed_ref, bf16[1024,3072]{1,0:T(8,128)(2,1)} %all-gather.6.cloned.1.call-done.w_ref, f32[2048,128]{1,0:T(8,128)S(1)} %get-tuple-element.43.cos_ref, f32[2048,128]{1,0:T(8,128)S(1)} %get-tuple-element.42.sin_ref), custom_call_target="tpu_custom_call" | custom-call | flops 12000000000 | bytes 25165824 | tf_op jit(solution)/shard_map/project/pallas_call | solution.py:216
  146.9 109.8 %attention.1 = (bf16[1024,1024]{1,0:T(8,128)(2,1)}, bf16[1024,1024]{1,0:T(8,128)(2,1)}, bf16[2048,1024]{1,0:T(8,128)(2,1)}, bf16[2048,1024]{1,0:T(8,128)(2,1)}) custom-call(s32[4]{0:T(128)} %and_select_fusion.lows, s32[1024,1]{1,0:T(8,128)} %copy.35.start_col, s32[1,1024]{1,0:T(1,128)} %bitcast.61, f32[2048,128]{1,0:T(8,128)} %copy-done.1, ...), custom_call_target="tpu_custom_call" | custom-call | flops 60000002048 | bytes 31457280 | tf_op jit(solution)/shard_map/attention/pallas_call | solution.py:174
  256.7 4.1 convolution_convert_fusion.3
  260.9 5.3 convolution_convert_fusion.2
  266.2 4.8 convolution_convert_fusion.1
  271.0 13.1 %pad_maximum_fusion = bf16[1024,3072]{0,1:T(8,128)(2,1)} fusion(bf16[1024,1024]{0,1:T(8,128)(2,1)S(1)} %convolution_convert_fusion.1, bf16[1024,1024]{0,1:T(8,128)(2,1)S(1)} %convolution_convert_fusion.2, bf16[1024,1024]{0,1:T(8,128)(2,1)S(1)} %convolution_convert_fusion.3), kind=kLoop, calls=%fused_computation | loop fusion | flops 18874368 | bytes 12582912 | tf_op jit(solution)/shard_map/concatenate | solution.py:628
  284.2 8.6 %copy.36 = bf16[1024,3072]{1,0:T(8,128)(2,1)} copy(bf16[1024,3072]{0,1:T(8,128)(2,1)} %pad_maximum_fusion) | data formatting | bytes 12582912 | tf_op jit(solution)/shard_map/concatenate | solution.py:628
  292.8 7.1 %fusion.25 = f32[2048,1024]{1,0:T(8,128)S(1)} fusion(bf16[2048,1024]{1,0:T(8,128)(2,1)} %get-tuple-element.22, bf16[1024,3072]{1,0:T(8,128)(2,1)} %all-gather.6.cloned.1.call-done.w_ref), kind=kOutput, calls=%fused_computation.37 | convolution fusion | flops 4294967296 | bytes 14680064 | tf_op jit(solution)/shard_map/dot_general | solution.py:623
  299.9 6.3 %convolution_add_fusion = f32[2048,1024]{1,0:T(8,128)S(1)} fusion(f32[2048,1024]{1,0:T(8,128)S(1)} %fusion.25, bf16[2048,1024]{1,0:T(8,128)(2,1)S(1)} %copy-done.30, bf16[1024,3072]{1,0:T(8,128)(2,1)} %all-gather.6.cloned.1.call-done.w_ref), kind=kOutput, calls=%fused_computation.31 | convolution fusion | flops 4297064448 | bytes 23068672 | tf_op jit(solution)/shard_map/dot_general | solution.py:623
  306.2 1.6 slice.66
  307.8 1.5 collective-permute-start.1
  309.4 2.5 fusion.11
  311.9 0.6 pad_maximum_fusion.2.vec_in
  312.5 3.7 convolution_convert_fusion
  316.2 4.4 fusion.21.base_out
  320.6 6.0 %slice_add_fusion.base_dn = f32[1024,1024]{1,0:T(8,128)} fusion(f32[2048,1024]{1,0:T(8,128)S(1)} %convolution_add_fusion, bf16[1024,1024]{1,0:T(8,128)(2,1)S(1)} %copy-done.27, bf16[1024,3072]{1,0:T(8,128)(2,1)} %all-gather.6.cloned.1.call-done.w_ref), kind=kOutput, calls=%fused_computation.28 | convolution fusion | flops 2148532224 | bytes 12582912 | tf_op jit(solution)/shard_map/dot_general | solution.py:633
  326.6 231.7 %reduce.1 = (f32[64,3072]{1,0:T(8,128)}, f32[64,1024]{1,0:T(8,128)}, f32[64,4096]{1,0:T(8,128)}, f32[256,1024]{1,0:T(8,128)}, f32[8,1024]{1,0:T(8,128)}, /*index...) custom-call(bf16[8,2,64,3072]{3,2,1,0:T(8,128)(2,1)} %bitcast.56, bf16[8,2,64,1024]{3,2,1,0:T(8,128)(2,1)} %bitcast.66, ...), custom_call_target="tpu_custom_call" | custom-call | flops 99999997952 | bytes 104857600 | tf_op jit(solution)/shard_map/reduce/pallas_call | solution.py:557
  558.4 0.8 slice_bitcast_fusion
  559.1 0.9 fusion.37
  560.0 0.6 fusion.34
  560.6 0.6 fusion.32
  561.2 4.5 fusion.29
  565.7 0.6 dynamic_slice.22
  566.4 0.1 copy-done.7
  566.5 0.6 copy-done.9
  567.1 4.9 fusion.18
  572.0 1.3 copy.50
  573.4 0.3 copy-done.14
  573.6 0.9 copy.51
  574.5 0.7 copy.52
  575.2 1.0 copy.53
  576.2 1.0 copy.54
  (82 shorter events, 0.2 us)
Async XLA Ops:
  7.2 71.3 %copy-start.2 = (bf16[1,1024,1024]{2,1,0:T(8,128)(2,1)S(1)}, bf16[1,1024,1024]{2,1,0:T(8,128)(2,1)}, u32[]{:S(2)}) copy-start(bf16[1,1024,1024]{2,1,0:T(8,128)(2,1)} %param.14) | copy-start | bytes 6291460
  7.2 53.5 %copy-start.26 = (bf16[256]{0:T(256)(128)(2,1)S(1)}, bf16[256]{0:T(256)(128)(2,1)}, u32[]{:S(2)}) copy-start(bf16[256]{0:T(256)(128)(2,1)} %param.21) | copy-start | bytes 1540
  7.2 95.2 %all-gather.8.cloned.1.call-start = ((), (), s32[]{:S(2)}) async-start(), calls=%async_computation.1 | async-start | bytes 2228224 | tf_op jit(solution)/shard_map/all_gather | solution.py:595
  7.9 109.5 %all-gather.6.cloned.1.call-start = ((), (), s32[]{:S(2)}) async-start(), calls=%async_computation | async-start | bytes 6684672 | tf_op jit(solution)/shard_map/all_gather | solution.py:595
  8.7 317.9 %all-gather.10.cloned.1.call-start = ((), (), s32[]{:S(2)}) async-start(), calls=%async_computation.2 | async-start | bytes 8912896 | tf_op jit(solution)/shard_map/all_gather | solution.py:595
  9.4 317.2 %all-gather.12.cloned.1.call-start = ((), (), s32[]{:S(2)}) async-start(), calls=%async_computation.3 | async-start | bytes 8912896 | tf_op jit(solution)/shard_map/all_gather | solution.py:595
  9.5 74.4 %collective-permute-start = (bf16[1024,1024]{1,0:T(8,128)(2,1)}, bf16[1024,1024]{1,0:T(8,128)(2,1)}, u32[]{:S(2)}, u32[]{:S(2)}) collective-permute-start(bf16[1024,1024]{1,0:T(8,128)(2,1)} %bitcast.51), channel_id=1, source_target_pairs={{0,1},{2,3},{4,5},{6,7},{8,9},{10,11},{12,13},{14,15},{16,17},{18,... | collective-permute-start | bytes 6291464 | tf_op jit(solution)/shard_map/ppermute | solution.py:597
  54.0 35.3 %copy-start.18 = (f32[1024]{0:T(1024)}, f32[1024]{0:T(1024)S(1)}, u32[]{:S(2)}) copy-start(f32[1024]{0:T(1024)S(1)} %convert_element_type.54) | copy-start | bytes 12292
  55.6 24.5 %copy-start.22 = (s32[1024]{0:T(1024)}, s32[1024]{0:T(1024)S(1)}, u32[]{:S(2)}) copy-start(s32[1024]{0:T(1024)S(1)} %fusion.31) | copy-start | bytes 12292
  56.7 23.4 %copy-start.23 = (f32[128]{0:T(128)S(1)}, f32[128]{0:T(128)}, u32[]{:S(2)}) copy-start(f32[128]{0:T(128)} %constant.62) | copy-start | bytes 1540
  56.7 23.4 %copy-start.24 = (f32[128]{0:T(128)S(1)}, f32[128]{0:T(128)}, u32[]{:S(2)}) copy-start(f32[128]{0:T(128)} %constant.63) | copy-start | bytes 1540
  79.4 9.9 %copy-start.16 = (f32[1024]{0:T(1024)}, f32[1024]{0:T(1024)S(1)}, u32[]{:S(2)}) copy-start(f32[1024]{0:T(1024)S(1)} %broadcast_multiply_fusion.3) | copy-start | bytes 12292
  79.4 9.9 %copy-start.3 = (bf16[1,1024,1024]{2,1,0:T(8,128)(2,1)S(1)}, bf16[1,1024,1024]{2,1,0:T(8,128)(2,1)}, u32[]{:S(2)}) copy-start(bf16[1,1024,1024]{2,1,0:T(8,128)(2,1)} %param.14) | copy-start | bytes 6291460
  80.1 13.6 %copy-start.20 = (f32[1024]{0:T(1024)}, f32[1024]{0:T(1024)S(1)}, u32[]{:S(2)}) copy-start(f32[1024]{0:T(1024)S(1)} %add_rsqrt_fusion.1) | copy-start | bytes 12292
  83.9 33.6 %copy-start = (f32[2048,128]{1,0:T(8,128)}, f32[2048,128]{1,0:T(8,128)S(1)}, u32[]{:S(2)}) copy-start(f32[2048,128]{1,0:T(8,128)S(1)} %get-tuple-element.42.sin_ref) | copy-start | bytes 3145732
  83.9 33.6 %copy-start.1 = (f32[2048,128]{1,0:T(8,128)}, f32[2048,128]{1,0:T(8,128)S(1)}, u32[]{:S(2)}) copy-start(f32[2048,128]{1,0:T(8,128)S(1)} %get-tuple-element.43.cos_ref) | copy-start | bytes 3145732
  146.9 109.8 %copy-start.6 = (bf16[1024,1024]{1,0:T(8,128)(2,1)S(1)}, bf16[1024,1024]{1,0:T(8,128)(2,1)}, u32[]{:S(2)}) copy-start(bf16[1024,1024]{1,0:T(8,128)(2,1)} %get-tuple-element.45.normed) | copy-start | bytes 6291460
  256.7 4.2 copy-start.10
  256.7 4.2 copy-start.31
  260.9 5.3 copy-start.29
  292.8 7.2 %copy-start.30 = (bf16[2048,1024]{1,0:T(8,128)(2,1)S(1)}, bf16[2048,1024]{1,0:T(8,128)(2,1)}, u32[]{:S(2)}) copy-start(bf16[2048,1024]{1,0:T(8,128)(2,1)} %get-tuple-element.23) | copy-start | bytes 12582916
  307.8 4.7 copy-start.8
  307.8 4.7 copy-start.28
  307.8 253.3 %collective-permute-start.1 = (bf16[1024,1024]{1,0:T(8,128)(2,1)}, bf16[1024,1024]{1,0:T(8,128)(2,1)}, u32[]{:S(2)}, u32[]{:S(2)}) collective-permute-start(bf16[1024,1024]{1,0:T(8,128)(2,1)} %slice.66), channel_id=1, source_target_pairs={{1,0},{3,2},{5,4},{7,6},{9,8},{11,10},{13,12},{15,14},{17,16},{19,... | collective-permute-start | bytes 6291464 | tf_op jit(solution)/shard_map/ppermute | solution.py:626
  312.5 3.7 copy-start.4
  312.5 3.7 copy-start.25
  316.2 4.4 copy-start.27
  326.6 234.6 %copy-start.17 = (f32[1024]{0:T(1024)S(1)}, f32[1024]{0:T(1024)}, u32[]{:S(2)}) copy-start(f32[1024]{0:T(1024)} %copy-done.16) | copy-start | bytes 12292
  326.6 234.6 %copy-start.19 = (f32[1024]{0:T(1024)S(1)}, f32[1024]{0:T(1024)}, u32[]{:S(2)}) copy-start(f32[1024]{0:T(1024)} %copy-done.18) | copy-start | bytes 12292
  326.6 234.6 %copy-start.21 = (f32[1024]{0:T(1024)S(1)}, f32[1024]{0:T(1024)}, u32[]{:S(2)}) copy-start(f32[1024]{0:T(1024)} %copy-done.20) | copy-start | bytes 12292
  561.2 5.2 copy-start.5
  561.2 5.3 copy-start.7
  561.2 5.9 %copy-start.9 = (bf16[1,1024,1024]{2,1,0:T(8,128)(2,1)S(1)}, bf16[1,1024,1024]{2,1,0:T(8,128)(2,1)}, u32[]{:S(2)}) copy-start(bf16[1,1024,1024]{2,1,0:T(8,128)(2,1)} %param.24) | copy-start | bytes 6291460
  567.1 4.9 copy-start.11
  572.0 1.6 copy-start.14
  572.0 2.5 copy-start.15
  572.0 3.2 copy-start.13
  572.0 4.2 copy-start.12
Sparse Core Ops, SparseCore 0:
  10.2 44.1 all-gather.7
  56.7 60.7 all-gather.5
  119.6 73.4 all-gather.9
  195.2 73.2 all-gather.11

commit v3 on v2

--- a/solution.py
+++ b/solution.py
@@ -13,6 +13,7 @@
 ROT = 32
 EPS = 1e-05
 GELU_COEF = 0.7978845608028654
+MESH = pl.DeviceIdType.MESH
 
 NEG = -1e30
 BQ = 256
@@ -191,45 +192,6 @@
     )(lows, starts[:, None], starts[None, :], cosine, sine, mixed, mixed, mixed, d_out)
 
 
-def qkv_kernel(cols, normed_ref, w_ref, cos_ref, sin_ref, out_ref):
-    block = pl.program_id(1)
-    mixed = dot_n(normed_ref[...], w_ref[...])
-
-    @pl.when(block < 2 * cols)
-    def _():
-        scale = jnp.where(block < cols, 0.125, 1.0)
-        cosine = cos_ref[...] * scale
-        sine = sin_ref[...] * scale
-        for i in range(mixed.shape[1] // 128):
-            lanes = slice(i * 128, (i + 1) * 128)
-            out_ref[:, lanes] = rotate(mixed[:, lanes], cosine, sine).astype(jnp.bfloat16)
-
-    @pl.when(block >= 2 * cols)
-    def _():
-        out_ref[...] = mixed.astype(jnp.bfloat16)
-
-
-def project(normed, w_qkv, cosine, sine):
-    rows, width = normed.shape
-    wide, tall = 512, 1024
-    cols = width // wide
-    return pl.pallas_call(
-        functools.partial(qkv_kernel, cols),
-        out_shape=jax.ShapeDtypeStruct((rows, 3 * width), jnp.bfloat16),
-        grid=(rows // tall, 3 * cols),
-        in_specs=[
-            pl.BlockSpec((tall, width), lambda i, j: (i, 0)),
-            pl.BlockSpec((width, wide), lambda i, j: (0, j)),
-            pl.BlockSpec((tall, 128), lambda i, j: (i, 0)),
-            pl.BlockSpec((tall, 128), lambda i, j: (i, 0)),
-        ],
-        out_specs=pl.BlockSpec((tall, wide), lambda i, j: (i, j)),
-        compiler_params=pltpu.CompilerParams(vmem_limit_bytes=48 * 2**20),
-        cost_estimate=pl.CostEstimate(flops=12 * 10**9, bytes_accessed=24 * 2**20, transcendentals=0),
-        name="project",
-    )(normed, w_qkv, cosine, sine)
-
-
 def rope_tables(position):
     lane = np.arange(128) % HEAD
     freqs = np.where(lane < ROT, 10000.0 ** (-2.0 * (lane // 2) / ROT), 0.0).astype(np.float32)
@@ -246,12 +208,245 @@
     return centered * scale, scale
 
 
-MESH = pl.DeviceIdType.MESH
+CHUNK = 256
+
+
+def gather_kernel(dims, w_out, w_qkv, x_hbm, grad, vec_own, cos_ref, sin_ref,
+                  wout_all, wqkv_all, normed_all, mixed_all, d_attended, prior_all, vec_all,
+                  wbuf, own, prior, normed, mixed, d_att, vec, vec_recv, in_sem, load_sem, out_sem, zsend, zrecv, ysend, yrecv,
+                  csend, crecv, psend, precv, vsend, vrecv):
+    rows, seqs, tokens, width = dims
+    bf, f32 = jnp.bfloat16, jnp.float32
+    levels = rows // 4
+    r, s = lax.axis_index("rows"), lax.axis_index("seq")
+    core, y, z = lax.rem(r, 2), lax.rem(r // 2, 2), r // 4
+    core_id = {"rows": r + 1 - 2 * core}
+    y_id = {"rows": r + 2 - 4 * y}
+    z_of = lambda d: lax.rem(z + d, levels)
+    z_id = lambda d: {"rows": z_of(d) * 4 + lax.rem(r, 4)}
+    has_next, has_prior = s < seqs - 1, s > 0
+    n_out, n_qkv = width // CHUNK, 3 * width // CHUNK
+    total = n_out + n_qkv
+    quarter = tokens // 4
+
+    def load(k):
+        source = w_out if k < n_out else w_qkv
+        col = (k if k < n_out else k - n_out) * CHUNK
+        return pltpu.make_async_copy(source.at[:, col:col + CHUNK], wbuf.at[k, z, y, core], load_sem.at[k])
+
+    fetch = pltpu.make_async_copy(x_hbm, own, in_sem)
+    fetch.start()
+    for k in range(total):
+        load(k).start()
+
+    barrier = pltpu.get_barrier_semaphore()
+    partners = [core_id, y_id] + [z_id(d) for d in range(1, levels)]
+    for partner in partners:
+        pl.semaphore_signal(barrier, inc=1, device_id=partner, device_id_type=MESH)
+
+    @pl.when(has_next)
+    def _():
+        pl.semaphore_signal(barrier, inc=1, device_id={"seq": s + 1}, device_id_type=MESH)
+
+    @pl.when(has_prior)
+    def _():
+        pl.semaphore_signal(barrier, inc=1, device_id={"seq": s - 1}, device_id_type=MESH)
+    pl.semaphore_wait(barrier, len(partners) + jnp.where(has_next, 1, 0) + jnp.where(has_prior, 1, 0))
+
+    def prior_copy(i):
+        block = pl.ds(i * quarter, quarter)
+        return pltpu.make_async_remote_copy(x_hbm.at[block], prior.at[block], psend.at[i], precv.at[i],
+                                            device_id={"seq": jnp.minimum(s + 1, seqs - 1)}, device_id_type=MESH)
+
+    def vec_copy(i, target):
+        return pltpu.make_async_remote_copy(vec.at[i], vec_recv.at[i], vsend.at[i], vrecv.at[i],
+                                            device_id=target, device_id_type=MESH)
+
+    def z_vec(d):
+        return pltpu.make_async_remote_copy(vec.at[0], vec_recv.at[1 + d], vsend.at[1 + d], vrecv.at[1 + d],
+                                            device_id=z_id(d), device_id_type=MESH)
+
+    def z_copy(k, d):
+        mine = wbuf.at[k, z, y, core]
+        return pltpu.make_async_remote_copy(mine, mine, zsend.at[k, d - 1], zrecv.at[k, d - 1],
+                                            device_id=z_id(d), device_id_type=MESH)
+
+    def z_landed(k, d):
+        theirs = wbuf.at[k, z_of(levels - d), y, core]
+        return pltpu.make_async_remote_copy(theirs, theirs, zsend.at[k, d - 1], zrecv.at[k, d - 1],
+                                            device_id=z_id(d), device_id_type=MESH)
+
+    def y_copy(k, side):
+        part = wbuf.at[k, :, side, core]
+        return pltpu.make_async_remote_copy(part, part, ysend.at[k], yrecv.at[k], device_id=y_id, device_id_type=MESH)
+
+    def core_copy(k, side):
+        part = wbuf.at[k, :, :, side]
+        return pltpu.make_async_remote_copy(part, part, csend.at[k], crecv.at[k], device_id=core_id, device_id_type=MESH)
+
+    vec[0] = vec_own[...]
+    for d in range(1, levels):
+        z_vec(d).start()
+
+    @pl.when(has_next)
+    def _():
+        for i in range(4):
+            prior_copy(i).start()
+    for k in range(total):
+        load(k).wait()
+        for d in range(1, levels):
+            z_copy(k, d).start()
+
+    for d in range(1, levels):
+        z_vec(d).wait()
+    value = vec[0]
+    for d in range(1, levels):
+        value = value + vec_recv[1 + d]
+    vec[1] = value
+    vec_copy(1, y_id).start()
+    fetch.wait()
+    vec_copy(1, y_id).wait()
+    vec[2] = value + vec_recv[1]
+    swap = pltpu.make_async_remote_copy(vec.at[2], vec_recv.at[0], vsend.at[0], vrecv.at[0], device_id=core_id,
+                                        device_id_type=MESH)
+    swap.start()
+    swap.wait()
+    vec_all[...] = vec[2] + vec_recv[0]
+    gain, bias = vec_all[0:1, :], vec_all[1:2, :]
+
+    def normalize(source, half):
+        def body(i, _):
+            block = pl.ds(pl.multiple_of(i * quarter, quarter), quarter)
+            values = source[block, :].astype(f32)
+            centered = values - jnp.mean(values, axis=1, keepdims=True)
+            unit = centered * lax.rsqrt(jnp.mean(centered * centered, axis=1, keepdims=True) + EPS)
+            normed[half, block, :] = (unit * gain + bias).astype(bf)
+            return 0
+        return body
+    lax.fori_loop(0, 4, normalize(own, 1), 0)
+
+    outs = []
+
+    def send_out(src, dst):
+        copy = pltpu.make_async_copy(src, dst, out_sem.at[len(outs)])
+        copy.start()
+        outs.append(copy)
+    send_out(normed.at[1], normed_all.at[1])
+
+    def multiply(half, j):
+        cols = slice(j * CHUNK, (j + 1) * CHUNK)
+        tall = tokens // 2
+
+        def body(i, _):
+            block = pl.ds(pl.multiple_of(i * tall, tall), tall)
+            product = dot_n(normed[half, block, :], wbuf[n_out + j].reshape(width, CHUNK))
+            if j * CHUNK < 2 * width:
+                scale = 0.125 if j * CHUNK < width else 1.0
+                place = pl.ds(pl.multiple_of(half * tokens + i * tall, tall), tall)
+                cosine, sine = cos_ref[place, :] * scale, sin_ref[place, :] * scale
+                for a in range(CHUNK // 128):
+                    mixed[half, block, j * CHUNK + a * 128:j * CHUNK + (a + 1) * 128] = rotate(
+                        product[:, a * 128:(a + 1) * 128], cosine, sine).astype(bf)
+            else:
+                mixed[half, block, cols] = product.astype(bf)
+            return 0
+        lax.fori_loop(0, 2, body, 0)
+        send_out(mixed.at[half, :, cols], mixed_all.at[half, :, cols])
+
+    def project_back():
+        tall = tokens // 4
+
+        def body(i, _):
+            block = pl.ds(pl.multiple_of(i * tall, tall), tall)
+            value = dot_t(grad[block, 0:CHUNK], wbuf[0].reshape(width, CHUNK))
+            for k in range(1, n_out):
+                value = value + dot_t(grad[block, k * CHUNK:(k + 1) * CHUNK], wbuf[k].reshape(width, CHUNK))
+            d_att[block, :] = value.astype(bf)
+            return 0
+        lax.fori_loop(0, 4, body, 0)
+        send_out(d_att, d_attended)
+
+    for it in range(total + 2):
+        if it < total:
+            for d in range(1, levels):
+                z_landed(it, d).wait_recv()
+            y_copy(it, y).start()
+        if 0 <= it - 1 < total:
+            y_copy(it - 1, 1 - y).wait_recv()
+            core_copy(it - 1, core).start()
+        if 0 <= it - 2 < total:
+            k = it - 2
+            core_copy(k, 1 - core).wait_recv()
+            if k < n_out:
+                send_out(wbuf.at[k], wout_all.at[:, :, :, :, k * CHUNK:(k + 1) * CHUNK])
+                if k == n_out - 1:
+                    project_back()
+            else:
+                send_out(wbuf.at[k], wqkv_all.at[:, :, :, :, (k - n_out) * CHUNK:(k - n_out + 1) * CHUNK])
+                multiply(1, k - n_out)
+
+    @pl.when(has_prior)
+    def _():
+        for i in range(4):
+            prior_copy(i).wait_recv()
+
+    @pl.when(jnp.logical_not(has_prior))
+    def _():
+        prior[...] = jnp.zeros_like(prior)
+    send_out(prior, prior_all)
+    lax.fori_loop(0, 4, normalize(prior, 0), 0)
+    send_out(normed.at[0], normed_all.at[0])
+    for j in range(n_qkv // 3, n_qkv):
+        multiply(0, j)
+
+    @pl.when(has_next)
+    def _():
+        for i in range(4):
+            prior_copy(i).wait_send()
+    for k in range(total):
+        for d in range(1, levels):
+            z_copy(k, d).wait_send()
+        y_copy(k, y).wait_send()
+        core_copy(k, core).wait_send()
+    for copy in outs:
+        copy.wait()
+
+
+def gather_all(rows, seqs, w_out, w_qkv, x, grad, vec_own, cosine, sine):
+    tokens, width = x.shape
+    share, levels = width // rows, rows // 4
+    bf, f32 = jnp.bfloat16, jnp.float32
+    vmem, hbm = pl.BlockSpec(memory_space=pltpu.VMEM), pl.BlockSpec(memory_space=pl.ANY)
+    dma = pltpu.SemaphoreType.DMA
+    total = 4 * width // CHUNK
+    shape = jax.ShapeDtypeStruct
+    wout_all, wqkv_all, normed, mixed, d_att, prior, vec = pl.pallas_call(
+        functools.partial(gather_kernel, (rows, seqs, tokens, width)),
+        out_shape=[shape((levels, 2, 2, share, width), bf), shape((levels, 2, 2, share, 3 * width), bf), shape((2, tokens, width), bf),
+                   shape((2, tokens, 3 * width), bf), shape((tokens, width), bf), shape((tokens, width), bf), shape((8, width), f32)],
+        in_specs=[hbm, hbm, hbm, vmem, vmem, vmem, vmem],
+        out_specs=[hbm] * 6 + [vmem],
+        scratch_shapes=[
+            pltpu.VMEM((total, levels, 2, 2, share, CHUNK), bf),
+            pltpu.VMEM((tokens, width), bf), pltpu.VMEM((tokens, width), bf), pltpu.VMEM((2, tokens, width), bf),
+            pltpu.VMEM((2, tokens, 3 * width), bf), pltpu.VMEM((tokens, width), bf),
+            pltpu.VMEM((3, 8, width), f32), pltpu.VMEM((1 + levels, 8, width), f32),
+            dma, dma((total,)), dma((2 * total + 8,)), dma((total, levels - 1)), dma((total, levels - 1)),
+            dma((total,)), dma((total,)), dma((total,)), dma((total,)), dma((4,)), dma((4,)), dma((1 + levels,)), dma((1 + levels,)),
+        ],
+        compiler_params=pltpu.CompilerParams(collective_id=0, has_side_effects=True, vmem_limit_bytes=60 * 2**20),
+        cost_estimate=pl.CostEstimate(flops=20 * 10**9, bytes_accessed=40 * 2**20, transcendentals=0),
+        name="gather",
+    )(w_out, w_qkv, x, grad, vec_own, cosine, sine)
+    return (wout_all.reshape(width, width), wqkv_all.reshape(width, 3 * width), normed.reshape(2 * tokens, width),
+            mixed.reshape(2 * tokens, 3 * width), d_att, prior, vec)
+
+
 RING = 12
-SLOTS = 4
-
-
-def reduce_kernel(dims, g_qkv, g_out, normed, normed_t, grad, grad_t, x_ref, w_in, w_back, b_in, base_out, base_dn,
+SLOTS = 6
+
+
+def reduce_kernel(dims, g_q, g_k, g_v, g_out, normed, normed_t, grad, grad_t, x_ref, w_in, w_back, b_in, base_out, base_dn,
                   vec_in, o_qkv, o_out, o_in, o_back, o_vec, block_out, d_normed,
                   buf, core_recv, chip, x_recv, y_recv, part, z_recv, fin, fin_recv, res, acc_out, hidden, d_pre, win_buf, wback_buf,
                   vec, vec_recv, load_sem, acc_sem, w_sem, send_sem, recv_sem, zsend_sem, zrecv_sem, vsend_sem, vrecv_sem):
@@ -317,15 +512,11 @@
                                       buf.at[slot, :, :, pl.ds(j * piece, piece)], load_sem.at[j]) for j in range(4)]
 
     def load(k):
-        @pl.when(k < n_qkv)
-        def _():
-            for copy in load_copies(g_qkv, k * 512, k):
-                copy.start()
-
-        @pl.when((k >= n_qkv) & (k < n_first))
-        def _():
-            for copy in load_copies(g_out, (k - n_qkv) * 512, k):
-                copy.start()
+        for i, source in enumerate((g_q, g_k, g_v, g_out)):
+            @pl.when((k >= i * n_out) & (k < (i + 1) * n_out))
+            def _():
+                for copy in load_copies(source, (k - i * n_out) * 512, k):
+                    copy.start()
 
     def weights(j):
         t = lax.rem(j, 2)
@@ -453,7 +644,7 @@
     def send_first(k, t):
         @pl.when(k < n_first)
         def _():
-            for copy in load_copies(g_qkv, 0, k):
+            for copy in load_copies(g_q, 0, k):
                 copy.wait()
         load(k + 1)
         core_copy(k).start()
@@ -509,7 +700,7 @@
 
     def step(it, _):
         for lag, body in enumerate(pipeline):
-            stage(lag, it, body)
+            stage(2 * lag, it, body)
 
         @pl.when(it < n_in)
         def _():
@@ -539,10 +730,10 @@
         def _():
             back_grads(it - n_in)
         return 0
-    lax.fori_loop(0, total + len(pipeline) - 1, step, 0)
-
-
-def reduce_all(rows, seqs, g_qkv, g_out, normed, normed_t, grad, grad_t, x, w_in, w_back, b_in, base_out, base_dn, vec_in):
+    lax.fori_loop(0, total + 2 * len(pipeline) - 2, step, 0)
+
+
+def reduce_all(rows, seqs, g_q, g_k, g_v, g_out, normed, normed_t, grad, grad_t, x, w_in, w_back, b_in, base_out, base_dn, vec_in):
     tokens, width = normed.shape
     ff = w_in.shape[1]
     share = width // rows
@@ -560,7 +751,7 @@
                    jax.ShapeDtypeStruct((share, ff), f32), jax.ShapeDtypeStruct((ff // rows, width), f32),
                    jax.ShapeDtypeStruct((8, width), f32), jax.ShapeDtypeStruct((tokens, width), bf),
                    jax.ShapeDtypeStruct((tokens, width), f32)],
-        in_specs=[hbm, hbm, vmem, vmem, vmem, vmem, vmem, hbm, hbm, vmem, hbm, hbm, vmem],
+        in_specs=[hbm, hbm, hbm, hbm, vmem, vmem, vmem, vmem, vmem, hbm, hbm, vmem, hbm, hbm, vmem],
         out_specs=[vmem] * 7,
         scratch_shapes=[
             pltpu.VMEM((RING, rows // 2, 2, q_rows, 128), bf),
@@ -586,18 +777,13 @@
         compiler_params=pltpu.CompilerParams(collective_id=1, has_side_effects=True, vmem_limit_bytes=62 * 2**20),
         cost_estimate=pl.CostEstimate(flops=100 * 10**9, bytes_accessed=100 * 2**20, transcendentals=0),
         name="reduce",
-    )(g_qkv.reshape(rows // 2, 2, share, 3 * width), g_out.reshape(rows // 2, 2, share, width), normed, normed_t, grad, grad_t, x,
+    )(*[g.reshape(rows // 2, 2, share, width) for g in (g_q, g_k, g_v, g_out)], normed, normed_t, grad, grad_t, x,
       w_in, w_back, b_in, base_out, base_dn, vec_in)
 
 
 def body(block_input, lengths, norm_gain, norm_bias, w_qkv, w_attn_out, w_fc_in, b_fc_in, w_fc_out, b_fc_out, cotangent):
     f32, bf = jnp.float32, jnp.bfloat16
-    gather = lambda w: lax.all_gather(w, "rows", axis=0, tiled=True)
     rows, seqs = lax.axis_size("rows"), lax.axis_size("seq")
-    prior_input = lax.ppermute(block_input[0], "seq", [(i, i + 1) for i in range(seqs - 1)])
-    gain, bias = gather(norm_gain).astype(f32), gather(norm_bias).astype(f32)
-    w_qkv_all, w_out_all = gather(w_qkv), gather(w_attn_out)
-    w_in_all, b_in_all, w_back_all, b_back_all = gather(w_fc_in), gather(b_fc_in), gather(w_fc_out), gather(b_fc_out)
     inputs = block_input[0].astype(f32)
     tokens, width = inputs.shape
     own_lengths = lengths[0]
@@ -611,13 +797,23 @@
     starts = (begin - first + tokens)[tokens:]
     lows = starts[::BQ] // BQ
 
+    share, wide = width // rows, 4 * width // rows
+    r = lax.axis_index("rows")
+    place = lambda vector, lines: jnp.where(np.arange(lines * width).reshape(rows, -1) // (lines * share) == r,
+                                            vector.astype(f32)[None, :], 0.0).reshape(lines, width)
+    vec_own = jnp.concatenate([place(norm_gain, 1), place(norm_bias, 1), place(b_fc_out, 1), place(b_fc_in, 4),
+                               jnp.zeros((1, width), f32)])
+    grad_out = cotangent[0]
+    w_out_all, w_qkv_all, normed_both, mixed, d_attended, prior_input, vectors = gather_all(
+        rows, seqs, w_attn_out, w_qkv, block_input[0], grad_out, vec_own, cosine, sine)
+    w_fc_in, w_fc_out, vectors = lax.optimization_barrier((w_fc_in, w_fc_out, vectors))
+    w_in_all = lax.all_gather(w_fc_in, "rows", axis=0, tiled=True)
+    w_back_all = lax.all_gather(w_fc_out, "rows", axis=0, tiled=True)
+    gain, bias, b_back_all = vectors[0], vectors[1], vectors[2]
+    b_in_all = vectors[3:7].reshape(1, 4 * width)
+    normed = normed_both[tokens:]
     unit, scale = layer_norm_stats(inputs)
-    normed = (unit * gain + bias).astype(bf)
     prior_unit, _ = layer_norm_stats(prior_input.astype(f32))
-    normed_both = jnp.concatenate([(prior_unit * gain + bias).astype(bf), normed], axis=0)
-    mixed = project(normed_both, w_qkv_all, cosine, sine)
-    grad_out = cotangent[0]
-    d_attended = jnp.dot(grad_out, w_out_all.T, preferred_element_type=f32).astype(bf)
     attended, d_q, d_k, d_v = attention(lows, starts, cosine, sine, mixed, d_attended)
 
     d_normed_both = jnp.dot(d_k, w_qkv_all[:, width:2 * width].T, preferred_element_type=f32) + jnp.dot(
@@ -625,25 +821,22 @@
     d_prior = d_normed_both[:tokens]
     back = lax.ppermute(d_prior.astype(bf), "seq", [(i + 1, i) for i in range(seqs - 1)])
     vec_in = jnp.stack([jnp.sum(d_prior * prior_unit, axis=0), jnp.sum(d_prior, axis=0)])
-    grad_w_qkv = jnp.concatenate([
-        jnp.dot(normed.T, d_q, preferred_element_type=f32).astype(bf),
-        jnp.dot(normed_both.T, d_k, preferred_element_type=f32).astype(bf),
-        jnp.dot(normed_both.T, d_v, preferred_element_type=f32).astype(bf)], axis=1)
+    grads = [jnp.dot(normed.T, d_q, preferred_element_type=f32).astype(bf),
+             jnp.dot(normed_both.T, d_k, preferred_element_type=f32).astype(bf),
+             jnp.dot(normed_both.T, d_v, preferred_element_type=f32).astype(bf)]
     grad_w_out = jnp.dot(attended.T, grad_out, preferred_element_type=f32).astype(bf)
     base_dn = d_normed_both[tokens:] + jnp.dot(d_q, w_qkv_all[:, :width].T, preferred_element_type=f32)
-    base_out = inputs + jnp.dot(attended, w_out_all, preferred_element_type=f32) + b_back_all.astype(f32)
+    base_out = inputs + jnp.dot(attended, w_out_all, preferred_element_type=f32) + b_back_all
 
     g_qkv, g_out, g_in, g_back, vec, block_output, d_normed = reduce_all(
-        rows, seqs, grad_w_qkv, grad_w_out, normed, normed.T, grad_out, grad_out.T, block_input[0], w_in_all, w_back_all,
-        b_in_all.astype(f32)[None], base_out, base_dn, vec_in)
+        rows, seqs, *grads, grad_w_out, normed, normed.T, grad_out, grad_out.T, block_input[0], w_in_all, w_back_all,
+        b_in_all, base_out, base_dn, vec_in)
 
     d_normed = d_normed + back.astype(f32)
     d_unit = d_normed * gain
     d_input = (d_unit - jnp.mean(d_unit, axis=1, keepdims=True)
                - unit * jnp.mean(d_unit * unit, axis=1, keepdims=True)) * scale
     grad_input = d_input + grad_out.astype(f32)
-    share, wide = width // rows, 4 * width // rows
-    r = lax.axis_index("rows")
     own = lambda vector, size: lax.dynamic_slice_in_dim(vector, r * size, size)
     return (block_output[None], grad_input[None], own(vec[0], share), own(vec[1], share), g_qkv, g_out, g_in,
             own(vec[3:7].reshape(4 * width), wide), g_back, own(vec[2], share))

time: 593 us -> 562 us (0.948)
  Pallas kernels: 371 us -> 433 us
  blocking collectives: 51 us -> 0 us
  other arithmetic: 47.6 us -> 27.4 us
  waiting for transfers between devices: 11.3 us -> 0.72 us
  starting transfers between devices: 7.87 us -> 1.76 us
    pallas_call x1, Pallas kernels: 29.4 us -> 87.8 us  [gather_all(): pl.pallas_call(functools.partial(gather_kernel, (rows, seqs, tokens, widt...]
    unnamed x1 -> x0, blocking collectives: 33.8 us -> none
    pallas_call x1, Pallas kernels: 110 us -> 131 us  [attention(): pl.pallas_call(functools.partial(attention_kernel, pairs, tokens), out_sh...]
    concatenate x2 -> x0, other arithmetic: 17.8 us -> none  [the longest x1 13.1 us: body(): jnp.concatenate([jnp.dot(normed.T, d_q, preferred_element_type=f32).astyp...]
    pallas_call x1, Pallas kernels: 232 us -> 214 us  [reduce_all(): pl.pallas_call(functools.partial(reduce_kernel, (rows, seqs, q_rows, edge...]
    all_gather x1 -> x0, blocking collectives: 17.2 us -> none  [body(): gather = lambda w: lax.all_gather(w, 'rows', axis=0, tiled=True)]
    all_gather x4 -> x2, waiting for transfers between devices: 9.22 us -> 0.01 us  [the longest x1 0.01 us: body(): w_in_all = lax.all_gather(w_fc_in, 'rows', axis=0, tiled=True)]
    concatenate x1, local copies, waits for them, and re-layouts: 8.63 us -> 0.65 us  [body(): jnp.concatenate([place(norm_gain, 1), place(norm_bias, 1), place(b_fc_out...]
  transfers between devices with their start and end apart: 6 -> 3, of which waited for: 1 -> 0; matrix products, arithmetic and copies ran while one was open for 19% -> 13% of each run, Pallas kernels for 64% -> 62%
where the time goes in v3:
time: 562 us; the launch traced here: 556 us
  Pallas kernels  433 us (77%)
  matrix products  43.1 us (8%)
  local copies, waits for them, and re-layouts  35.5 us (6%)
  other arithmetic  27.4 us (5%)
  between operations  14.5 us (3%)
    pallas_call x1, Pallas kernels, reduce_all(): pl.pallas_call(functools.partial(reduce_kernel, (rows, seqs, q_rows, edge...  214 us
    pallas_call x1, Pallas kernels, attention(): pl.pallas_call(functools.partial(attention_kernel, pairs, tokens), out_sh...  131 us
    pallas_call x1, Pallas kernels, gather_all(): pl.pallas_call(functools.partial(gather_kernel, (rows, seqs, tokens, widt...  87.8 us
  transfers between devices with their start and end apart: 3, of which 0 were waited for; matrix products, arithmetic and copies ran while one was open for 13% of the time, Pallas kernels for 62%

profile of v3, /device:TPU:0, one launch (start us, length us, event | category | flops | bytes accessed | tf_op | source)
XLA Modules:
  0.0 555.5 jit_solution(6827410922026905407)
XLA Ops:
  7.2 0.0 all-gather.3.cloned.1.call-start
  7.2 0.7 convert_element_type.46
  7.9 0.7 convert_element_type.47
  8.5 0.7 convert_element_type.48
  9.2 0.7 compare_select_fusion.1
  9.9 0.1 reshape.113
  10.0 0.1 reshape.114
  10.1 0.1 reshape.115
  10.1 0.7 convert_element_type.49
  10.8 0.7 compare_select_fusion
  11.5 0.8 select_reduce_fusion.1
  12.3 0.7 select_reduce_fusion
  13.1 6.2 %fusion.24 = (f32[2048,128]{1,0:T(8,128)}, f32[2048,128]{1,0:T(8,128)}) fusion(f32[128]{0:T(128)} %constant.70, f32[128]{0:T(128)} %constant.69, f32[2048]{0:T(1024)S(1)} %subtract_convert_fusion), kind=kLoop, calls=%fused_computation.40 | loop fusion | flops 524288 | bytes 2106368 | tf_op jit(solution)/shard_map/mul | solution.py:200
  19.3 0.6 concatenate.3.vec_own
  20.0 87.8 %gather.1 = (bf16[4,2,2,64,1024]{4,3,2,1,0:T(8,128)(2,1)}, bf16[4,2,2,64,3072]{4,3,2,1,0:T(8,128)(2,1)}, bf16[2,1024,1024]{2,1,0:T(8,128)(2,1)}, bf16[2,1024,307...) custom-call(bf16[64,1024]{1,0:T(8,128)(2,1)} %w_out.1, ...), custom_call_target="tpu_custom_call" | custom-call | flops 20000000000 | bytes 41943040 | tf_op jit(solution)/shard_map/gather/pallas_call | solution.py:423
  107.8 0.0 all-gather.3.cloned.1.call-update
  107.8 0.0 all-gather.5.cloned.1.call-start
  107.8 0.7 all-gather.5.cloned.1.call-update
  108.6 0.0 copy-start.15
  108.6 0.1 slice.51
  108.7 1.0 copy.36.start_col
  109.7 0.5 and_select_fusion.lows
  110.2 130.8 %attention.1 = (bf16[1024,1024]{1,0:T(8,128)(2,1)}, bf16[1024,1024]{1,0:T(8,128)(2,1)}, bf16[2048,1024]{1,0:T(8,128)(2,1)}, bf16[2048,1024]{1,0:T(8,128)(2,1)}) custom-call(s32[4]{0:T(128)} %and_select_fusion.lows, s32[1024,1]{1,0:T(8,128)} %copy.36.start_col, s32[1,1024]{1,0:T(1,128)} %bitcast.76, f32[2048,128]{1,0:T(8,128)} %get-tuple-element.64.cos_ref, ...), custom_call_target="tpu_custom_call" | custom-call | flops 60000002048 | bytes 31457280 | tf_op jit(solution)/shard_map/attention/pallas_call | solution.py:175
  241.0 7.1 %fusion.19 = f32[2048,1024]{1,0:T(8,128)S(1)} fusion(bf16[2048,1024]{1,0:T(8,128)(2,1)} %get-tuple-element.35, bf16[1024,3072]{1,0:T(8,128)(2,1)} %bitcast.86), kind=kOutput, calls=%fused_computation.29 | convolution fusion | flops 4294967296 | bytes 14680064 | tf_op jit(solution)/shard_map/dot_general | solution.py:819
  248.2 6.3 %convolution_add_fusion = f32[2048,1024]{1,0:T(8,128)S(1)} fusion(f32[2048,1024]{1,0:T(8,128)S(1)} %fusion.19, bf16[2048,1024]{1,0:T(8,128)(2,1)S(1)} %copy-done.19, bf16[1024,3072]{1,0:T(8,128)(2,1)} %bitcast.87), kind=kOutput, calls=%fused_computation.23 | convolution fusion | flops 4297064448 | bytes 23068672 | tf_op jit(solution)/shard_map/dot_general | solution.py:819
  254.5 3.2 copy-done.7
  257.7 1.7 slice.91
  259.4 1.7 collective-permute-start
  261.1 6.3 %copy.35 = bf16[2,1024,1024]{1,2,0:T(8,128)(2,1)} copy(bf16[2,1024,1024]{2,1,0:T(8,128)(2,1)} %get-tuple-element.31) | data formatting | bytes 8388608 | tf_op jit(solution)/shard_map/gather/pallas_call | solution.py:423
  267.4 4.2 slice_bitcast_fusion
  271.6 4.1 copy.37.normed
  275.7 0.6 copy.39
  276.3 3.9 copy.38.grad_t
  280.2 0.3 convert_reduce_fusion.1
  280.6 0.0 copy-start
  280.6 0.7 fusion.12
  281.3 2.9 fusion.14
  284.2 0.6 pad_maximum_fusion.vec_in
  284.8 0.3 convert_reduce_fusion
  285.2 0.7 fusion.11
  285.9 0.0 copy-start.5
  285.9 0.0 copy-start.21
  286.0 3.7 convolution_convert_fusion.3
  289.7 3.8 convolution_convert_fusion
  293.5 4.3 fusion.15.base_out
  297.8 6.1 %slice_add_fusion.base_dn = f32[1024,1024]{1,0:T(8,128)} fusion(f32[2048,1024]{1,0:T(8,128)S(1)} %bitcast.68, bf16[1024,1024]{1,0:T(8,128)(2,1)S(1)} %copy-done.17, bf16[1024,3072]{1,0:T(8,128)(2,1)} %bitcast.88), kind=kOutput, calls=%fused_computation.21 | convolution fusion | flops 2148532224 | bytes 12582912 | tf_op jit(solution)/shard_map/dot_general | solution.py:828
  304.0 6.0 %convolution_convert_fusion.1 = bf16[1024,1024]{1,0:T(8,128)(2,1)} fusion(bf16[2048,1024]{1,0:T(8,128)(2,1)S(1)} %bitcast.69, bf16[2048,1024]{1,0:T(8,128)(2,1)S(1)} %copy-done.20), kind=kOutput, calls=%fused_computation.32 | convolution fusion | flops 4296015872 | bytes 10485760 | tf_op jit(solution)/shard_map/dot_general | solution.py:826
  310.0 5.8 %convolution_convert_fusion.2 = bf16[1024,1024]{1,0:T(8,128)(2,1)} fusion(bf16[2048,1024]{1,0:T(8,128)(2,1)S(1)} %bitcast.70, bf16[2048,1024]{1,0:T(8,128)(2,1)S(1)} %copy-done.18), kind=kOutput, calls=%fused_computation.33 | convolution fusion | flops 4296015872 | bytes 10485760 | tf_op jit(solution)/shard_map/dot_general | solution.py:825
  315.7 214.0 %reduce.1 = (f32[64,3072]{1,0:T(8,128)}, f32[64,1024]{1,0:T(8,128)}, f32[64,4096]{1,0:T(8,128)}, f32[256,1024]{1,0:T(8,128)}, f32[8,1024]{1,0:T(8,128)}, /*index...) custom-call(bf16[8,2,64,1024]{3,2,1,0:T(8,128)(2,1)} %bitcast.90, bf16[8,2,64,1024]{3,2,1,0:T(8,128)(2,1)} %bitcast.93, ...), custom_call_target="tpu_custom_call" | custom-call | flops 99999997952 | bytes 104857600 | tf_op jit(solution)/shard_map/reduce/pallas_call | solution.py:748
  529.7 0.8 slice_bitcast_fusion.2
  530.5 0.9 fusion.30
  531.4 0.6 fusion.28
  531.9 0.6 fusion.26
  532.5 4.5 fusion.23
  537.1 0.6 dynamic_slice.22
  537.7 0.1 copy-done.3
  537.8 0.6 copy-done.6
  538.4 4.9 fusion.10
  543.4 1.3 copy.48
  544.7 0.3 copy-done.12
  545.0 0.9 copy.49
  545.9 0.7 copy.50
  546.6 1.0 copy.51
  547.5 1.0 copy.52
  (57 shorter events, 0.2 us)
Async XLA Ops:
  7.2 308.6 %all-gather.3.cloned.1.call-start = ((), (), s32[]{:S(2)}) async-start(), calls=%async_computation | async-start | bytes 8912896 | tf_op jit(solution)/shard_map/all_gather | solution.py:810
  107.8 207.9 %all-gather.5.cloned.1.call-start = ((), (), s32[]{:S(2)}) async-start(), calls=%async_computation.1 | async-start | bytes 8912896 | tf_op jit(solution)/shard_map/all_gather | solution.py:811
  108.6 1.6 copy-start.15
  241.0 7.2 %copy-start.19 = (bf16[2048,1024]{1,0:T(8,128)(2,1)S(1)}, bf16[2048,1024]{1,0:T(8,128)(2,1)}, u32[]{:S(2)}) copy-start(bf16[2048,1024]{1,0:T(8,128)(2,1)} %get-tuple-element.36) | copy-start | bytes 12582916
  254.5 3.2 copy-start.7
  259.4 273.2 %collective-permute-start = (bf16[1024,1024]{1,0:T(8,128)(2,1)}, bf16[1024,1024]{1,0:T(8,128)(2,1)}, u32[]{:S(2)}, u32[]{:S(2)}) collective-permute-start(bf16[1024,1024]{1,0:T(8,128)(2,1)} %slice.91), channel_id=1, source_target_pairs={{1,0},{3,2},{5,4},{7,6},{9,8},{11,10},{13,12},{15,14},{17,16},{19,... | collective-permute-start | bytes 6291464 | tf_op jit(solution)/shard_map/ppermute | solution.py:822
  267.4 8.3 %copy-start.14 = (f32[8,1024]{1,0:T(8,128)S(1)}, f32[8,1024]{1,0:T(8,128)}, u32[]{:S(2)}) copy-start(f32[8,1024]{1,0:T(8,128)} %get-tuple-element.41) | copy-start | bytes 98308
  271.6 8.7 %copy-start.2 = (bf16[1024,1024]{1,0:T(8,128)(2,1)S(1)}, bf16[1024,1024]{1,0:T(8,128)(2,1)}, u32[]{:S(2)}) copy-start(bf16[1024,1024]{1,0:T(8,128)(2,1)} %get-tuple-element.44) | copy-start | bytes 6291460
  280.6 4.3 copy-start
  281.3 4.6 copy-start.4
  281.3 4.6 copy-start.17
  285.9 3.7 copy-start.5
  285.9 3.7 copy-start.21
  289.6 3.8 copy-start.16
  289.7 8.2 %slice-start = ((s8[8388608]{0:T(1024)(128)(4,1)}), s8[4194304]{0:T(1024)(128)(4,1)S(1)}, s32[]{:S(2)}) async-start(s8[8388608]{0:T(1024)(128)(4,1)} %bitcast.67), calls=%async_computation.2 | async-start | bytes 8388608
  293.5 4.3 slice-start.1
  297.8 6.1 %copy-start.8 = (bf16[2,1024,1024]{2,1,0:T(8,128)(2,1)S(1)}, bf16[2,1024,1024]{2,1,0:T(8,128)(2,1)}, u32[]{:S(2)}) copy-start(bf16[2,1024,1024]{2,1,0:T(8,128)(2,1)} %get-tuple-element.31) | copy-start | bytes 12582916
  297.8 6.1 %copy-start.20 = (bf16[2048,1024]{1,0:T(8,128)(2,1)S(1)}, bf16[2048,1024]{1,0:T(8,128)(2,1)}, u32[]{:S(2)}) copy-start(bf16[2048,1024]{1,0:T(8,128)(2,1)} %get-tuple-element.36) | copy-start | bytes 12582916
  304.0 6.0 %copy-start.18 = (bf16[2048,1024]{1,0:T(8,128)(2,1)S(1)}, bf16[2048,1024]{1,0:T(8,128)(2,1)}, u32[]{:S(2)}) copy-start(bf16[2048,1024]{1,0:T(8,128)(2,1)} %get-tuple-element.35) | copy-start | bytes 12582916
  532.5 5.2 copy-start.1
  532.5 5.3 copy-start.3
  532.5 5.9 %copy-start.6 = (bf16[1,1024,1024]{2,1,0:T(8,128)(2,1)S(1)}, bf16[1,1024,1024]{2,1,0:T(8,128)(2,1)}, u32[]{:S(2)}) copy-start(bf16[1,1024,1024]{2,1,0:T(8,128)(2,1)} %param.28) | copy-start | bytes 6291460
  538.4 4.9 copy-start.9
  543.4 1.6 copy-start.12
  543.4 2.5 copy-start.13
  543.4 3.2 copy-start.11
  543.4 4.2 copy-start.10
Sparse Core Ops, SparseCore 0:
  107.9 75.4 all-gather.2
  185.6 73.1 all-gather.4

commit v4 on v3

--- a/solution.py
+++ b/solution.py
@@ -17,6 +17,7 @@
 
 NEG = -1e30
 BQ = 256
+PAIRS = 4
 
 def dot_t(a, b):
     return lax.dot_general(a, b, (((1,), (1,)), ((), ())), preferred_element_type=jnp.float32)
@@ -27,113 +28,108 @@
 def dot_c(a, b):
     return lax.dot_general(a, b, (((0,), (0,)), ((), ())), preferred_element_type=jnp.float32)
 
-def attention_kernel(pairs, tokens, lows, start_col, start_row, cos_ref, sin_ref, q_ref, k_ref, v_ref, do_ref,
-                     out_ref, dq_ref, dk_ref, dv_ref, bias, bias_t, dk_acc, dv_acc, m_sc, l_sc, acc_sc, dq_sc):
+def attention_kernel(pairs, tokens, lows, start_row, cos_ref, sin_ref, q_ref, k_ref, v_ref, do_ref,
+                     out_ref, turned_ref, dq_ref, dk_ref, dv_ref, bias, scores, weights, k_turned, v_turned, dk_acc, dv_acc, out_acc, dq_acc, slope):
+    bf, f32 = jnp.bfloat16, jnp.float32
     blocks = tokens // BQ
     span = blocks + 1
-    lane = lax.broadcasted_iota(jnp.int32, (BQ, 128), 1)
-    even = lane < 64
+    heads = 2 * pairs
+    even = lax.broadcasted_iota(jnp.int32, (BQ, 128), 1) < HEAD
+    fold = lambda x, op: op(x.reshape(BQ // 8, 8, BQ), axis=0)
 
     @pl.when(pl.program_id(0) == 0)
     def _():
         for qb in range(blocks):
-            start_c = start_col[qb * BQ:(qb + 1) * BQ, :]
-            start_r = start_row[:, qb * BQ:(qb + 1) * BQ]
-            q_c = tokens + qb * BQ + lax.broadcasted_iota(jnp.int32, (BQ, BQ), 0)
-            q_r = tokens + qb * BQ + lax.broadcasted_iota(jnp.int32, (BQ, BQ), 1)
+            start = start_row[:, qb * BQ:(qb + 1) * BQ]
+            query = tokens + qb * BQ + lax.broadcasted_iota(jnp.int32, (BQ, BQ), 1)
 
             def fill(kb, _):
-                k_r = kb * BQ + lax.broadcasted_iota(jnp.int32, (BQ, BQ), 1)
-                k_c = kb * BQ + lax.broadcasted_iota(jnp.int32, (BQ, BQ), 0)
-                slot = qb * span + kb - qb
-                bias[slot] = jnp.where((k_r >= start_c) & (k_r <= q_c), 0.0, NEG)
-                bias_t[slot] = jnp.where((k_c >= start_r) & (k_c <= q_r), 0.0, NEG)
+                key = kb * BQ + lax.broadcasted_iota(jnp.int32, (BQ, BQ), 0)
+                bias[qb * span + kb - qb] = jnp.where((key >= start) & (key <= query), 0.0, NEG).astype(bf)
                 return 0
             lax.fori_loop(lows[qb], blocks + qb + 1, fill, 0)
 
+    def prepare(kb, _):
+        rows = pl.ds(pl.multiple_of(kb * BQ, BQ), BQ)
+        for p in range(pairs):
+            cols = slice(p * 128, (p + 1) * 128)
+            k_turned[p, :, rows] = k_ref[rows, cols].T
+            v_turned[p, :, rows] = v_ref[rows, cols].T
+        return 0
+    lax.fori_loop(lows[0], 2 * blocks, prepare, 0)
     dk_acc[...] = jnp.zeros_like(dk_acc)
     dv_acc[...] = jnp.zeros_like(dv_acc)
-    heads = 2 * pairs
 
     def one_q(qb, _):
         q_rows = pl.ds(pl.multiple_of(qb * BQ, BQ), BQ)
-        low = lows[qb]
-        high = blocks + qb + 1
+        own_rows = pl.ds(pl.multiple_of(tokens + qb * BQ, BQ), BQ)
+        low, high = lows[qb], blocks + qb + 1
         q_h = []
         for p in range(pairs):
             q = q_ref[q_rows, p * 128:(p + 1) * 128]
             q_h += [jnp.where(even, q, 0), jnp.where(even, 0, q)]
-        m_sc[...] = jnp.full_like(m_sc, NEG)
-        l_sc[...] = jnp.zeros_like(l_sc)
-        acc_sc[...] = jnp.zeros_like(acc_sc)
-
-        def forward(kb, _):
-            k_rows = pl.ds(pl.multiple_of(kb * BQ, BQ), BQ)
-            b = bias[qb * span + kb - qb]
+
+        def score(kb, tops):
+            rows = pl.ds(pl.multiple_of(kb * BQ, BQ), BQ)
+            b = bias[qb * span + kb - qb].astype(f32)
+            new = []
+            for h in range(heads):
+                s = dot_t(k_ref[rows, (h // 2) * 128:(h // 2 + 1) * 128], q_h[h]) + b
+                scores[kb - qb, h] = s
+                new.append(jnp.maximum(tops[h], fold(s, jnp.max)))
+            return tuple(new)
+        tops = lax.fori_loop(low, high, score, tuple(jnp.full((8, BQ), NEG, f32) for _ in range(heads)))
+        tops = [jnp.max(t, axis=0, keepdims=True) for t in tops]
+        out_acc[...] = jnp.zeros_like(out_acc)
+        dq_acc[...] = jnp.zeros_like(dq_acc)
+
+        def attend(kb, sums):
+            rows = pl.ds(pl.multiple_of(kb * BQ, BQ), BQ)
+            new = []
+            for h in range(heads):
+                e = jnp.exp(scores[kb - qb, h] - tops[h])
+                new.append(sums[h] + fold(e, jnp.sum))
+                e = e.astype(bf)
+                weights[kb - qb, h] = e
+            for h in range(heads):
+                half = slice((h % 2) * HEAD, (h % 2 + 1) * HEAD)
+                out_acc[h // 2, half, :] += dot_n(v_turned[h // 2, half, rows], weights[kb - qb, h])
+            return tuple(new)
+        sums = lax.fori_loop(low, high, attend, tuple(jnp.zeros((8, BQ), f32) for _ in range(heads)))
+
+        do_h, deltas = [], []
+        for p in range(pairs):
+            cols = slice(p * 128, (p + 1) * 128)
+            inverse = [1.0 / jnp.sum(sums[h], axis=0, keepdims=True) for h in (2 * p, 2 * p + 1)]
+            inverse = jnp.concatenate([jnp.broadcast_to(v, (HEAD, BQ)) for v in inverse], axis=0)
+            out = out_acc[p] * inverse
+            out_ref[q_rows, cols] = out.T.astype(bf)
+            turned_ref[cols, q_rows] = out.astype(bf)
+            d_out = do_ref[q_rows, cols].astype(f32).T * inverse
+            product = out * d_out
+            deltas += [jnp.sum(product[:HEAD], axis=0, keepdims=True), jnp.sum(product[HEAD:], axis=0, keepdims=True)]
+            d_out = d_out.T.astype(bf)
+            do_h += [jnp.where(even, d_out, 0), jnp.where(even, 0, d_out)]
+
+        def back(kb, _):
+            rows = pl.ds(pl.multiple_of(kb * BQ, BQ), BQ)
+            for p in range(pairs):
+                v = v_ref[rows, p * 128:(p + 1) * 128]
+                for h in (2 * p, 2 * p + 1):
+                    d_prob = dot_t(v, do_h[h])
+                    slope[h] = (weights[kb - qb, h].astype(f32) * (d_prob - deltas[h])).astype(bf)
             for p in range(pairs):
                 cols = slice(p * 128, (p + 1) * 128)
-                k = k_ref[k_rows, cols]
-                v = v_ref[k_rows, cols]
-                outs, scales = [], []
-                for h in (2 * p, 2 * p + 1):
-                    s = dot_t(q_h[h], k) + b
-                    m_old = m_sc[h]
-                    m_new = jnp.maximum(m_old, jnp.max(s, axis=1, keepdims=True))
-                    e = jnp.exp(s - m_new[:, :1])
-                    a = jnp.exp(m_old - m_new)
-                    l_sc[h] = a * l_sc[h] + jnp.sum(e, axis=1, keepdims=True)
-                    m_sc[h] = m_new
-                    outs.append(dot_n(e.astype(jnp.bfloat16), v))
-                    scales.append(a)
-                acc_sc[p] = acc_sc[p] * jnp.where(even, scales[0], scales[1]) + jnp.where(even, outs[0], outs[1])
+                dv_acc[rows, cols] += dot_n(weights[kb - qb, 2 * p], do_h[2 * p]) + dot_n(weights[kb - qb, 2 * p + 1], do_h[2 * p + 1])
+                dk_acc[rows, cols] += dot_n(slope[2 * p], q_h[2 * p]) + dot_n(slope[2 * p + 1], q_h[2 * p + 1])
+            for h in range(heads):
+                half = slice((h % 2) * HEAD, (h % 2 + 1) * HEAD)
+                dq_acc[h // 2, half, :] += dot_n(k_turned[h // 2, half, rows], slope[h])
             return 0
-        lax.fori_loop(low, high, forward, 0)
-
-        do_h, lse_r, delta_r = [], [], []
-        for p in range(pairs):
-            cols = slice(p * 128, (p + 1) * 128)
-            o = acc_sc[p] / jnp.where(even, l_sc[2 * p], l_sc[2 * p + 1])
-            out_ref[q_rows, cols] = o.astype(jnp.bfloat16)
-            do = do_ref[q_rows, cols]
-            prod = o * do.astype(jnp.float32)
-            for h in (2 * p, 2 * p + 1):
-                mine = even if h % 2 == 0 else ~even
-                delta = jnp.sum(jnp.where(mine, prod, 0.0), axis=1, keepdims=True)
-                lse = m_sc[h] + jnp.log(l_sc[h])
-                both = jnp.where(even, lse, delta)
-                turned = both.T
-                lse_r.append(turned[0:1, :])
-                delta_r.append(turned[64:65, :])
-                do_h.append(jnp.where(mine, do, 0))
-        dq_sc[...] = jnp.zeros_like(dq_sc)
-
-        def backward(kb, _):
-            k_rows = pl.ds(pl.multiple_of(kb * BQ, BQ), BQ)
-            b = bias_t[qb * span + kb - qb]
-            for p in range(pairs):
-                cols = slice(p * 128, (p + 1) * 128)
-                k = k_ref[k_rows, cols]
-                v = v_ref[k_rows, cols]
-                dqs, dks, dvs = [], None, None
-                for h in (2 * p, 2 * p + 1):
-                    s = dot_t(k, q_h[h]) + b
-                    prob = jnp.exp(s - lse_r[h])
-                    dp = dot_t(v, do_h[h])
-                    ds = (prob * (dp - delta_r[h])).astype(jnp.bfloat16)
-                    dv = dot_n(prob.astype(jnp.bfloat16), do_h[h])
-                    dk = dot_n(ds, q_h[h])
-                    dvs = dv if dvs is None else dvs + dv
-                    dks = dk if dks is None else dks + dk
-                    dqs.append(dot_c(ds, k))
-                dv_acc[k_rows, cols] += dvs
-                dk_acc[k_rows, cols] += dks
-                dq_sc[p] += jnp.where(even, dqs[0], dqs[1])
-            return 0
-        lax.fori_loop(low, high, backward, 0)
-        own_rows = pl.ds(pl.multiple_of(tokens + qb * BQ, BQ), BQ)
+        lax.fori_loop(low, high, back, 0)
         for p in range(pairs):
             dq_ref[q_rows, p * 128:(p + 1) * 128] = unrotate(
-                dq_sc[p] * 0.125, cos_ref[own_rows, :], sin_ref[own_rows, :]).astype(jnp.bfloat16)
+                dq_acc[p].T * 0.125, cos_ref[own_rows, :], sin_ref[own_rows, :]).astype(bf)
         return 0
     lax.fori_loop(0, blocks, one_q, 0)
 
@@ -141,10 +137,11 @@
         rows = pl.ds(pl.multiple_of(kb * BQ, BQ), BQ)
         for p in range(pairs):
             cols = slice(p * 128, (p + 1) * 128)
-            dk_ref[rows, cols] = unrotate(dk_acc[rows, cols], cos_ref[rows, :], sin_ref[rows, :]).astype(jnp.bfloat16)
-            dv_ref[rows, cols] = dv_acc[rows, cols].astype(jnp.bfloat16)
+            dk_ref[rows, cols] = unrotate(dk_acc[rows, cols], cos_ref[rows, :], sin_ref[rows, :]).astype(bf)
+            dv_ref[rows, cols] = dv_acc[rows, cols].astype(bf)
         return 0
     lax.fori_loop(0, 2 * blocks, finish, 0)
+
 
 def swap_pairs(x):
     odd = lax.broadcasted_iota(jnp.int32, x.shape, 1) % 2 == 1
@@ -159,11 +156,11 @@
 
 def attention(lows, starts, cosine, sine, mixed, d_out):
     tokens, width = d_out.shape
-    pairs = 2
+    pairs = PAIRS
     wide = 128 * pairs
     groups = width // wide
     blocks = tokens // BQ
-    whole = lambda shape: pl.BlockSpec(shape, lambda g, lows: (0,) * len(shape))
+    whole = lambda shape: pl.BlockSpec(shape, lambda g, lows: (0,) * len(shape), pipeline_mode=pl.Buffered(1))
     own = pl.BlockSpec((tokens, wide), lambda g, lows: (0, g))
     both = pl.BlockSpec((2 * tokens, wide), lambda g, lows: (0, g))
     q_spec = pl.BlockSpec((tokens, wide), lambda g, lows: (1, g))
@@ -174,22 +171,22 @@
     one, two = jax.ShapeDtypeStruct((tokens, width), bf), jax.ShapeDtypeStruct((2 * tokens, width), bf)
     return pl.pallas_call(
         functools.partial(attention_kernel, pairs, tokens),
-        out_shape=[one, one, two, two],
+        out_shape=[one, jax.ShapeDtypeStruct((width, tokens), bf), one, two, two],
         grid_spec=pltpu.PrefetchScalarGridSpec(
             num_scalar_prefetch=1,
             grid=(groups,),
-            in_specs=[whole((tokens, 1)), whole((1, tokens)), whole((2 * tokens, 128)), whole((2 * tokens, 128)),
-                      q_spec, k_spec, v_spec, own],
-            out_specs=[own, own, both, both],
-            scratch_shapes=[pltpu.VMEM((slots, BQ, BQ), f32), pltpu.VMEM((slots, BQ, BQ), f32),
-                            pltpu.VMEM((2 * tokens, wide), f32), pltpu.VMEM((2 * tokens, wide), f32),
-                            pltpu.VMEM((2 * pairs, BQ, 128), f32), pltpu.VMEM((2 * pairs, BQ, 128), f32),
-                            pltpu.VMEM((pairs, BQ, 128), f32), pltpu.VMEM((pairs, BQ, 128), f32)],
+            in_specs=[whole((1, tokens)), whole((2 * tokens, 128)), whole((2 * tokens, 128)), q_spec, k_spec, v_spec, own],
+            out_specs=[own, pl.BlockSpec((wide, tokens), lambda g, lows: (g, 0)), own, both, both],
+            scratch_shapes=[pltpu.VMEM((slots, BQ, BQ), bf), pltpu.VMEM((blocks + 1, 2 * pairs, BQ, BQ), f32),
+                            pltpu.VMEM((blocks + 1, 2 * pairs, BQ, BQ), bf), pltpu.VMEM((pairs, 128, 2 * tokens), bf),
+                            pltpu.VMEM((pairs, 128, 2 * tokens), bf), pltpu.VMEM((2 * tokens, wide), f32),
+                            pltpu.VMEM((2 * tokens, wide), f32), pltpu.VMEM((pairs, 128, BQ), f32),
+                            pltpu.VMEM((pairs, 128, BQ), f32), pltpu.VMEM((2 * pairs, BQ, BQ), bf)],
         ),
-        compiler_params=pltpu.CompilerParams(vmem_limit_bytes=56 * 2**20),
+        compiler_params=pltpu.CompilerParams(vmem_limit_bytes=62 * 2**20),
         cost_estimate=pl.CostEstimate(flops=60 * 10**9, bytes_accessed=30 * 2**20, transcendentals=0),
         name="attention",
-    )(lows, starts[:, None], starts[None, :], cosine, sine, mixed, mixed, mixed, d_out)
+    )(lows, starts[None, :], cosine, sine, mixed, mixed, mixed, d_out)
 
 
 def rope_tables(position):
@@ -209,11 +206,12 @@
 
 
 CHUNK = 256
+AHEAD = 3
 
 
 def gather_kernel(dims, w_out, w_qkv, x_hbm, grad, vec_own, cos_ref, sin_ref,
-                  wout_all, wqkv_all, normed_all, mixed_all, d_attended, prior_all, vec_all,
-                  wbuf, own, prior, normed, mixed, d_att, vec, vec_recv, in_sem, load_sem, out_sem, zsend, zrecv, ysend, yrecv,
+                  wout_all, wqkv_all, normed_own, normed_prior, turned_own, turned_prior, grad_turned, mixed_all, d_attended, prior_all, vec_all,
+                  wbuf, own, prior, normed, turned, mixed, d_att, vec, vec_recv, in_sem, load_sem, out_sem, zsend, zrecv, ysend, yrecv,
                   csend, crecv, psend, precv, vsend, vrecv):
     rows, seqs, tokens, width = dims
     bf, f32 = jnp.bfloat16, jnp.float32
@@ -290,40 +288,50 @@
 
     @pl.when(has_next)
     def _():
-        for i in range(4):
+        for i in range(2):
             prior_copy(i).start()
-    for k in range(total):
+
+    @pl.when(jnp.logical_not(has_prior))
+    def _():
+        prior[...] = jnp.zeros_like(prior)
+
+    def z_start(k):
         load(k).wait()
         for d in range(1, levels):
             z_copy(k, d).start()
-
-    for d in range(1, levels):
-        z_vec(d).wait()
-    value = vec[0]
-    for d in range(1, levels):
-        value = value + vec_recv[1 + d]
-    vec[1] = value
-    vec_copy(1, y_id).start()
-    fetch.wait()
-    vec_copy(1, y_id).wait()
-    vec[2] = value + vec_recv[1]
+    for k in range(AHEAD):
+        z_start(k)
+
     swap = pltpu.make_async_remote_copy(vec.at[2], vec_recv.at[0], vsend.at[0], vrecv.at[0], device_id=core_id,
                                         device_id_type=MESH)
-    swap.start()
-    swap.wait()
-    vec_all[...] = vec[2] + vec_recv[0]
-    gain, bias = vec_all[0:1, :], vec_all[1:2, :]
-
-    def normalize(source, half):
-        def body(i, _):
-            block = pl.ds(pl.multiple_of(i * quarter, quarter), quarter)
-            values = source[block, :].astype(f32)
-            centered = values - jnp.mean(values, axis=1, keepdims=True)
-            unit = centered * lax.rsqrt(jnp.mean(centered * centered, axis=1, keepdims=True) + EPS)
-            normed[half, block, :] = (unit * gain + bias).astype(bf)
-            return 0
-        return body
-    lax.fori_loop(0, 4, normalize(own, 1), 0)
+
+    def share_vectors(it):
+        if it == 0:
+            for d in range(1, levels):
+                z_vec(d).wait()
+            value = vec[0]
+            for d in range(1, levels):
+                value = value + vec_recv[1 + d]
+            vec[1] = value
+            vec_copy(1, y_id).start()
+        if it == 1:
+            vec_copy(1, y_id).wait()
+            vec[2] = vec[1] + vec_recv[1]
+            swap.start()
+        if it == 2:
+            swap.wait()
+            vec_all[...] = vec[2] + vec_recv[0]
+
+    def normalize(source, half, i):
+        block = slice(i * quarter, (i + 1) * quarter)
+        values = source[block, :].astype(f32)
+        centered = values - jnp.mean(values, axis=1, keepdims=True)
+        unit = centered * lax.rsqrt(jnp.mean(centered * centered, axis=1, keepdims=True) + EPS)
+        normed[half, block, :] = (unit * vec_all[0:1, :] + vec_all[1:2, :]).astype(bf)
+
+    def turn(source, place, i):
+        block = slice(i * quarter, (i + 1) * quarter)
+        turned[place, :, block] = source[block, :].T
 
     outs = []
 
@@ -331,27 +339,23 @@
         copy = pltpu.make_async_copy(src, dst, out_sem.at[len(outs)])
         copy.start()
         outs.append(copy)
-    send_out(normed.at[1], normed_all.at[1])
-
-    def multiply(half, j):
+
+    def multiply(half, j, parts):
         cols = slice(j * CHUNK, (j + 1) * CHUNK)
         tall = tokens // 2
-
-        def body(i, _):
-            block = pl.ds(pl.multiple_of(i * tall, tall), tall)
+        for i in parts:
+            block = slice(i * tall, (i + 1) * tall)
             product = dot_n(normed[half, block, :], wbuf[n_out + j].reshape(width, CHUNK))
             if j * CHUNK < 2 * width:
                 scale = 0.125 if j * CHUNK < width else 1.0
-                place = pl.ds(pl.multiple_of(half * tokens + i * tall, tall), tall)
+                place = slice(half * tokens + i * tall, half * tokens + (i + 1) * tall)
                 cosine, sine = cos_ref[place, :] * scale, sin_ref[place, :] * scale
                 for a in range(CHUNK // 128):
                     mixed[half, block, j * CHUNK + a * 128:j * CHUNK + (a + 1) * 128] = rotate(
                         product[:, a * 128:(a + 1) * 128], cosine, sine).astype(bf)
             else:
                 mixed[half, block, cols] = product.astype(bf)
-            return 0
-        lax.fori_loop(0, 2, body, 0)
-        send_out(mixed.at[half, :, cols], mixed_all.at[half, :, cols])
+            send_out(mixed.at[half, block, cols], mixed_all.at[half, block, cols])
 
     def project_back():
         tall = tokens // 4
@@ -366,14 +370,35 @@
         lax.fori_loop(0, 4, body, 0)
         send_out(d_att, d_attended)
 
+    def prior_landed(i):
+        @pl.when(has_prior)
+        def _():
+            prior_copy(i).wait_recv()
+
+    def prior_next(i):
+        @pl.when(has_next)
+        def _():
+            prior_copy(i).wait_send()
+            prior_copy(i + 2).start()
+
     for it in range(total + 2):
         if it < total:
             for d in range(1, levels):
                 z_landed(it, d).wait_recv()
+            if it + AHEAD < total:
+                z_start(it + AHEAD)
             y_copy(it, y).start()
         if 0 <= it - 1 < total:
             y_copy(it - 1, 1 - y).wait_recv()
             core_copy(it - 1, core).start()
+        share_vectors(it)
+        if it == 3:
+            fetch.wait()
+        if 3 <= it <= 4:
+            normalize(own, 1, 2 * it - 6)
+            normalize(own, 1, 2 * it - 5)
+        if it == 5:
+            send_out(normed.at[1], normed_own)
         if 0 <= it - 2 < total:
             k = it - 2
             core_copy(k, 1 - core).wait_recv()
@@ -383,25 +408,37 @@
                     project_back()
             else:
                 send_out(wbuf.at[k], wqkv_all.at[:, :, :, :, (k - n_out) * CHUNK:(k - n_out + 1) * CHUNK])
-                multiply(1, k - n_out)
-
-    @pl.when(has_prior)
-    def _():
-        for i in range(4):
-            prior_copy(i).wait_recv()
-
-    @pl.when(jnp.logical_not(has_prior))
-    def _():
-        prior[...] = jnp.zeros_like(prior)
+                multiply(1, k - n_out, (0, 1))
+        if it < 4:
+            turn(grad, 2, it)
+        if it == 4:
+            send_out(turned.at[2], grad_turned)
+        if 8 <= it < 12:
+            turn(normed.at[1], 1, it - 8)
+        if it == 12:
+            send_out(turned.at[1], turned_own)
+        if it in (4, 8):
+            prior_next(it // 4 - 1)
+        if it in (5, 9, 13):
+            i = it // 4 - 1
+            prior_landed(i)
+            normalize(prior, 0, i)
+            turn(normed.at[0], 0, i)
+        if it - 2 - n_out >= n_qkv // 3:
+            multiply(0, it - 2 - n_out, (0,))
+
+    prior_landed(3)
+    normalize(prior, 0, 3)
+    turn(normed.at[0], 0, 3)
     send_out(prior, prior_all)
-    lax.fori_loop(0, 4, normalize(prior, 0), 0)
-    send_out(normed.at[0], normed_all.at[0])
+    send_out(normed.at[0], normed_prior)
+    send_out(turned.at[0], turned_prior)
     for j in range(n_qkv // 3, n_qkv):
-        multiply(0, j)
+        multiply(0, j, (1,))
 
     @pl.when(has_next)
     def _():
-        for i in range(4):
+        for i in (2, 3):
             prior_copy(i).wait_send()
     for k in range(total):
         for d in range(1, levels):
@@ -420,26 +457,27 @@
     dma = pltpu.SemaphoreType.DMA
     total = 4 * width // CHUNK
     shape = jax.ShapeDtypeStruct
-    wout_all, wqkv_all, normed, mixed, d_att, prior, vec = pl.pallas_call(
+    token, turned = shape((tokens, width), bf), shape((width, tokens), bf)
+    wout_all, wqkv_all, normed, normed_prior, turned_own, turned_prior, grad_turned, mixed, d_att, prior, vec = pl.pallas_call(
         functools.partial(gather_kernel, (rows, seqs, tokens, width)),
-        out_shape=[shape((levels, 2, 2, share, width), bf), shape((levels, 2, 2, share, 3 * width), bf), shape((2, tokens, width), bf),
-                   shape((2, tokens, 3 * width), bf), shape((tokens, width), bf), shape((tokens, width), bf), shape((8, width), f32)],
+        out_shape=[shape((levels, 2, 2, share, width), bf), shape((levels, 2, 2, share, 3 * width), bf), token, token,
+                   turned, turned, turned, shape((2, tokens, 3 * width), bf), token, token, shape((8, width), f32)],
         in_specs=[hbm, hbm, hbm, vmem, vmem, vmem, vmem],
-        out_specs=[hbm] * 6 + [vmem],
+        out_specs=[hbm] * 10 + [vmem],
         scratch_shapes=[
             pltpu.VMEM((total, levels, 2, 2, share, CHUNK), bf),
-            pltpu.VMEM((tokens, width), bf), pltpu.VMEM((tokens, width), bf), pltpu.VMEM((2, tokens, width), bf),
+            pltpu.VMEM((tokens, width), bf), pltpu.VMEM((tokens, width), bf), pltpu.VMEM((2, tokens, width), bf), pltpu.VMEM((3, width, tokens), bf),
             pltpu.VMEM((2, tokens, 3 * width), bf), pltpu.VMEM((tokens, width), bf),
             pltpu.VMEM((3, 8, width), f32), pltpu.VMEM((1 + levels, 8, width), f32),
-            dma, dma((total,)), dma((2 * total + 8,)), dma((total, levels - 1)), dma((total, levels - 1)),
+            dma, dma((total,)), dma((5 * total,)), dma((total, levels - 1)), dma((total, levels - 1)),
             dma((total,)), dma((total,)), dma((total,)), dma((total,)), dma((4,)), dma((4,)), dma((1 + levels,)), dma((1 + levels,)),
         ],
         compiler_params=pltpu.CompilerParams(collective_id=0, has_side_effects=True, vmem_limit_bytes=60 * 2**20),
         cost_estimate=pl.CostEstimate(flops=20 * 10**9, bytes_accessed=40 * 2**20, transcendentals=0),
         name="gather",
     )(w_out, w_qkv, x, grad, vec_own, cosine, sine)
-    return (wout_all.reshape(width, width), wqkv_all.reshape(width, 3 * width), normed.reshape(2 * tokens, width),
-            mixed.reshape(2 * tokens, 3 * width), d_att, prior, vec)
+    return (wout_all.reshape(width, width), wqkv_all.reshape(width, 3 * width), normed, normed_prior, turned_own, turned_prior,
+            grad_turned, mixed.reshape(2 * tokens, 3 * width), d_att, prior, vec)
 
 
 RING = 12
@@ -804,32 +842,33 @@
     vec_own = jnp.concatenate([place(norm_gain, 1), place(norm_bias, 1), place(b_fc_out, 1), place(b_fc_in, 4),
                                jnp.zeros((1, width), f32)])
     grad_out = cotangent[0]
-    w_out_all, w_qkv_all, normed_both, mixed, d_attended, prior_input, vectors = gather_all(
+    (w_out_all, w_qkv_all, normed, normed_prior, turned_own, turned_prior, grad_turned, mixed, d_attended, prior_input,
+     vectors) = gather_all(
         rows, seqs, w_attn_out, w_qkv, block_input[0], grad_out, vec_own, cosine, sine)
     w_fc_in, w_fc_out, vectors = lax.optimization_barrier((w_fc_in, w_fc_out, vectors))
     w_in_all = lax.all_gather(w_fc_in, "rows", axis=0, tiled=True)
     w_back_all = lax.all_gather(w_fc_out, "rows", axis=0, tiled=True)
     gain, bias, b_back_all = vectors[0], vectors[1], vectors[2]
     b_in_all = vectors[3:7].reshape(1, 4 * width)
-    normed = normed_both[tokens:]
     unit, scale = layer_norm_stats(inputs)
     prior_unit, _ = layer_norm_stats(prior_input.astype(f32))
-    attended, d_q, d_k, d_v = attention(lows, starts, cosine, sine, mixed, d_attended)
+    attended, attended_turned, d_q, d_k, d_v = attention(lows, starts, cosine, sine, mixed, d_attended)
 
     d_normed_both = jnp.dot(d_k, w_qkv_all[:, width:2 * width].T, preferred_element_type=f32) + jnp.dot(
         d_v, w_qkv_all[:, 2 * width:].T, preferred_element_type=f32)
     d_prior = d_normed_both[:tokens]
     back = lax.ppermute(d_prior.astype(bf), "seq", [(i + 1, i) for i in range(seqs - 1)])
     vec_in = jnp.stack([jnp.sum(d_prior * prior_unit, axis=0), jnp.sum(d_prior, axis=0)])
-    grads = [jnp.dot(normed.T, d_q, preferred_element_type=f32).astype(bf),
-             jnp.dot(normed_both.T, d_k, preferred_element_type=f32).astype(bf),
-             jnp.dot(normed_both.T, d_v, preferred_element_type=f32).astype(bf)]
-    grad_w_out = jnp.dot(attended.T, grad_out, preferred_element_type=f32).astype(bf)
+    product = lambda turned, values: jnp.dot(turned, values, preferred_element_type=f32)
+    grads = [product(turned_own, d_q).astype(bf),
+             (product(turned_own, d_k[tokens:]) + product(turned_prior, d_k[:tokens])).astype(bf),
+             (product(turned_own, d_v[tokens:]) + product(turned_prior, d_v[:tokens])).astype(bf)]
+    grad_w_out = product(attended_turned, grad_out).astype(bf)
     base_dn = d_normed_both[tokens:] + jnp.dot(d_q, w_qkv_all[:, :width].T, preferred_element_type=f32)
     base_out = inputs + jnp.dot(attended, w_out_all, preferred_element_type=f32) + b_back_all
 
     g_qkv, g_out, g_in, g_back, vec, block_output, d_normed = reduce_all(
-        rows, seqs, *grads, grad_w_out, normed, normed.T, grad_out, grad_out.T, block_input[0], w_in_all, w_back_all,
+        rows, seqs, *grads, grad_w_out, normed, turned_own, grad_out, grad_turned, block_input[0], w_in_all, w_back_all,
         b_in_all, base_out, base_dn, vec_in)
 
     d_normed = d_normed + back.astype(f32)

time: 562 us -> 452 us (0.80)
  Pallas kernels: 433 us -> 316 us
  waiting for transfers between devices: 0.72 us -> 28.2 us
  local copies, waits for them, and re-layouts: 35.5 us -> 15.9 us
    pallas_call x1, Pallas kernels: 131 us -> 67.7 us  [attention(): pl.pallas_call(functools.partial(attention_kernel, pairs, tokens), out_sh...]
    pallas_call x1, Pallas kernels: 214 us -> 171 us  [reduce_all(): pl.pallas_call(functools.partial(reduce_kernel, (rows, seqs, q_rows, edge...]
    all_gather x1, waiting for transfers between devices: 0.01 us -> 27.5 us  [body(): w_back_all = lax.all_gather(w_fc_out, 'rows', axis=0, tiled=True)]
    pallas_call x1, Pallas kernels: 87.8 us -> 77.6 us  [gather_all(): pl.pallas_call(functools.partial(gather_kernel, (rows, seqs, tokens, widt...]
    transpose x2 -> x0, local copies, waits for them, and re-layouts: 8.15 us -> none  [the longest x1 4.21 us: body(): grads = [jnp.dot(normed.T, d_q, preferred_element_type=f32).astype(bf), j...]
    pallas_call x1 -> x0, local copies, waits for them, and re-layouts: 6.3 us -> none  [gather_all(): pl.pallas_call(functools.partial(gather_kernel, (rows, seqs, tokens, widt...]
    dot_general x4 -> x6, matrix products: 19.3 us -> 19.6 us  [body(): jnp.dot(turned, values, preferred_element_type=f32)]
  transfers between devices with their start and end apart: 3 -> 3, of which waited for: 0 -> 1; matrix products, arithmetic and copies ran while one was open for 13% -> 12% of each run, Pallas kernels for 62% -> 53%
where the time goes in v4:
time: 452 us; the launch traced here: 448 us
  Pallas kernels  316 us (70%)
  matrix products  43.9 us (10%)
  waiting for transfers between devices  28.2 us (6%)
  other arithmetic  27.6 us (6%)
  local copies, waits for them, and re-layouts  15.9 us (4%)
  between operations  14.6 us (3%)
    pallas_call x1, Pallas kernels, reduce_all(): pl.pallas_call(functools.partial(reduce_kernel, (rows, seqs, q_rows, edge...  171 us
    pallas_call x1, Pallas kernels, gather_all(): pl.pallas_call(functools.partial(gather_kernel, (rows, seqs, tokens, widt...  77.6 us
    pallas_call x1, Pallas kernels, attention(): pl.pallas_call(functools.partial(attention_kernel, pairs, tokens), out_sh...  67.7 us
    all_gather x1, waiting for transfers between devices, body(): w_back_all = lax.all_gather(w_fc_out, 'rows', axis=0, tiled=True)  27.5 us
    dot_general x6, matrix products, body(): jnp.dot(turned, values, preferred_element_type=f32)  19.6 us
    unnamed x59, local copies, waits for them, and re-layouts  10.6 us
  transfers between devices with their start and end apart: 3, of which 1 were waited for; matrix products, arithmetic and copies ran while one was open for 12% of the time, Pallas kernels for 53%

profile of v4, /device:TPU:0, one launch (start us, length us, event | category | flops | bytes accessed | tf_op | source)
XLA Modules:
  0.0 448.1 jit_solution(14164340853657881615)
XLA Ops:
  7.2 0.0 all-gather.3.cloned.1.call-start
  7.2 0.7 convert_element_type.46
  7.9 0.7 convert_element_type.47
  8.5 0.7 convert_element_type.48
  9.2 0.7 compare_select_fusion.1
  9.9 0.1 reshape.109
  10.0 0.1 reshape.110
  10.1 0.1 reshape.111
  10.1 0.7 convert_element_type.49
  10.8 0.7 compare_select_fusion
  11.5 0.8 select_reduce_fusion.1
  12.3 0.7 select_reduce_fusion
  13.1 6.2 %fusion.36 = (f32[2048,128]{1,0:T(8,128)}, f32[2048,128]{1,0:T(8,128)}) fusion(f32[128]{0:T(128)} %constant.70, f32[128]{0:T(128)} %constant.69, f32[2048]{0:T(1024)S(1)} %subtract_convert_fusion), kind=kLoop, calls=%fused_computation.46 | loop fusion | flops 524288 | bytes 2106368 | tf_op jit(solution)/shard_map/mul | solution.py:197
  19.3 0.7 concatenate.3.vec_own
  20.0 77.6 %gather.1 = (bf16[4,2,2,64,1024]{4,3,2,1,0:T(8,128)(2,1)}, bf16[4,2,2,64,3072]{4,3,2,1,0:T(8,128)(2,1)}, bf16[1024,1024]{1,0:T(8,128)(2,1)}, bf16[1024,1024]{1,0...) custom-call(bf16[64,1024]{1,0:T(8,128)(2,1)} %w_out.1, ...), custom_call_target="tpu_custom_call" | custom-call | flops 20000000000 | bytes 41943040 | tf_op jit(solution)/shard_map/gather/pallas_call | solution.py:461
  97.6 0.0 all-gather.3.cloned.1.call-update
  97.6 0.0 all-gather.5.cloned.1.call-start
  97.7 0.7 all-gather.5.cloned.1.call-update
  98.4 0.0 copy-start.13
  98.4 0.1 slice.55
  98.5 0.5 and_select_fusion.lows
  99.0 67.7 %attention.1 = (bf16[1024,1024]{1,0:T(8,128)(2,1)}, bf16[1024,1024]{1,0:T(8,128)(2,1)}, bf16[1024,1024]{1,0:T(8,128)(2,1)}, bf16[2048,1024]{1,0:T(8,128)(2,1)}, bf16[2048,1024]{1,0:T(8,128)(2,1)}) custom-call(s32[4]{0:T(128)} %and_select_fusion.lows, s32[1,1024]{1,0:T(1,128)} %bitcast.66, f32[2048,128]{1,0:T(8,128)} %get-tuple-element.70.cos_ref, ...), custom_call_target="tpu_custom_call" | custom-call | flops 60000002048 | bytes 31457280 | tf_op jit(solution)/shard_map/attention/pallas_call | solution.py:172
  166.8 7.3 %fusion.19 = f32[2048,1024]{1,0:T(8,128)S(1)} fusion(bf16[2048,1024]{1,0:T(8,128)(2,1)} %get-tuple-element.39, bf16[1024,3072]{1,0:T(8,128)(2,1)} %bitcast.73), kind=kOutput, calls=%fused_computation.31 | convolution fusion | flops 4294967296 | bytes 14680064 | tf_op jit(solution)/shard_map/dot_general | solution.py:857
  174.1 6.4 %convolution_add_fusion = f32[2048,1024]{1,0:T(8,128)S(1)} fusion(f32[2048,1024]{1,0:T(8,128)S(1)} %fusion.19, bf16[2048,1024]{1,0:T(8,128)(2,1)S(1)} %copy-done.16, bf16[1024,3072]{1,0:T(8,128)(2,1)} %bitcast.74), kind=kOutput, calls=%fused_computation.25 | convolution fusion | flops 4297064448 | bytes 23068672 | tf_op jit(solution)/shard_map/dot_general | solution.py:857
  180.4 3.2 copy-done.4
  183.7 1.6 slice.107
  185.3 1.3 collective-permute-start
  186.6 0.6 copy.28
  187.2 0.3 convert_reduce_fusion.1
  187.6 0.0 copy-start
  187.6 0.7 fusion.12
  188.3 3.1 fusion.14
  191.4 0.6 pad_maximum_fusion.vec_in
  192.0 0.3 convert_reduce_fusion
  192.4 0.7 fusion.11
  193.1 0.0 copy-start.15
  193.2 2.3 fusion.21
  195.5 0.0 copy-start.5
  195.5 2.3 fusion.25
  197.9 3.7 convolution_convert_fusion
  201.7 0.0 slice-start
  201.7 3.7 convolution_convert_fusion.1
  205.3 4.4 fusion.15.base_out
  209.7 6.3 %slice_add_fusion.base_dn = f32[1024,1024]{1,0:T(8,128)} fusion(f32[2048,1024]{1,0:T(8,128)S(1)} %bitcast.56, bf16[1024,1024]{1,0:T(8,128)(2,1)S(1)} %copy-done.18, bf16[1024,3072]{1,0:T(8,128)(2,1)} %bitcast.75), kind=kOutput, calls=%fused_computation.21 | convolution fusion | flops 2148532224 | bytes 12582912 | tf_op jit(solution)/shard_map/dot_general | solution.py:867
  216.1 3.9 add_convert_fusion
  219.9 3.7 add_convert_fusion.1
  223.6 27.5 %all-gather.5.cloned.1.call-done.w_back = bf16[4096,1024]{1,0:T(8,128)(2,1)} async-done(((bf16[256,1024]{1,0:T(8,128)(2,1)}), bf16[4096,1024]{1,0:T(8,128)(2,1)}) %all-gather.5.cloned.1.call-update) | async-done | bytes 8388624 | tf_op jit(solution)/shard_map/all_gather | solution.py:850
  251.1 171.1 %reduce.1 = (f32[64,3072]{1,0:T(8,128)}, f32[64,1024]{1,0:T(8,128)}, f32[64,4096]{1,0:T(8,128)}, f32[256,1024]{1,0:T(8,128)}, f32[8,1024]{1,0:T(8,128)}, /*index...) custom-call(bf16[8,2,64,1024]{3,2,1,0:T(8,128)(2,1)} %bitcast.78, bf16[8,2,64,1024]{3,2,1,0:T(8,128)(2,1)} %bitcast.80, ...), custom_call_target="tpu_custom_call" | custom-call | flops 99999997952 | bytes 104857600 | tf_op jit(solution)/shard_map/reduce/pallas_call | solution.py:786
  422.2 0.8 slice_bitcast_fusion
  423.0 0.9 fusion.42
  423.8 0.6 fusion.40
  424.4 0.6 fusion.38
  425.0 0.0 copy-start.6
  425.0 4.5 %fusion.35 = (f32[1024]{0:T(1024)S(1)}, f32[1024]{0:T(1024)S(1)}) fusion(f32[1024]{0:T(1024)S(1)} %bitcast.60, f32[1024,1024]{1,0:T(8,128)} %get-tuple-element.54, bf16[1024,1024]{1,0:T(8,128)(2,1)} %collective-permute-done, f32[1024]{0:T(1024)S(1)} %add_rsqrt_fusion, f32[1024]{0:T(1024)S(1)} %broadcast_multiply_fusion.1, bf16[1,1024,1024]{2,1,0:T(8,128)(2,1)} %param.18), kind=kLoop, calls=%fused_computation.45 | loop fusion | flops 9435136 | bytes 8409088 | tf_op jit(solution)/shard_map/reduce_sum | solution.py:876
  429.5 0.6 dynamic_slice.22
  430.2 0.1 copy-done.3
  430.3 0.6 copy-done.6
  430.9 4.9 %fusion.10 = f32[1,1024,1024]{2,1,0:T(8,128)} fusion(f32[1024]{0:T(1024)S(1)} %get-tuple-element.74, f32[1024]{0:T(1024)S(1)} %add_rsqrt_fusion, f32[1024]{0:T(1024)S(1)} %broadcast_multiply_fusion.1, f32[1024]{0:T(1024)S(1)} %get-tuple-element.75, f32[1024]{0:T(1024)S(1)} %bitcast.61, f32[1024,1024]{1,0:T(8,128)S(1)} %copy-done.3, ...), kind=kLoop, calls=%fused_computation.15 | loop fusion | flops 12582912 | bytes 14700544 | tf_op jit(solution)/shard_map/broadcast_in_dim | solution.py:880
  435.9 1.3 copy.37
  437.2 0.3 copy-done.10
  437.5 0.9 copy.38
  438.4 0.7 copy.39
  439.1 1.0 copy.40
  440.0 1.0 copy.41
  (56 shorter events, 0.2 us)
Async XLA Ops:
  7.2 216.4 %all-gather.3.cloned.1.call-start = ((), (), s32[]{:S(2)}) async-start(), calls=%async_computation | async-start | bytes 8912896 | tf_op jit(solution)/shard_map/all_gather | solution.py:849
  97.6 153.4 %all-gather.5.cloned.1.call-start = ((), (), s32[]{:S(2)}) async-start(), calls=%async_computation.1 | async-start | bytes 8912896 | tf_op jit(solution)/shard_map/all_gather | solution.py:850
  98.4 0.6 copy-start.13
  166.8 7.3 %copy-start.16 = (bf16[2048,1024]{1,0:T(8,128)(2,1)S(1)}, bf16[2048,1024]{1,0:T(8,128)(2,1)}, u32[]{:S(2)}) copy-start(bf16[2048,1024]{1,0:T(8,128)(2,1)} %get-tuple-element.41) | copy-start | bytes 12582916
  180.4 3.2 copy-start.4
  183.7 2.9 copy-start.12
  183.7 3.6 copy-start.2
  185.3 239.7 %collective-permute-start = (bf16[1024,1024]{1,0:T(8,128)(2,1)}, bf16[1024,1024]{1,0:T(8,128)(2,1)}, u32[]{:S(2)}, u32[]{:S(2)}) collective-permute-start(bf16[1024,1024]{1,0:T(8,128)(2,1)} %slice.107), channel_id=1, source_target_pairs={{1,0},{3,2},{5,4},{7,6},{9,8},{11,10},{13,12},{15,14},{17,16},{19,... | collective-permute-start | bytes 6291464 | tf_op jit(solution)/shard_map/ppermute | solution.py:860
  187.6 4.4 copy-start
  188.3 4.8 %copy-start.17 = (bf16[2048,1024]{1,0:T(8,128)(2,1)S(1)}, bf16[2048,1024]{1,0:T(8,128)(2,1)}, u32[]{:S(2)}) copy-start(bf16[2048,1024]{1,0:T(8,128)(2,1)} %get-tuple-element.41) | copy-start | bytes 12582916
  188.3 4.8 %copy-start.19 = (bf16[1024,1024]{1,0:T(8,128)(2,1)S(1)}, bf16[1024,1024]{1,0:T(8,128)(2,1)}, u32[]{:S(2)}) copy-start(bf16[1024,1024]{1,0:T(8,128)(2,1)} %get-tuple-element.40) | copy-start | bytes 6291460
  193.1 2.4 copy-start.15
  195.5 2.4 copy-start.5
  195.5 2.4 copy-start.22
  197.9 3.8 copy-start.18
  197.9 3.8 copy-start.21
  201.7 3.7 copy-start.14
  201.7 3.7 copy-start.20
  201.7 8.1 %slice-start = ((s8[8388608]{0:T(1024)(128)(4,1)}), s8[4194304]{0:T(1024)(128)(4,1)S(1)}, s32[]{:S(2)}) async-start(s8[8388608]{0:T(1024)(128)(4,1)} %bitcast.55), calls=%async_computation.2 | async-start | bytes 8388608
  205.3 4.4 slice-start.1
  425.0 5.2 %copy-start.1 = (bf16[1,1024,1024]{2,1,0:T(8,128)(2,1)S(1)}, bf16[1,1024,1024]{2,1,0:T(8,128)(2,1)}, u32[]{:S(2)}) copy-start(bf16[1,1024,1024]{2,1,0:T(8,128)(2,1)} %param.18) | copy-start | bytes 6291460
  425.0 5.3 %copy-start.3 = (f32[1024,1024]{1,0:T(8,128)S(1)}, f32[1024,1024]{1,0:T(8,128)}, u32[]{:S(2)}) copy-start(f32[1024,1024]{1,0:T(8,128)} %get-tuple-element.54) | copy-start | bytes 12582916
  425.0 5.9 %copy-start.6 = (bf16[1,1024,1024]{2,1,0:T(8,128)(2,1)S(1)}, bf16[1,1024,1024]{2,1,0:T(8,128)(2,1)}, u32[]{:S(2)}) copy-start(bf16[1,1024,1024]{2,1,0:T(8,128)(2,1)} %param.28) | copy-start | bytes 6291460
  430.9 4.9 %copy-start.7 = (bf16[1024,1024]{1,0:T(8,128)(2,1)S(1)}, bf16[1024,1024]{1,0:T(8,128)(2,1)}, u32[]{:S(2)}) copy-start(bf16[1024,1024]{1,0:T(8,128)(2,1)} %get-tuple-element.53) | copy-start | bytes 6291460
  435.8 1.6 copy-start.10
  435.8 2.5 copy-start.11
  435.8 3.2 copy-start.9
  435.8 4.2 copy-start.8
Sparse Core Ops, SparseCore 0:
  97.8 77.9 all-gather.2
  177.9 73.1 all-gather.4

commit v5 on v4

--- a/solution.py
+++ b/solution.py
@@ -480,14 +480,14 @@
             grad_turned, mixed.reshape(2 * tokens, 3 * width), d_att, prior, vec)
 
 
-RING = 12
+RING = 6
 SLOTS = 6
 
 
 def reduce_kernel(dims, g_q, g_k, g_v, g_out, normed, normed_t, grad, grad_t, x_ref, w_in, w_back, b_in, base_out, base_dn,
-                  vec_in, o_qkv, o_out, o_in, o_back, o_vec, block_out, d_normed,
+                  vec_in, gain_in, returned, o_qkv, o_out, o_in, o_back, o_vec, block_out, d_normed,
                   buf, core_recv, chip, x_recv, y_recv, part, z_recv, fin, fin_recv, res, acc_out, hidden, d_pre, win_buf, wback_buf,
-                  vec, vec_recv, load_sem, acc_sem, w_sem, send_sem, recv_sem, zsend_sem, zrecv_sem, vsend_sem, vrecv_sem):
+                  came, vec, vec_recv, came_sem, load_sem, acc_sem, w_sem, send_sem, recv_sem, zsend_sem, zrecv_sem, vsend_sem, vrecv_sem):
     rows, seqs, q_rows, edge, tokens, width, ff = dims
     bf, f32 = jnp.bfloat16, jnp.float32
     levels = rows // 4
@@ -515,6 +515,8 @@
     n_qkv, n_out, n_in, n_back = 3 * width // 512, width // 512, ff // 512, width // 128
     n_first = n_qkv + n_out
     n_mlp = n_first + n_in
+    assert n_first == n_in
+    ready = lambda k: (k < n_mlp) & (lax.rem(k, 2) == 0)
     total = n_mlp + n_back
     own_rows = pl.ds(pl.multiple_of(odd * edge, edge), region)
     c_mine = pl.ds(pl.multiple_of(odd * (q_rows - edge), edge), edge)
@@ -551,9 +553,9 @@
 
     def load(k):
         for i, source in enumerate((g_q, g_k, g_v, g_out)):
-            @pl.when((k >= i * n_out) & (k < (i + 1) * n_out))
+            @pl.when(ready(k) & (k // 2 >= i * n_out) & (k // 2 < (i + 1) * n_out))
             def _():
-                for copy in load_copies(source, (k - i * n_out) * 512, k):
+                for copy in load_copies(source, (k // 2 - i * n_out) * 512, k):
                     copy.start()
 
     def weights(j):
@@ -601,7 +603,7 @@
             return sums + jnp.sum(down.astype(f32), axis=0, keepdims=True)
         sums = lax.fori_loop(0, tokens // tall, rows_step, jnp.zeros((1, 512), f32))
         vec[pl.ds(3 + j // 2, 1), pl.ds(pl.multiple_of(lax.rem(j, 2) * 512, 512), 512)] = sums
-        slot = lax.rem(n_first + j, RING)
+        slot = lax.rem(2 * j + 1, RING)
         per = 8
         big = per * width // rows
 
@@ -614,26 +616,43 @@
             return 0
         lax.fori_loop(0, rows // per, grads_step, 0)
 
-    def finish_tokens():
-        gain = vec_in[0:1, :]
-        bias = vec_in[1:2, :]
-        back = jnp.zeros((1, width), f32)
-        tall = 256
-        def step(i, sums):
+    tall_end = tokens // 4
+
+    def returned_copy(i):
+        return pltpu.make_async_copy(returned.at[pl.ds(pl.multiple_of(i * tall_end, tall_end), tall_end)], came, came_sem)
+
+    def finish_tokens(i):
+        @pl.when(i == 0)
+        def _():
+            returned_copy(0).start()
+            vec[0:2, :] = vec_in[...]
+            vec[2:3, :] = jnp.zeros((1, width), f32)
+            vec[7:8, :] = jnp.zeros((1, width), f32)
+        returned_copy(i).wait()
+        small = tall_end // 4
+
+        def part(n, sums):
             gain, bias, back = sums
-            block = pl.ds(pl.multiple_of(i * tall, tall), tall)
+            block = pl.ds(pl.multiple_of(i * tall_end + n * small, small), small)
             block_out[block, :] = acc_out[block, :].astype(bf)
             values = x_ref[block, :].astype(f32)
             centered = values - jnp.mean(values, axis=1, keepdims=True)
-            unit = centered * lax.rsqrt(jnp.mean(centered * centered, axis=1, keepdims=True) + EPS)
+            scale = lax.rsqrt(jnp.mean(centered * centered, axis=1, keepdims=True) + EPS)
+            unit = centered * scale
             d = d_normed[block, :]
+            g = grad[block, :].astype(f32)
+            d_unit = (d + came[pl.ds(pl.multiple_of(n * small, small), small), :].astype(f32)) * gain_in[...]
+            inner = jnp.mean(d_unit * unit, axis=1, keepdims=True)
+            d_normed[block, :] = g + (d_unit - jnp.mean(d_unit, axis=1, keepdims=True) - unit * inner) * scale
             return (gain + jnp.sum(d * unit, axis=0, keepdims=True), bias + jnp.sum(d, axis=0, keepdims=True),
-                    back + jnp.sum(grad[block, :].astype(f32), axis=0, keepdims=True))
-        gain, bias, back = lax.fori_loop(0, tokens // tall, step, (gain, bias, back))
-        vec[0:1, :] = gain
-        vec[1:2, :] = bias
-        vec[2:3, :] = back
-        vec[7:8, :] = jnp.zeros((1, width), f32)
+                    back + jnp.sum(g, axis=0, keepdims=True))
+        sums = lax.fori_loop(0, 4, part, (vec[0:1, :], vec[1:2, :], vec[2:3, :]))
+        for row in range(3):
+            vec[row:row + 1, :] = sums[row]
+
+        @pl.when(i < 3)
+        def _():
+            returned_copy(i + 1).start()
 
     def back_grads(j):
         value = dot_n(grad_t[pl.ds(pl.multiple_of(j * 128, 128), 128), :], hidden[...]).astype(bf)
@@ -654,17 +673,17 @@
             for j in range(4):
                 out[:, pl.ds(pl.multiple_of(col + 128 * j, 128), 128)] = res[j * piece:(j + 1) * piece, :]
 
-        @pl.when(k < n_qkv)
-        def _():
-            place(o_qkv, k * 512)
-
-        @pl.when((k >= n_qkv) & (k < n_first))
-        def _():
-            place(o_out, (k - n_qkv) * 512)
-
-        @pl.when((k >= n_first) & (k < n_mlp))
-        def _():
-            place(o_in, (k - n_first) * 512)
+        @pl.when(ready(k) & (k < 2 * n_qkv))
+        def _():
+            place(o_qkv, (k // 2) * 512)
+
+        @pl.when(ready(k) & (k >= 2 * n_qkv))
+        def _():
+            place(o_out, (k // 2 - n_qkv) * 512)
+
+        @pl.when((k < n_mlp) & (lax.rem(k, 2) == 1))
+        def _():
+            place(o_in, (k // 2) * 512)
 
         @pl.when(k >= n_mlp)
         def _():
@@ -680,7 +699,7 @@
             body(k, lax.rem(k, SLOTS))
 
     def send_first(k, t):
-        @pl.when(k < n_first)
+        @pl.when(ready(k))
         def _():
             for copy in load_copies(g_q, 0, k):
                 copy.wait()
@@ -740,17 +759,20 @@
         for lag, body in enumerate(pipeline):
             stage(2 * lag, it, body)
 
-        @pl.when(it < n_in)
-        def _():
-            mlp(it)
-
-        @pl.when(it == n_in)
-        def _():
-            finish_tokens()
+        @pl.when((it < n_mlp) & (lax.rem(it, 2) == 0))
+        def _():
+            mlp(it // 2)
+
+        @pl.when((it >= n_mlp - 1) & (it < n_mlp + 3))
+        def _():
+            finish_tokens(it - (n_mlp - 1))
+
+        @pl.when(it == n_mlp + 2)
+        def _():
             for i, target in vec_stages[0]:
                 vec_copy(i, target).start()
         for number, stages in enumerate(vec_stages):
-            @pl.when(it == n_in + 1 + number)
+            @pl.when(it == n_mlp + 4 + 2 * number)
             def _():
                 for i, target in stages:
                     vec_copy(i, target).wait()
@@ -764,14 +786,15 @@
                 else:
                     o_vec[...] = value
 
-        @pl.when((it >= n_in) & (it < n_in + n_back))
-        def _():
-            back_grads(it - n_in)
+        @pl.when((it >= n_mlp - 1) & (it < total - 1))
+        def _():
+            back_grads(it - (n_mlp - 1))
         return 0
     lax.fori_loop(0, total + 2 * len(pipeline) - 2, step, 0)
 
 
-def reduce_all(rows, seqs, g_q, g_k, g_v, g_out, normed, normed_t, grad, grad_t, x, w_in, w_back, b_in, base_out, base_dn, vec_in):
+def reduce_all(rows, seqs, g_q, g_k, g_v, g_out, normed, normed_t, grad, grad_t, x, w_in, w_back, b_in, base_out, base_dn, vec_in, gain,
+               returned):
     tokens, width = normed.shape
     ff = w_in.shape[1]
     share = width // rows
@@ -789,7 +812,7 @@
                    jax.ShapeDtypeStruct((share, ff), f32), jax.ShapeDtypeStruct((ff // rows, width), f32),
                    jax.ShapeDtypeStruct((8, width), f32), jax.ShapeDtypeStruct((tokens, width), bf),
                    jax.ShapeDtypeStruct((tokens, width), f32)],
-        in_specs=[hbm, hbm, hbm, hbm, vmem, vmem, vmem, vmem, vmem, hbm, hbm, vmem, hbm, hbm, vmem],
+        in_specs=[hbm, hbm, hbm, hbm, vmem, vmem, vmem, vmem, vmem, hbm, hbm, vmem, hbm, hbm, vmem, vmem, hbm],
         out_specs=[vmem] * 7,
         scratch_shapes=[
             pltpu.VMEM((RING, rows // 2, 2, q_rows, 128), bf),
@@ -807,8 +830,10 @@
             pltpu.VMEM((tokens, 512), bf),
             pltpu.VMEM((2, width, 512), bf),
             pltpu.VMEM((2, 512, width), bf),
+            pltpu.VMEM((tokens // 4, width), bf),
             pltpu.VMEM((8, width), f32),
             pltpu.VMEM((1 + levels + finals, 8, width), f32),
+            dma,
             dma((4,)), dma((2,)), dma((2, 2)), dma((3 + finals, SLOTS)), dma((3 + finals, SLOTS)),
             dma((levels - 1, SLOTS)), dma((levels - 1, SLOTS)), dma((1 + levels + finals,)), dma((1 + levels + finals,)),
         ],
@@ -816,7 +841,7 @@
         cost_estimate=pl.CostEstimate(flops=100 * 10**9, bytes_accessed=100 * 2**20, transcendentals=0),
         name="reduce",
     )(*[g.reshape(rows // 2, 2, share, width) for g in (g_q, g_k, g_v, g_out)], normed, normed_t, grad, grad_t, x,
-      w_in, w_back, b_in, base_out, base_dn, vec_in)
+      w_in, w_back, b_in, base_out, base_dn, vec_in, gain, returned)
 
 
 def body(block_input, lengths, norm_gain, norm_bias, w_qkv, w_attn_out, w_fc_in, b_fc_in, w_fc_out, b_fc_out, cotangent):
@@ -850,7 +875,6 @@
     w_back_all = lax.all_gather(w_fc_out, "rows", axis=0, tiled=True)
     gain, bias, b_back_all = vectors[0], vectors[1], vectors[2]
     b_in_all = vectors[3:7].reshape(1, 4 * width)
-    unit, scale = layer_norm_stats(inputs)
     prior_unit, _ = layer_norm_stats(prior_input.astype(f32))
     attended, attended_turned, d_q, d_k, d_v = attention(lows, starts, cosine, sine, mixed, d_attended)
 
@@ -867,15 +891,10 @@
     base_dn = d_normed_both[tokens:] + jnp.dot(d_q, w_qkv_all[:, :width].T, preferred_element_type=f32)
     base_out = inputs + jnp.dot(attended, w_out_all, preferred_element_type=f32) + b_back_all
 
-    g_qkv, g_out, g_in, g_back, vec, block_output, d_normed = reduce_all(
+    g_qkv, g_out, g_in, g_back, vec, block_output, grad_input = reduce_all(
         rows, seqs, *grads, grad_w_out, normed, turned_own, grad_out, grad_turned, block_input[0], w_in_all, w_back_all,
-        b_in_all, base_out, base_dn, vec_in)
-
-    d_normed = d_normed + back.astype(f32)
-    d_unit = d_normed * gain
-    d_input = (d_unit - jnp.mean(d_unit, axis=1, keepdims=True)
-               - unit * jnp.mean(d_unit * unit, axis=1, keepdims=True)) * scale
-    grad_input = d_input + grad_out.astype(f32)
+        b_in_all, base_out, base_dn, vec_in, gain[None], back)
+
     own = lambda vector, size: lax.dynamic_slice_in_dim(vector, r * size, size)
     return (block_output[None], grad_input[None], own(vec[0], share), own(vec[1], share), g_qkv, g_out, g_in,
             own(vec[3:7].reshape(4 * width), wide), g_back, own(vec[2], share))

time: 452 us -> 431 us (0.954); the launches traced: 448 us -> 433 us
  other arithmetic: 27.6 us -> 17.3 us
  Pallas kernels: 316 us -> 308 us
    pallas_call x1, Pallas kernels: 171 us -> 151 us  [reduce_all(): pl.pallas_call(functools.partial(reduce_kernel, (rows, seqs, q_rows, edge...]
    pallas_call x1, Pallas kernels: 77.6 us -> 89.7 us  [gather_all(): pl.pallas_call(functools.partial(gather_kernel, (rows, seqs, tokens, widt...]
    all_gather x1, waiting for transfers between devices: 27.5 us -> 15.7 us  [body(): w_back_all = lax.all_gather(w_fc_out, 'rows', axis=0, tiled=True)]
    ppermute x1, waiting for transfers between devices: 0.01 us -> 11.3 us  [body(): lax.ppermute(d_prior.astype(bf), 'seq', [(i + 1, i) for i in range(seqs -...]
    broadcast_in_dim x1 -> x0, other arithmetic: 4.9 us -> none  [body(): grad_input[None]]
    unnamed x59 -> x54, local copies, waits for them, and re-layouts: 10.6 us -> 14.4 us
  transfers between devices with their start and end apart: 3 -> 3, of which waited for: 1 -> 2; matrix products, arithmetic and copies ran while one was open for 12% -> 12% of each run, Pallas kernels for 53% -> 16%
where the time goes in v5:
time: 431 us; the launch traced here: 433 us
  Pallas kernels  308 us (71%)
  matrix products  43.7 us (10%)
  waiting for transfers between devices  27.8 us (6%)
  local copies, waits for them, and re-layouts  20.4 us (5%)
  other arithmetic  17.3 us (4%)
  between operations  14.5 us (3%)
    pallas_call x1, Pallas kernels, reduce_all(): pl.pallas_call(functools.partial(reduce_kernel, (rows, seqs, q_rows, edge...  151 us
    pallas_call x1, Pallas kernels, gather_all(): pl.pallas_call(functools.partial(gather_kernel, (rows, seqs, tokens, widt...  89.7 us
    pallas_call x1, Pallas kernels, attention(): pl.pallas_call(functools.partial(attention_kernel, pairs, tokens), out_sh...  67.8 us
    dot_general x6, matrix products, body(): jnp.dot(turned, values, preferred_element_type=f32)  19.6 us
    all_gather x1, waiting for transfers between devices, body(): w_back_all = lax.all_gather(w_fc_out, 'rows', axis=0, tiled=True)  15.7 us
    unnamed x54, local copies, waits for them, and re-layouts  14.4 us
    ppermute x1, waiting for transfers between devices, body(): lax.ppermute(d_prior.astype(bf), 'seq', [(i + 1, i) for i in range(seqs -...  11.3 us
  transfers between devices with their start and end apart: 3, of which 2 were waited for; matrix products, arithmetic and copies ran while one was open for 12% of the time, Pallas kernels for 16%

profile of v5, /device:TPU:0, one launch (start us, length us, event | category | flops | bytes accessed | tf_op | source)
XLA Modules:
  0.0 433.2 jit_solution(1627046692344334046)
XLA Ops:
  7.2 0.0 all-gather.3.cloned.1.call-start
  7.2 0.7 convert_element_type.40
  7.9 0.7 convert_element_type.41
  8.5 0.7 convert_element_type.42
  9.2 0.7 compare_select_fusion.1
  9.9 0.1 reshape.89
  10.0 0.1 reshape.90
  10.1 0.1 reshape.91
  10.1 0.7 convert_element_type.43
  10.8 0.7 compare_select_fusion
  11.5 0.8 select_reduce_fusion.1
  12.3 0.7 select_reduce_fusion
  13.1 6.2 %fusion.24 = (f32[2048,128]{1,0:T(8,128)}, f32[2048,128]{1,0:T(8,128)}) fusion(f32[128]{0:T(128)} %constant.66, f32[128]{0:T(128)} %constant.65, f32[2048]{0:T(1024)S(1)} %subtract_convert_fusion), kind=kLoop, calls=%fused_computation.31 | loop fusion | flops 524288 | bytes 2106368 | tf_op jit(solution)/shard_map/mul | solution.py:197
  19.3 0.7 concatenate.3.vec_own
  20.0 89.7 %gather.1 = (bf16[4,2,2,64,1024]{4,3,2,1,0:T(8,128)(2,1)}, bf16[4,2,2,64,3072]{4,3,2,1,0:T(8,128)(2,1)}, bf16[1024,1024]{1,0:T(8,128)(2,1)}, bf16[1024,1024]{1,0...) custom-call(bf16[64,1024]{1,0:T(8,128)(2,1)} %w_out.1, ...), custom_call_target="tpu_custom_call" | custom-call | flops 20000000000 | bytes 41943040 | tf_op jit(solution)/shard_map/gather/pallas_call | solution.py:461
  109.7 0.0 all-gather.3.cloned.1.call-update
  109.7 0.0 all-gather.5.cloned.1.call-start
  109.8 0.7 all-gather.5.cloned.1.call-update
  110.5 0.0 copy-start.8
  110.5 0.1 slice.55
  110.6 0.5 and_select_fusion.lows
  111.1 0.0 copy-done.8
  111.1 67.8 %attention.1 = (bf16[1024,1024]{1,0:T(8,128)(2,1)}, bf16[1024,1024]{1,0:T(8,128)(2,1)}, bf16[1024,1024]{1,0:T(8,128)(2,1)}, bf16[2048,1024]{1,0:T(8,128)(2,1)}, bf16[2048,1024]{1,0:T(8,128)(2,1)}) custom-call(s32[4]{0:T(128)} %and_select_fusion.lows, s32[1,1024]{1,0:T(1,128)} %bitcast.54, f32[2048,128]{1,0:T(8,128)} %get-tuple-element.68.cos_ref, ...), custom_call_target="tpu_custom_call" | custom-call | flops 60000002048 | bytes 31457280 | tf_op jit(solution)/shard_map/attention/pallas_call | solution.py:172
  178.9 7.3 %fusion.8 = f32[2048,1024]{1,0:T(8,128)S(1)} fusion(bf16[2048,1024]{1,0:T(8,128)(2,1)} %get-tuple-element.39, bf16[1024,3072]{1,0:T(8,128)(2,1)} %bitcast.65), kind=kOutput, calls=%fused_computation.17 | convolution fusion | flops 4294967296 | bytes 14680064 | tf_op jit(solution)/shard_map/dot_general | solution.py:881
  186.2 6.4 %convolution_add_fusion = f32[2048,1024]{1,0:T(8,128)S(1)} fusion(f32[2048,1024]{1,0:T(8,128)S(1)} %fusion.8, bf16[2048,1024]{1,0:T(8,128)(2,1)S(1)} %copy-done.13, bf16[1024,3072]{1,0:T(8,128)(2,1)} %bitcast.66), kind=kOutput, calls=%fused_computation.11 | convolution fusion | flops 4297064448 | bytes 23068672 | tf_op jit(solution)/shard_map/dot_general | solution.py:881
  192.5 0.0 copy-start.1
  192.6 3.2 copy-done.1
  195.8 1.7 slice.107
  197.5 1.3 collective-permute-start
  198.8 0.6 copy.28
  199.5 0.3 convert_reduce_fusion
  199.8 0.7 fusion.2
  200.5 0.6 fusion.31
  201.1 3.3 fusion.4
  204.4 0.2 copy-done.14
  204.6 0.7 copy-done.16
  205.3 2.3 fusion.10
  207.7 2.3 fusion.14
  210.1 0.0 copy-start.9
  210.1 0.0 copy-start.17
  210.1 0.0 slice-start
  210.1 3.7 convolution_convert_fusion.1
  213.8 0.0 copy-done.9
  213.8 4.4 %add_add_fusion.base_out = f32[1024,1024]{1,0:T(8,128)} fusion(f32[1024]{0:T(1024)S(1)} %bitcast.55, bf16[1024,1024]{1,0:T(8,128)(2,1)S(1)} %copy-done.17, bf16[1024,1024]{1,0:T(8,128)(2,1)S(1)} %bitcast.68, bf16[1,1024,1024]{2,1,0:T(8,128)(2,1)S(1)} %copy-done.9), kind=kOutput, calls=%fused_computation.8 | convolution fusion | flops 2150629376 | bytes 10489856 | tf_op jit(solution)/shard_map/dot_general | solution.py:892
  218.2 6.1 %slice_add_fusion.base_dn = f32[1024,1024]{1,0:T(8,128)} fusion(f32[2048,1024]{1,0:T(8,128)S(1)} %bitcast.47, bf16[1024,1024]{1,0:T(8,128)(2,1)S(1)} %copy-done.15, bf16[1024,3072]{1,0:T(8,128)(2,1)} %bitcast.67), kind=kOutput, calls=%fused_computation.7 | convolution fusion | flops 2148532224 | bytes 12582912 | tf_op jit(solution)/shard_map/dot_general | solution.py:891
  224.3 0.6 pad_maximum_fusion.vec_in
  224.9 0.0 copy-done.10
  224.9 3.6 convolution_convert_fusion
  228.6 3.9 add_convert_fusion
  232.4 3.7 add_convert_fusion.1
  236.1 11.3 %collective-permute-done.returned = bf16[1024,1024]{1,0:T(8,128)(2,1)} collective-permute-done((bf16[1024,1024]{1,0:T(8,128)(2,1)}, bf16[1024,1024]{1,0:T(8,128)(2,1)}, u32[]{:S(2)}, u32[]{:S(2)}) %collective-permute-start) | collective-permute-done | bytes 2097184 | tf_op jit(solution)/shard_map/ppermute | solution.py:884
  247.5 15.7 %all-gather.5.cloned.1.call-done.w_back = bf16[4096,1024]{1,0:T(8,128)(2,1)} async-done(((bf16[256,1024]{1,0:T(8,128)(2,1)}), bf16[4096,1024]{1,0:T(8,128)(2,1)}) %all-gather.5.cloned.1.call-update) | async-done | bytes 8388624 | tf_op jit(solution)/shard_map/all_gather | solution.py:875
  263.2 150.8 %reduce.1 = (f32[64,3072]{1,0:T(8,128)}, f32[64,1024]{1,0:T(8,128)}, f32[64,4096]{1,0:T(8,128)}, f32[256,1024]{1,0:T(8,128)}, f32[8,1024]{1,0:T(8,128)}, /*index...) custom-call(bf16[8,2,64,1024]{3,2,1,0:T(8,128)(2,1)} %bitcast.69, bf16[8,2,64,1024]{3,2,1,0:T(8,128)(2,1)} %bitcast.72, ...), custom_call_target="tpu_custom_call" | custom-call | flops 99999997952 | bytes 104857600 | tf_op jit(solution)/shard_map/reduce/pallas_call | solution.py:809
  414.0 0.9 fusion.30
  414.8 0.8 slice_bitcast_fusion
  415.6 0.6 fusion.28
  416.2 0.6 fusion.26
  416.8 0.6 dynamic_slice.22
  417.4 3.2 copy.38
  420.7 2.0 copy.39
  422.7 0.9 copy.40
  423.6 0.7 copy.41
  424.3 1.0 copy.42
  425.2 1.0 copy.43
  (44 shorter events, 0.1 us)
Async XLA Ops:
  7.2 240.3 %all-gather.3.cloned.1.call-start = ((), (), s32[]{:S(2)}) async-start(), calls=%async_computation | async-start | bytes 8912896 | tf_op jit(solution)/shard_map/all_gather | solution.py:874
  109.7 153.4 %all-gather.5.cloned.1.call-start = ((), (), s32[]{:S(2)}) async-start(), calls=%async_computation.1 | async-start | bytes 8912896 | tf_op jit(solution)/shard_map/all_gather | solution.py:875
  110.5 0.6 copy-start.8
  178.9 7.3 %copy-start.13 = (bf16[2048,1024]{1,0:T(8,128)(2,1)S(1)}, bf16[2048,1024]{1,0:T(8,128)(2,1)}, u32[]{:S(2)}) copy-start(bf16[2048,1024]{1,0:T(8,128)(2,1)} %get-tuple-element.41) | copy-start | bytes 12582916
  192.5 3.3 copy-start.1
  195.8 3.0 copy-start.7
  195.8 3.7 copy-start
  197.5 49.9 %collective-permute-start = (bf16[1024,1024]{1,0:T(8,128)(2,1)}, bf16[1024,1024]{1,0:T(8,128)(2,1)}, u32[]{:S(2)}, u32[]{:S(2)}) collective-permute-start(bf16[1024,1024]{1,0:T(8,128)(2,1)} %slice.107), channel_id=1, source_target_pairs={{1,0},{3,2},{5,4},{7,6},{9,8},{11,10},{13,12},{15,14},{17,16},{19,... | collective-permute-start | bytes 6291464 | tf_op jit(solution)/shard_map/ppermute | solution.py:884
  201.1 3.5 copy-start.14
  201.1 4.2 copy-start.16
  205.3 2.4 copy-start.12
  207.7 2.4 copy-start.15
  207.7 2.4 copy-start.18
  210.1 3.7 copy-start.9
  210.1 3.7 copy-start.11
  210.1 3.7 copy-start.17
  210.1 8.1 %slice-start = ((s8[8388608]{0:T(1024)(128)(4,1)}), s8[4194304]{0:T(1024)(128)(4,1)S(1)}, s32[]{:S(2)}) async-start(s8[8388608]{0:T(1024)(128)(4,1)} %bitcast.46), calls=%async_computation.2 | async-start | bytes 8388608
  213.8 4.4 %slice-start.1 = ((s8[8388608]{0:T(1024)(128)(4,1)}), s8[4194304]{0:T(1024)(128)(4,1)S(1)}, s32[]{:S(2)}) async-start(s8[8388608]{0:T(1024)(128)(4,1)} %bitcast.46), calls=%async_computation.3 | async-start | bytes 8388608
  218.2 6.7 %copy-start.10 = (bf16[1,1024,1024]{2,1,0:T(8,128)(2,1)S(1)}, bf16[1,1024,1024]{2,1,0:T(8,128)(2,1)}, u32[]{:S(2)}) copy-start(bf16[1,1024,1024]{2,1,0:T(8,128)(2,1)} %param.28) | copy-start | bytes 6291460
  218.2 6.7 %copy-start.19 = (bf16[1024,1024]{1,0:T(8,128)(2,1)S(1)}, bf16[1024,1024]{1,0:T(8,128)(2,1)}, u32[]{:S(2)}) copy-start(bf16[1024,1024]{1,0:T(8,128)(2,1)} %get-tuple-element.42) | copy-start | bytes 6291460
  417.4 3.2 copy-start.2
  420.6 2.0 copy-start.5
  420.7 2.9 copy-start.6
  422.7 1.6 copy-start.4
  422.7 2.6 copy-start.3
Sparse Core Ops, SparseCore 0:
  109.9 77.9 all-gather.2
  190.0 73.1 all-gather.4

commit v6 on v5

--- a/solution.py
+++ b/solution.py
@@ -189,14 +189,6 @@
     )(lows, starts[None, :], cosine, sine, mixed, mixed, mixed, d_out)
 
 
-def rope_tables(position):
-    lane = np.arange(128) % HEAD
-    freqs = np.where(lane < ROT, 10000.0 ** (-2.0 * (lane // 2) / ROT), 0.0).astype(np.float32)
-    sign = np.where(lane % 2 == 0, -1.0, 1.0).astype(np.float32)
-    angles = position.astype(jnp.float32)[:, None] * freqs[None, :]
-    return jnp.cos(angles), jnp.sin(angles) * sign[None, :]
-
-
 def layer_norm_stats(values):
     mean = jnp.mean(values, axis=1, keepdims=True)
     centered = values - mean
@@ -209,9 +201,9 @@
 AHEAD = 3
 
 
-def gather_kernel(dims, w_out, w_qkv, x_hbm, grad, vec_own, cos_ref, sin_ref,
-                  wout_all, wqkv_all, normed_own, normed_prior, turned_own, turned_prior, grad_turned, mixed_all, d_attended, prior_all, vec_all,
-                  wbuf, own, prior, normed, turned, mixed, d_att, vec, vec_recv, in_sem, load_sem, out_sem, zsend, zrecv, ysend, yrecv,
+def gather_kernel(dims, w_out, w_qkv, x_hbm, grad, vec_own, lengths, freqs,
+                  wout_all, wqkv_all, normed_own, normed_prior, turned_own, turned_prior, grad_turned, mixed_all, d_attended, prior_all, cos_all, sin_all, vec_all,
+                  wbuf, own, prior, normed, turned, mixed, d_att, cos_ref, sin_ref, vec, vec_recv, in_sem, load_sem, out_sem, zsend, zrecv, ysend, yrecv,
                   csend, crecv, psend, precv, vsend, vrecv):
     rows, seqs, tokens, width = dims
     bf, f32 = jnp.bfloat16, jnp.float32
@@ -381,6 +373,18 @@
             prior_copy(i).wait_send()
             prior_copy(i + 2).start()
 
+    def angles(i):
+        block = slice(i * quarter, (i + 1) * quarter)
+        index = (s - 1) * tokens + i * quarter + lax.broadcasted_iota(jnp.int32, (quarter, 128), 0)
+        begin = jnp.zeros_like(index)
+        end = jnp.int32(0)
+        for j in range(lengths.shape[1]):
+            end = end + lengths[0, j]
+            begin = begin + jnp.where(end <= index, lengths[0, j], 0)
+        angle = (index - begin).astype(f32) * freqs[0:1, :]
+        cos_ref[block, :] = jnp.cos(angle)
+        sin_ref[block, :] = jnp.sin(angle) * freqs[1:2, :]
+
     for it in range(total + 2):
         if it < total:
             for d in range(1, levels):
@@ -392,6 +396,12 @@
             y_copy(it - 1, 1 - y).wait_recv()
             core_copy(it - 1, core).start()
         share_vectors(it)
+        if it < 4:
+            angles(2 * it)
+            angles(2 * it + 1)
+        if it == 4:
+            send_out(cos_ref, cos_all)
+            send_out(sin_ref, sin_all)
         if it == 3:
             fetch.wait()
         if 3 <= it <= 4:
@@ -449,7 +459,14 @@
         copy.wait()
 
 
-def gather_all(rows, seqs, w_out, w_qkv, x, grad, vec_own, cosine, sine):
+def rope_rows():
+    lane = np.arange(128) % HEAD
+    freqs = np.where(lane < ROT, 10000.0 ** (-2.0 * (lane // 2) / ROT), 0.0)
+    sign = np.where(lane % 2 == 0, -1.0, 1.0)
+    return np.concatenate([freqs[None], sign[None], np.zeros((6, 128))]).astype(np.float32)
+
+
+def gather_all(rows, seqs, w_out, w_qkv, x, grad, vec_own, lengths):
     tokens, width = x.shape
     share, levels = width // rows, rows // 4
     bf, f32 = jnp.bfloat16, jnp.float32
@@ -458,16 +475,18 @@
     total = 4 * width // CHUNK
     shape = jax.ShapeDtypeStruct
     token, turned = shape((tokens, width), bf), shape((width, tokens), bf)
-    wout_all, wqkv_all, normed, normed_prior, turned_own, turned_prior, grad_turned, mixed, d_att, prior, vec = pl.pallas_call(
+    wout_all, wqkv_all, normed, normed_prior, turned_own, turned_prior, grad_turned, mixed, d_att, prior, cosine, sine, vec = pl.pallas_call(
         functools.partial(gather_kernel, (rows, seqs, tokens, width)),
         out_shape=[shape((levels, 2, 2, share, width), bf), shape((levels, 2, 2, share, 3 * width), bf), token, token,
-                   turned, turned, turned, shape((2, tokens, 3 * width), bf), token, token, shape((8, width), f32)],
-        in_specs=[hbm, hbm, hbm, vmem, vmem, vmem, vmem],
-        out_specs=[hbm] * 10 + [vmem],
+                   turned, turned, turned, shape((2, tokens, 3 * width), bf), token, token,
+                   shape((2 * tokens, 128), f32), shape((2 * tokens, 128), f32), shape((8, width), f32)],
+        in_specs=[hbm, hbm, hbm, vmem, vmem, pl.BlockSpec(memory_space=pltpu.SMEM), vmem],
+        out_specs=[hbm] * 12 + [vmem],
         scratch_shapes=[
             pltpu.VMEM((total, levels, 2, 2, share, CHUNK), bf),
             pltpu.VMEM((tokens, width), bf), pltpu.VMEM((tokens, width), bf), pltpu.VMEM((2, tokens, width), bf), pltpu.VMEM((3, width, tokens), bf),
             pltpu.VMEM((2, tokens, 3 * width), bf), pltpu.VMEM((tokens, width), bf),
+            pltpu.VMEM((2 * tokens, 128), f32), pltpu.VMEM((2 * tokens, 128), f32),
             pltpu.VMEM((3, 8, width), f32), pltpu.VMEM((1 + levels, 8, width), f32),
             dma, dma((total,)), dma((5 * total,)), dma((total, levels - 1)), dma((total, levels - 1)),
             dma((total,)), dma((total,)), dma((total,)), dma((total,)), dma((4,)), dma((4,)), dma((1 + levels,)), dma((1 + levels,)),
@@ -475,19 +494,19 @@
         compiler_params=pltpu.CompilerParams(collective_id=0, has_side_effects=True, vmem_limit_bytes=60 * 2**20),
         cost_estimate=pl.CostEstimate(flops=20 * 10**9, bytes_accessed=40 * 2**20, transcendentals=0),
         name="gather",
-    )(w_out, w_qkv, x, grad, vec_own, cosine, sine)
+    )(w_out, w_qkv, x, grad, vec_own, lengths, rope_rows())
     return (wout_all.reshape(width, width), wqkv_all.reshape(width, 3 * width), normed, normed_prior, turned_own, turned_prior,
-            grad_turned, mixed.reshape(2 * tokens, 3 * width), d_att, prior, vec)
+            grad_turned, mixed.reshape(2 * tokens, 3 * width), d_att, prior, cosine, sine, vec)
 
 
 RING = 6
 SLOTS = 6
 
 
-def reduce_kernel(dims, g_q, g_k, g_v, g_out, normed, normed_t, grad, grad_t, x_ref, w_in, w_back, b_in, base_out, base_dn,
-                  vec_in, gain_in, returned, o_qkv, o_out, o_in, o_back, o_vec, block_out, d_normed,
+def reduce_kernel(dims, g_q, g_k, g_v, g_out, normed, normed_t_hbm, grad, grad_t_hbm, x_hbm, w_in, w_back, b_in, base_out, base_dn,
+                  vec_in, gain_in, returned, o_qkv, o_out, o_in, o_back, o_vec, block_hbm, input_hbm,
                   buf, core_recv, chip, x_recv, y_recv, part, z_recv, fin, fin_recv, res, acc_out, hidden, d_pre, win_buf, wback_buf,
-                  came, vec, vec_recv, came_sem, load_sem, acc_sem, w_sem, send_sem, recv_sem, zsend_sem, zrecv_sem, vsend_sem, vrecv_sem):
+                  normed_t, grad_t, x_ref, block_out, d_normed, came, vec, vec_recv, late_sem, done_sem, came_sem, load_sem, acc_sem, w_sem, send_sem, recv_sem, zsend_sem, zrecv_sem, vsend_sem, vrecv_sem):
     rows, seqs, q_rows, edge, tokens, width, ff = dims
     bf, f32 = jnp.bfloat16, jnp.float32
     levels = rows // 4
@@ -565,44 +584,49 @@
                 pltpu.make_async_copy(w_back.at[cols, :], wback_buf.at[t], w_sem.at[1, t])]
 
     starts = [pltpu.make_async_copy(base_out, acc_out, acc_sem.at[0]), pltpu.make_async_copy(base_dn, d_normed, acc_sem.at[1])]
-    for copy in weights(0) + starts:
+    late = [pltpu.make_async_copy(normed_t_hbm, normed_t, late_sem.at[0]), pltpu.make_async_copy(x_hbm, x_ref, late_sem.at[1]),
+            pltpu.make_async_copy(grad_t_hbm, grad_t, late_sem.at[2])]
+    for copy in weights(0) + starts + late:
         copy.start()
     load(0)
 
-    def mlp(j):
-        @pl.when(j == 0)
-        def _():
-            for copy in starts:
-                copy.wait()
-        for copy in weights(j):
-            copy.wait()
-
-        @pl.when(j + 1 < n_in)
-        def _():
-            for copy in weights(j + 1):
-                copy.start()
+    def mlp_rows(j, i):
         t = lax.rem(j, 2)
         cols = pl.ds(pl.multiple_of(j * 512, 512), 512)
-        tall = 512
-        bias = b_in[:, cols]
-
-        def rows_step(i, sums):
-            block = pl.ds(pl.multiple_of(i * tall, tall), tall)
-            pre = dot_n(normed[block, :], win_buf[t]) + bias
-            up = dot_t(grad[block, :], wback_buf[t])
-            square = pre * pre
-            turn = jnp.tanh(pre * (GELU_COEF + (GELU_COEF * 0.044715) * square))
-            half = 0.5 + 0.5 * turn
-            hid = (pre * half).astype(bf)
-            slope = half + (0.5 * pre) * (1.0 - turn * turn) * (GELU_COEF + (3 * 0.044715 * GELU_COEF) * square)
-            down = (up * slope).astype(bf)
-            hidden[block, cols] = hid
-            d_pre[block, :] = down
-            acc_out[block, :] += dot_n(hid, wback_buf[t])
-            d_normed[block, :] += dot_t(down, win_buf[t])
-            return sums + jnp.sum(down.astype(f32), axis=0, keepdims=True)
-        sums = lax.fori_loop(0, tokens // tall, rows_step, jnp.zeros((1, 512), f32))
-        vec[pl.ds(3 + j // 2, 1), pl.ds(pl.multiple_of(lax.rem(j, 2) * 512, 512), 512)] = sums
+        tall = tokens // 2
+        block = slice(i * tall, (i + 1) * tall)
+        if i == 0:
+            @pl.when(j == 0)
+            def _():
+                for copy in starts:
+                    copy.wait()
+            for copy in weights(j):
+                copy.wait()
+
+            @pl.when(j + 1 < n_in)
+            def _():
+                for copy in weights(j + 1):
+                    copy.start()
+        pre = dot_n(normed[block, :], win_buf[t]) + b_in[:, cols]
+        up = dot_t(grad[block, :], wback_buf[t])
+        square = pre * pre
+        turn = jnp.tanh(pre * (GELU_COEF + (GELU_COEF * 0.044715) * square))
+        half = 0.5 + 0.5 * turn
+        hid = (pre * half).astype(bf)
+        slope = half + (0.5 * pre) * (1.0 - turn * turn) * (GELU_COEF + (3 * 0.044715 * GELU_COEF) * square)
+        down = (up * slope).astype(bf)
+        hidden[block, cols] = hid
+        d_pre[block, :] = down
+        acc_out[block, :] += dot_n(hid, wback_buf[t])
+        d_normed[block, :] += dot_t(down, win_buf[t])
+        sums = jnp.sum(down.astype(f32), axis=0, keepdims=True)
+        place = (pl.ds(3 + j // 2, 1), pl.ds(pl.multiple_of(lax.rem(j, 2) * 512, 512), 512))
+        vec[place] = sums if i == 0 else vec[place] + sums
+
+    def mlp_grads(j):
+        @pl.when(j == 0)
+        def _():
+            late[0].wait()
         slot = lax.rem(2 * j + 1, RING)
         per = 8
         big = per * width // rows
@@ -620,6 +644,11 @@
 
     def returned_copy(i):
         return pltpu.make_async_copy(returned.at[pl.ds(pl.multiple_of(i * tall_end, tall_end), tall_end)], came, came_sem)
+
+    def done_copies(i):
+        block = pl.ds(i * tall_end if isinstance(i, int) else pl.multiple_of(i * tall_end, tall_end), tall_end)
+        return [pltpu.make_async_copy(block_out.at[block], block_hbm.at[block], done_sem.at[0, i]),
+                pltpu.make_async_copy(d_normed.at[block], input_hbm.at[block], done_sem.at[1, i])]
 
     def finish_tokens(i):
         @pl.when(i == 0)
@@ -649,6 +678,8 @@
         sums = lax.fori_loop(0, 4, part, (vec[0:1, :], vec[1:2, :], vec[2:3, :]))
         for row in range(3):
             vec[row:row + 1, :] = sums[row]
+        for copy in done_copies(i):
+            copy.start()
 
         @pl.when(i < 3)
         def _():
@@ -761,7 +792,17 @@
 
         @pl.when((it < n_mlp) & (lax.rem(it, 2) == 0))
         def _():
-            mlp(it // 2)
+            mlp_rows(it // 2, 1)
+            mlp_grads(it // 2)
+
+        @pl.when((it < n_mlp - 1) & (lax.rem(it, 2) == 1))
+        def _():
+            mlp_rows(it // 2 + 1, 0)
+
+        @pl.when(it == n_mlp - 1)
+        def _():
+            for copy in late[1:]:
+                copy.wait()
 
         @pl.when((it >= n_mlp - 1) & (it < n_mlp + 3))
         def _():
@@ -790,7 +831,11 @@
         def _():
             back_grads(it - (n_mlp - 1))
         return 0
+    mlp_rows(jnp.int32(0), 0)
     lax.fori_loop(0, total + 2 * len(pipeline) - 2, step, 0)
+    for i in range(4):
+        for copy in done_copies(i):
+            copy.wait()
 
 
 def reduce_all(rows, seqs, g_q, g_k, g_v, g_out, normed, normed_t, grad, grad_t, x, w_in, w_back, b_in, base_out, base_dn, vec_in, gain,
@@ -812,8 +857,8 @@
                    jax.ShapeDtypeStruct((share, ff), f32), jax.ShapeDtypeStruct((ff // rows, width), f32),
                    jax.ShapeDtypeStruct((8, width), f32), jax.ShapeDtypeStruct((tokens, width), bf),
                    jax.ShapeDtypeStruct((tokens, width), f32)],
-        in_specs=[hbm, hbm, hbm, hbm, vmem, vmem, vmem, vmem, vmem, hbm, hbm, vmem, hbm, hbm, vmem, vmem, hbm],
-        out_specs=[vmem] * 7,
+        in_specs=[hbm, hbm, hbm, hbm, vmem, hbm, vmem, hbm, hbm, hbm, hbm, vmem, hbm, hbm, vmem, vmem, hbm],
+        out_specs=[vmem] * 5 + [hbm] * 2,
         scratch_shapes=[
             pltpu.VMEM((RING, rows // 2, 2, q_rows, 128), bf),
             pltpu.VMEM((SLOTS, rows // 2, q_rows, 128), bf),
@@ -830,10 +875,15 @@
             pltpu.VMEM((tokens, 512), bf),
             pltpu.VMEM((2, width, 512), bf),
             pltpu.VMEM((2, 512, width), bf),
+            pltpu.VMEM((width, tokens), bf),
+            pltpu.VMEM((width, tokens), bf),
+            pltpu.VMEM((tokens, width), bf),
+            pltpu.VMEM((tokens, width), bf),
+            pltpu.VMEM((tokens, width), f32),
             pltpu.VMEM((tokens // 4, width), bf),
             pltpu.VMEM((8, width), f32),
             pltpu.VMEM((1 + levels + finals, 8, width), f32),
-            dma,
+            dma((3,)), dma((2, 4)), dma,
             dma((4,)), dma((2,)), dma((2, 2)), dma((3 + finals, SLOTS)), dma((3 + finals, SLOTS)),
             dma((levels - 1, SLOTS)), dma((levels - 1, SLOTS)), dma((1 + levels + finals,)), dma((1 + levels + finals,)),
         ],
@@ -852,12 +902,11 @@
     own_lengths = lengths[0]
     count = own_lengths.shape[0]
     first = lax.axis_index("seq") * tokens
-    index = first - tokens + jnp.arange(2 * tokens, dtype=jnp.int32)
+    index = first + jnp.arange(tokens, dtype=jnp.int32)
     order = np.arange(count)
     ends = jnp.sum(jnp.where(order[None, :] <= order[:, None], own_lengths[None, :], 0), axis=1)
     begin = jnp.sum(jnp.where(ends[None, :] <= index[:, None], own_lengths[None, :], 0), axis=1)
-    cosine, sine = rope_tables(index - begin)
-    starts = (begin - first + tokens)[tokens:]
+    starts = begin - first + tokens
     lows = starts[::BQ] // BQ
 
     share, wide = width // rows, 4 * width // rows
@@ -868,8 +917,8 @@
                                jnp.zeros((1, width), f32)])
     grad_out = cotangent[0]
     (w_out_all, w_qkv_all, normed, normed_prior, turned_own, turned_prior, grad_turned, mixed, d_attended, prior_input,
-     vectors) = gather_all(
-        rows, seqs, w_attn_out, w_qkv, block_input[0], grad_out, vec_own, cosine, sine)
+     cosine, sine, vectors) = gather_all(
+        rows, seqs, w_attn_out, w_qkv, block_input[0], grad_out, vec_own, lengths)
     w_fc_in, w_fc_out, vectors = lax.optimization_barrier((w_fc_in, w_fc_out, vectors))
     w_in_all = lax.all_gather(w_fc_in, "rows", axis=0, tiled=True)
     w_back_all = lax.all_gather(w_fc_out, "rows", axis=0, tiled=True)

time: 431 us -> 415 us (0.963); the launches traced: 433 us -> 407 us
  Pallas kernels: 308 us -> 292 us
  other arithmetic: 17.3 us -> 9.76 us
    ppermute x1, waiting for transfers between devices: 11.3 us -> 0.01 us  [body(): lax.ppermute(d_prior.astype(bf), 'seq', [(i + 1, i) for i in range(seqs -...]
    pallas_call x1, Pallas kernels: 89.7 us -> 78.6 us  [gather_all(): pl.pallas_call(functools.partial(gather_kernel, (rows, seqs, tokens, widt...]
    all_gather x1, waiting for transfers between devices: 15.7 us -> 24.8 us  [body(): w_back_all = lax.all_gather(w_fc_out, 'rows', axis=0, tiled=True)]
    mul x1 -> x0, other arithmetic: 6.23 us -> none  [rope_tables(): return (jnp.cos(angles), jnp.sin(angles) * sign[None, :])]
    pallas_call x1, Pallas kernels: 151 us -> 146 us  [reduce_all(): pl.pallas_call(functools.partial(reduce_kernel, (rows, seqs, q_rows, edge...]
    unnamed x54 -> x58, local copies, waits for them, and re-layouts: 14.4 us -> 14.3 us
  transfers between devices with their start and end apart: 3 -> 3, of which waited for: 2 -> 1; matrix products, arithmetic and copies ran while one was open for 12% -> 13% of each run, Pallas kernels for 16% -> 17%
where the time goes in v6:
time: 415 us; the launch traced here: 407 us
  Pallas kernels  292 us (70%)
  matrix products  43.7 us (11%)
  waiting for transfers between devices  25.5 us (6%)
  local copies, waits for them, and re-layouts  20.3 us (5%)
  between operations  14.5 us (3%)
  other arithmetic  9.76 us (2%)
    pallas_call x1, Pallas kernels, reduce_all(): pl.pallas_call(functools.partial(reduce_kernel, (rows, seqs, q_rows, edge...  146 us
    pallas_call x1, Pallas kernels, gather_all(): pl.pallas_call(functools.partial(gather_kernel, (rows, seqs, tokens, widt...  78.6 us
    pallas_call x1, Pallas kernels, attention(): pl.pallas_call(functools.partial(attention_kernel, pairs, tokens), out_sh...  67.8 us
    all_gather x1, waiting for transfers between devices, body(): w_back_all = lax.all_gather(w_fc_out, 'rows', axis=0, tiled=True)  24.8 us
    dot_general x6, matrix products, body(): jnp.dot(turned, values, preferred_element_type=f32)  19.6 us
    unnamed x58, local copies, waits for them, and re-layouts  14.3 us
  transfers between devices with their start and end apart: 3, of which 1 were waited for; matrix products, arithmetic and copies ran while one was open for 13% of the time, Pallas kernels for 17%

profile of v6, /device:TPU:0, one launch (start us, length us, event | category | flops | bytes accessed | tf_op | source)
XLA Modules:
  0.0 407.2 jit_solution(11022291255350056769)
XLA Ops:
  7.2 0.0 all-gather.3.cloned.1.call-start
  7.2 0.7 convert_element_type.33
  7.9 0.7 convert_element_type.34
  8.5 0.7 convert_element_type.35
  9.2 0.7 compare_select_fusion.1
  9.9 0.1 reshape.97
  10.0 0.1 reshape.98
  10.1 0.1 reshape.99
  10.1 0.7 convert_element_type.36
  10.8 0.7 compare_select_fusion
  11.5 0.7 concatenate.3.vec_own
  12.2 78.6 %gather.1 = (bf16[4,2,2,64,1024]{4,3,2,1,0:T(8,128)(2,1)}, bf16[4,2,2,64,3072]{4,3,2,1,0:T(8,128)(2,1)}, bf16[1024,1024]{1,0:T(8,128)(2,1)}, bf16[1024,1024]{1,0...) custom-call(bf16[64,1024]{1,0:T(8,128)(2,1)} %w_out.1, ...), custom_call_target="tpu_custom_call" | custom-call | flops 20000000000 | bytes 41943040 | tf_op jit(solution)/shard_map/gather/pallas_call | solution.py:478
  90.8 0.0 all-gather.3.cloned.1.call-update
  90.8 0.0 all-gather.5.cloned.1.call-start
  90.9 0.7 all-gather.5.cloned.1.call-update
  91.6 0.0 copy-done.9
  91.6 0.0 copy-done.13
  91.6 0.1 select_reduce_fusion.1
  91.8 0.1 select_reduce_fusion
  91.9 0.0 copy-start.8
  91.9 0.1 slice.51
  92.0 0.5 and_select_fusion.lows
  92.5 67.8 %attention.1 = (bf16[1024,1024]{1,0:T(8,128)(2,1)}, bf16[1024,1024]{1,0:T(8,128)(2,1)}, bf16[1024,1024]{1,0:T(8,128)(2,1)}, bf16[2048,1024]{1,0:T(8,128)(2,1)}, bf16[2048,1024]{1,0:T(8,128)(2,1)}) custom-call(s32[4]{0:T(128)} %and_select_fusion.lows, s32[1,1024]{1,0:T(1,128)} %bitcast.54, f32[2048,128]{1,0:T(8,128)} %get-tuple-element.38.cos_ref, ...), custom_call_target="tpu_custom_call" | custom-call | flops 60000002048 | bytes 31457280 | tf_op jit(solution)/shard_map/attention/pallas_call | solution.py:172
  160.3 7.3 %fusion.8 = f32[2048,1024]{1,0:T(8,128)S(1)} fusion(bf16[2048,1024]{1,0:T(8,128)(2,1)} %get-tuple-element.43, bf16[1024,3072]{1,0:T(8,128)(2,1)} %bitcast.65), kind=kOutput, calls=%fused_computation.17 | convolution fusion | flops 4294967296 | bytes 14680064 | tf_op jit(solution)/shard_map/dot_general | solution.py:930
  167.6 6.3 %convolution_add_fusion = f32[2048,1024]{1,0:T(8,128)S(1)} fusion(f32[2048,1024]{1,0:T(8,128)S(1)} %fusion.8, bf16[2048,1024]{1,0:T(8,128)(2,1)S(1)} %copy-done.15, bf16[1024,3072]{1,0:T(8,128)(2,1)} %bitcast.66), kind=kOutput, calls=%fused_computation.11 | convolution fusion | flops 4297064448 | bytes 23068672 | tf_op jit(solution)/shard_map/dot_general | solution.py:930
  173.8 0.0 copy-start.1
  173.8 3.2 copy-done.1
  177.1 1.7 slice.99
  178.8 1.3 collective-permute-start
  180.1 0.6 copy.27
  180.7 0.3 convert_reduce_fusion
  181.1 0.7 fusion.2
  181.8 0.6 fusion.29
  182.4 3.3 fusion.4
  185.7 0.2 copy-done.16
  185.9 0.7 copy-done.18
  186.6 2.3 fusion.10
  189.0 2.3 fusion.14
  191.3 0.0 copy-start.10
  191.4 0.0 copy-start.19
  191.4 0.0 slice-start
  191.4 3.7 convolution_convert_fusion.1
  195.1 0.0 copy-done.10
  195.1 0.0 copy-done.19
  195.1 4.4 %add_add_fusion.base_out = f32[1024,1024]{1,0:T(8,128)} fusion(f32[1024]{0:T(1024)S(1)} %bitcast.55, bf16[1024,1024]{1,0:T(8,128)(2,1)S(1)} %copy-done.19, bf16[1024,1024]{1,0:T(8,128)(2,1)S(1)} %bitcast.68, bf16[1,1024,1024]{2,1,0:T(8,128)(2,1)S(1)} %copy-done.10), kind=kOutput, calls=%fused_computation.8 | convolution fusion | flops 2150629376 | bytes 10489856 | tf_op jit(solution)/shard_map/dot_general | solution.py:941
  199.5 6.2 %slice_add_fusion.base_dn = f32[1024,1024]{1,0:T(8,128)} fusion(f32[2048,1024]{1,0:T(8,128)S(1)} %bitcast.47, bf16[1024,1024]{1,0:T(8,128)(2,1)S(1)} %copy-done.17, bf16[1024,3072]{1,0:T(8,128)(2,1)} %bitcast.67), kind=kOutput, calls=%fused_computation.7 | convolution fusion | flops 2148532224 | bytes 12582912 | tf_op jit(solution)/shard_map/dot_general | solution.py:940
  205.7 0.6 pad_maximum_fusion.vec_in
  206.3 3.7 convolution_convert_fusion
  209.9 3.9 add_convert_fusion
  213.8 3.7 add_convert_fusion.1
  217.5 0.0 collective-permute-done.returned
  217.5 24.8 %all-gather.5.cloned.1.call-done.w_back = bf16[4096,1024]{1,0:T(8,128)(2,1)} async-done(((bf16[256,1024]{1,0:T(8,128)(2,1)}), bf16[4096,1024]{1,0:T(8,128)(2,1)}) %all-gather.5.cloned.1.call-update) | async-done | bytes 8388624 | tf_op jit(solution)/shard_map/all_gather | solution.py:924
  242.3 145.6 %reduce.1 = (f32[64,3072]{1,0:T(8,128)}, f32[64,1024]{1,0:T(8,128)}, f32[64,4096]{1,0:T(8,128)}, f32[256,1024]{1,0:T(8,128)}, f32[8,1024]{1,0:T(8,128)}, /*index...) custom-call(bf16[8,2,64,1024]{3,2,1,0:T(8,128)(2,1)} %bitcast.69, bf16[8,2,64,1024]{3,2,1,0:T(8,128)(2,1)} %bitcast.72, ...), custom_call_target="tpu_custom_call" | custom-call | flops 99999997952 | bytes 104857600 | tf_op jit(solution)/shard_map/reduce/pallas_call | solution.py:854
  387.9 0.9 fusion.28
  388.8 0.8 slice_bitcast_fusion
  389.6 0.6 fusion.26
  390.1 0.6 fusion.24
  390.7 0.6 dynamic_slice.22
  391.4 3.2 copy.37
  394.6 2.0 copy.38
  396.6 0.9 copy.39
  397.5 0.7 copy.40
  398.2 1.0 copy.41
  399.2 1.0 copy.42
  (46 shorter events, 0.1 us)
Async XLA Ops:
  7.2 210.3 %all-gather.3.cloned.1.call-start = ((), (), s32[]{:S(2)}) async-start(), calls=%async_computation | async-start | bytes 8912896 | tf_op jit(solution)/shard_map/all_gather | solution.py:923
  12.2 79.4 %copy-start.9 = (s32[1,4]{1,0:T(1,128)S(1)}, s32[1,4]{1,0:T(1,128)}, u32[]{:S(2)}) copy-start(s32[1,4]{1,0:T(1,128)} %lengths.1) | copy-start | bytes 52
  12.2 79.4 %copy-start.13 = (pred[4,4]{1,0:T(4,128)(4,1)S(1)}, pred[4,4]{1,0:T(4,128)(4,1)}, u32[]{:S(2)}) copy-start(pred[4,4]{1,0:T(4,128)(4,1)} %constant.53.clone) | copy-start | bytes 52
  90.8 151.4 %all-gather.5.cloned.1.call-start = ((), (), s32[]{:S(2)}) async-start(), calls=%async_computation.1 | async-start | bytes 8912896 | tf_op jit(solution)/shard_map/all_gather | solution.py:924
  91.9 0.6 copy-start.8
  160.3 7.3 %copy-start.15 = (bf16[2048,1024]{1,0:T(8,128)(2,1)S(1)}, bf16[2048,1024]{1,0:T(8,128)(2,1)}, u32[]{:S(2)}) copy-start(bf16[2048,1024]{1,0:T(8,128)(2,1)} %get-tuple-element.45) | copy-start | bytes 12582916
  173.8 3.3 copy-start.1
  177.1 3.0 copy-start.7
  177.1 3.7 copy-start
  178.8 38.7 %collective-permute-start = (bf16[1024,1024]{1,0:T(8,128)(2,1)}, bf16[1024,1024]{1,0:T(8,128)(2,1)}, u32[]{:S(2)}, u32[]{:S(2)}) collective-permute-start(bf16[1024,1024]{1,0:T(8,128)(2,1)} %slice.99), channel_id=1, source_target_pairs={{1,0},{3,2},{5,4},{7,6},{9,8},{11,10},{13,12},{15,14},{17,16},{19,... | collective-permute-start | bytes 6291464 | tf_op jit(solution)/shard_map/ppermute | solution.py:933
  182.4 3.5 copy-start.16
  182.4 4.2 %copy-start.18 = (bf16[1024,1024]{1,0:T(8,128)(2,1)S(1)}, bf16[1024,1024]{1,0:T(8,128)(2,1)}, u32[]{:S(2)}) copy-start(bf16[1024,1024]{1,0:T(8,128)(2,1)} %get-tuple-element.44) | copy-start | bytes 6291460
  186.6 2.4 copy-start.14
  188.9 2.4 copy-start.17
  188.9 2.4 copy-start.20
  191.3 3.7 copy-start.10
  191.3 3.7 copy-start.12
  191.4 3.7 copy-start.19
  191.4 8.1 %slice-start = ((s8[8388608]{0:T(1024)(128)(4,1)}), s8[4194304]{0:T(1024)(128)(4,1)S(1)}, s32[]{:S(2)}) async-start(s8[8388608]{0:T(1024)(128)(4,1)} %bitcast.46), calls=%async_computation.2 | async-start | bytes 8388608
  195.1 4.4 %slice-start.1 = ((s8[8388608]{0:T(1024)(128)(4,1)}), s8[4194304]{0:T(1024)(128)(4,1)S(1)}, s32[]{:S(2)}) async-start(s8[8388608]{0:T(1024)(128)(4,1)} %bitcast.46), calls=%async_computation.3 | async-start | bytes 8388608
  199.5 6.8 %copy-start.11 = (bf16[1,1024,1024]{2,1,0:T(8,128)(2,1)S(1)}, bf16[1,1024,1024]{2,1,0:T(8,128)(2,1)}, u32[]{:S(2)}) copy-start(bf16[1,1024,1024]{2,1,0:T(8,128)(2,1)} %param.27) | copy-start | bytes 6291460
  199.5 6.8 %copy-start.21 = (bf16[1024,1024]{1,0:T(8,128)(2,1)S(1)}, bf16[1024,1024]{1,0:T(8,128)(2,1)}, u32[]{:S(2)}) copy-start(bf16[1024,1024]{1,0:T(8,128)(2,1)} %get-tuple-element.46) | copy-start | bytes 6291460
  391.4 3.2 copy-start.2
  394.6 2.0 copy-start.5
  394.6 2.9 copy-start.6
  396.6 1.6 copy-start.4
  396.6 2.6 copy-start.3
Sparse Core Ops, SparseCore 0:
  91.0 75.8 all-gather.2
  169.0 73.2 all-gather.4

commit v7 on v6

--- a/solution.py
+++ b/solution.py
@@ -201,7 +201,7 @@
 AHEAD = 3
 
 
-def gather_kernel(dims, w_out, w_qkv, x_hbm, grad, vec_own, lengths, freqs,
+def gather_kernel(dims, w_out, w_qkv, x_hbm, grad, gain_own, bias_own, b_out_own, b_in_own, lengths, freqs,
                   wout_all, wqkv_all, normed_own, normed_prior, turned_own, turned_prior, grad_turned, mixed_all, d_attended, prior_all, cos_all, sin_all, vec_all,
                   wbuf, own, prior, normed, turned, mixed, d_att, cos_ref, sin_ref, vec, vec_recv, in_sem, load_sem, out_sem, zsend, zrecv, ysend, yrecv,
                   csend, crecv, psend, precv, vsend, vrecv):
@@ -274,7 +274,14 @@
         part = wbuf.at[k, :, :, side]
         return pltpu.make_async_remote_copy(part, part, csend.at[k], crecv.at[k], device_id=core_id, device_id_type=MESH)
 
-    vec[0] = vec_own[...]
+    vec[0] = jnp.zeros((8, width), f32)
+    for line, own_ref in ((0, gain_own), (1, bias_own), (2, b_out_own), (3, b_in_own)):
+        size = own_ref.shape[1]
+        lane = lax.broadcasted_iota(jnp.int32, (size, width), 1)
+        hot = jnp.where(lax.rem(lane, size) == lax.broadcasted_iota(jnp.int32, (size, width), 0), 1.0, 0.0).astype(bf)
+        value = dot_n(jnp.broadcast_to(own_ref[...], (16, size)), hot)[0:1, :]
+        inside = lane[0:1, :] // size == lax.rem(r, width // size)
+        vec[0, pl.ds(line + r * size // width, 1), :] = jnp.where(inside, value, 0.0)
     for d in range(1, levels):
         z_vec(d).start()
 
@@ -466,7 +473,7 @@
     return np.concatenate([freqs[None], sign[None], np.zeros((6, 128))]).astype(np.float32)
 
 
-def gather_all(rows, seqs, w_out, w_qkv, x, grad, vec_own, lengths):
+def gather_all(rows, seqs, w_out, w_qkv, x, grad, vectors, lengths):
     tokens, width = x.shape
     share, levels = width // rows, rows // 4
     bf, f32 = jnp.bfloat16, jnp.float32
@@ -480,7 +487,7 @@
         out_shape=[shape((levels, 2, 2, share, width), bf), shape((levels, 2, 2, share, 3 * width), bf), token, token,
                    turned, turned, turned, shape((2, tokens, 3 * width), bf), token, token,
                    shape((2 * tokens, 128), f32), shape((2 * tokens, 128), f32), shape((8, width), f32)],
-        in_specs=[hbm, hbm, hbm, vmem, vmem, pl.BlockSpec(memory_space=pltpu.SMEM), vmem],
+        in_specs=[hbm, hbm, hbm, vmem, vmem, vmem, vmem, vmem, pl.BlockSpec(memory_space=pltpu.SMEM), vmem],
         out_specs=[hbm] * 12 + [vmem],
         scratch_shapes=[
             pltpu.VMEM((total, levels, 2, 2, share, CHUNK), bf),
@@ -494,7 +501,7 @@
         compiler_params=pltpu.CompilerParams(collective_id=0, has_side_effects=True, vmem_limit_bytes=60 * 2**20),
         cost_estimate=pl.CostEstimate(flops=20 * 10**9, bytes_accessed=40 * 2**20, transcendentals=0),
         name="gather",
-    )(w_out, w_qkv, x, grad, vec_own, lengths, rope_rows())
+    )(w_out, w_qkv, x, grad, *[v[None] for v in vectors], lengths, rope_rows())
     return (wout_all.reshape(width, width), wqkv_all.reshape(width, 3 * width), normed, normed_prior, turned_own, turned_prior,
             grad_turned, mixed.reshape(2 * tokens, 3 * width), d_att, prior, cosine, sine, vec)
 
@@ -911,14 +918,10 @@
 
     share, wide = width // rows, 4 * width // rows
     r = lax.axis_index("rows")
-    place = lambda vector, lines: jnp.where(np.arange(lines * width).reshape(rows, -1) // (lines * share) == r,
-                                            vector.astype(f32)[None, :], 0.0).reshape(lines, width)
-    vec_own = jnp.concatenate([place(norm_gain, 1), place(norm_bias, 1), place(b_fc_out, 1), place(b_fc_in, 4),
-                               jnp.zeros((1, width), f32)])
     grad_out = cotangent[0]
     (w_out_all, w_qkv_all, normed, normed_prior, turned_own, turned_prior, grad_turned, mixed, d_attended, prior_input,
      cosine, sine, vectors) = gather_all(
-        rows, seqs, w_attn_out, w_qkv, block_input[0], grad_out, vec_own, lengths)
+        rows, seqs, w_attn_out, w_qkv, block_input[0], grad_out, (norm_gain, norm_bias, b_fc_out, b_fc_in), lengths)
     w_fc_in, w_fc_out, vectors = lax.optimization_barrier((w_fc_in, w_fc_out, vectors))
     w_in_all = lax.all_gather(w_fc_in, "rows", axis=0, tiled=True)
     w_back_all = lax.all_gather(w_fc_out, "rows", axis=0, tiled=True)
@@ -927,9 +930,8 @@
     prior_unit, _ = layer_norm_stats(prior_input.astype(f32))
     attended, attended_turned, d_q, d_k, d_v = attention(lows, starts, cosine, sine, mixed, d_attended)
 
-    d_normed_both = jnp.dot(d_k, w_qkv_all[:, width:2 * width].T, preferred_element_type=f32) + jnp.dot(
-        d_v, w_qkv_all[:, 2 * width:].T, preferred_element_type=f32)
-    d_prior = d_normed_both[:tokens]
+    w_k, w_v = w_qkv_all[:, width:2 * width].T, w_qkv_all[:, 2 * width:].T
+    d_prior = jnp.dot(d_k[:tokens], w_k, preferred_element_type=f32) + jnp.dot(d_v[:tokens], w_v, preferred_element_type=f32)
     back = lax.ppermute(d_prior.astype(bf), "seq", [(i + 1, i) for i in range(seqs - 1)])
     vec_in = jnp.stack([jnp.sum(d_prior * prior_unit, axis=0), jnp.sum(d_prior, axis=0)])
     product = lambda turned, values: jnp.dot(turned, values, preferred_element_type=f32)
@@ -937,7 +939,8 @@
              (product(turned_own, d_k[tokens:]) + product(turned_prior, d_k[:tokens])).astype(bf),
              (product(turned_own, d_v[tokens:]) + product(turned_prior, d_v[:tokens])).astype(bf)]
     grad_w_out = product(attended_turned, grad_out).astype(bf)
-    base_dn = d_normed_both[tokens:] + jnp.dot(d_q, w_qkv_all[:, :width].T, preferred_element_type=f32)
+    base_dn = (jnp.dot(d_k[tokens:], w_k, preferred_element_type=f32) + jnp.dot(d_v[tokens:], w_v, preferred_element_type=f32)
+               + jnp.dot(d_q, w_qkv_all[:, :width].T, preferred_element_type=f32))
     base_out = inputs + jnp.dot(attended, w_out_all, preferred_element_type=f32) + b_back_all
 
     g_qkv, g_out, g_in, g_back, vec, block_output, grad_input = reduce_all(

time: 415 us -> 410 us (0.988)
  other arithmetic: 9.76 us -> 3.97 us
  local copies, waits for them, and re-layouts: 20.3 us -> 15 us
  waiting for transfers between devices: 25.5 us -> 30 us
    dot_general x2 -> x4, matrix products: 13.5 us -> 19.7 us  [the longest x1 5.74 us: body(): jnp.dot(d_v[:tokens], w_v, preferred_element_type=f32)]
    all_gather x1, waiting for transfers between devices: 24.8 us -> 29.3 us  [body(): w_back_all = lax.all_gather(w_fc_out, 'rows', axis=0, tiled=True)]
where the time goes in v7:
time: 410 us; the launch traced here: 404 us
  Pallas kernels  293 us (71%)
  matrix products  46 us (11%)
  waiting for transfers between devices  30 us (7%)
  local copies, waits for them, and re-layouts  15 us (4%)
  between operations  14.6 us (4%)
    pallas_call x1, Pallas kernels, reduce_all(): pl.pallas_call(functools.partial(reduce_kernel, (rows, seqs, q_rows, edge...  146 us
    pallas_call x1, Pallas kernels, gather_all(): pl.pallas_call(functools.partial(gather_kernel, (rows, seqs, tokens, widt...  78.9 us
    pallas_call x1, Pallas kernels, attention(): pl.pallas_call(functools.partial(attention_kernel, pairs, tokens), out_sh...  68 us
    all_gather x1, waiting for transfers between devices, body(): w_back_all = lax.all_gather(w_fc_out, 'rows', axis=0, tiled=True)  29.3 us
    dot_general x6, matrix products, body(): jnp.dot(turned, values, preferred_element_type=f32)  19.6 us
    unnamed x58, local copies, waits for them, and re-layouts  10.5 us
  transfers between devices with their start and end apart: 3, of which 1 were waited for; matrix products, arithmetic and copies ran while one was open for 13% of the time, Pallas kernels for 17%

profile of v7, /device:TPU:0, one launch (start us, length us, event | category | flops | bytes accessed | tf_op | source)
XLA Modules:
  0.0 403.9 jit_solution(11379288703466563196)
XLA Ops:
  7.2 0.0 all-gather.3.cloned.1.call-start
  7.2 1.2 broadcast_in_dim.52.b_in_own
  8.4 78.9 %gather.1 = (bf16[4,2,2,64,1024]{4,3,2,1,0:T(8,128)(2,1)}, bf16[4,2,2,64,3072]{4,3,2,1,0:T(8,128)(2,1)}, bf16[1024,1024]{1,0:T(8,128)(2,1)}, bf16[1024,1024]{1,0...) custom-call(bf16[64,1024]{1,0:T(8,128)(2,1)} %w_out.1, ...), custom_call_target="tpu_custom_call" | custom-call | flops 20000000000 | bytes 41943040 | tf_op jit(solution)/shard_map/gather/pallas_call | solution.py:485
  87.3 0.0 copy-start
  87.3 0.0 all-gather.3.cloned.1.call-update
  87.4 0.0 all-gather.5.cloned.1.call-start
  87.4 0.7 all-gather.5.cloned.1.call-update
  88.1 0.0 copy-done.9
  88.1 0.0 copy-done.13
  88.1 0.1 select_reduce_fusion.1
  88.3 0.1 select_reduce_fusion
  88.4 0.0 copy-start.8
  88.4 0.1 slice.49
  88.5 1.9 convert_reduce_fusion
  90.4 0.5 and_select_fusion.lows
  90.9 0.0 copy-done
  90.9 0.7 fusion.2
  91.6 0.0 copy-done.8
  91.6 68.0 %attention.1 = (bf16[1024,1024]{1,0:T(8,128)(2,1)}, bf16[1024,1024]{1,0:T(8,128)(2,1)}, bf16[1024,1024]{1,0:T(8,128)(2,1)}, bf16[2048,1024]{1,0:T(8,128)(2,1)}, bf16[2048,1024]{1,0:T(8,128)(2,1)}) custom-call(s32[4]{0:T(128)} %and_select_fusion.lows, s32[1,1024]{1,0:T(1,128)} %bitcast.51, f32[2048,128]{1,0:T(8,128)} %get-tuple-element.38.cos_ref, ...), custom_call_target="tpu_custom_call" | custom-call | flops 60000002048 | bytes 31457280 | tf_op jit(solution)/shard_map/attention/pallas_call | solution.py:172
  159.7 0.0 copy-start.14
  159.7 4.9 %fusion.9 = f32[1024,1024]{1,0:T(8,128)S(1)} fusion(bf16[1024,3072]{1,0:T(8,128)(2,1)} %bitcast.67, bf16[2048,1024]{1,0:T(8,128)(2,1)} %get-tuple-element.43), kind=kOutput, calls=%fused_computation.18 | convolution fusion | flops 2147483648 | bytes 8388608 | tf_op jit(solution)/shard_map/dot_general | solution.py:934
  164.5 0.0 copy-done.1
  164.6 0.0 copy-done.14
  164.6 0.0 copy-start.7
  164.6 5.7 %fusion.4 = (f32[1024]{0:T(1024)S(1)}, f32[1024]{0:T(1024)S(1)}, bf16[1024,1024]{1,0:T(8,128)(2,1)}) fusion(bf16[1024,1024]{1,0:T(8,128)(2,1)S(1)} %copy-done.1, f32[1024]{0:T(1024)S(1)} %add_rsqrt_fusion, f32[1024]{0:T(1024)S(1)} %broadcast_multiply_fusion, f32[1024,1024]{1,0:T(8,128)S(1)} %fusion.9, bf16[1024,3072]{1,0:T(8,128)(2,1)} %bitcast.68, ...), kind=kOutput, calls=%fused_computation.6 | convolution fusion | flops 2155870208 | bytes 12599296 | tf_op jit(solution)/shard_map/dot_general | solution.py:934
  170.3 1.5 collective-permute-start
  171.8 0.6 copy.23
  172.4 0.6 pad_maximum_fusion.vec_in
  173.0 0.6 fusion.28
  173.6 4.7 %fusion.11 = f32[1024,1024]{1,0:T(8,128)S(1)} fusion(bf16[1024,3072]{1,0:T(8,128)(2,1)} %bitcast.69, bf16[2048,1024]{1,0:T(8,128)(2,1)} %get-tuple-element.43), kind=kOutput, calls=%fused_computation.20 | convolution fusion | flops 2147483648 | bytes 8388608 | tf_op jit(solution)/shard_map/dot_general | solution.py:942
  178.4 0.0 copy-start.16
  178.4 0.0 slice-start
  178.4 2.3 fusion.16
  180.8 0.0 slice-start.1
  180.8 0.0 copy-start.17
  180.8 2.3 fusion.21
  183.1 0.2 copy-done.17
  183.3 2.4 fusion.5
  185.7 0.0 copy-start.10
  185.7 0.0 copy-start.19
  185.7 3.7 convolution_convert_fusion.1
  189.4 0.0 copy-done.12
  189.4 4.4 %add_add_fusion.1.base_out = f32[1024,1024]{1,0:T(8,128)} fusion(f32[1024]{0:T(1024)S(1)} %bitcast.54, bf16[1024,1024]{1,0:T(8,128)(2,1)S(1)} %copy-done.19, bf16[1024,1024]{1,0:T(8,128)(2,1)S(1)} %bitcast.74, bf16[1,1024,1024]{2,1,0:T(8,128)(2,1)S(1)} %copy-done.10), kind=kOutput, calls=%fused_computation.8 | convolution fusion | flops 2150629376 | bytes 10489856 | tf_op jit(solution)/shard_map/dot_general | solution.py:944
  193.8 3.9 add_convert_fusion
  197.7 0.0 copy-done.20
  197.7 3.6 convolution_convert_fusion
  201.4 3.7 add_convert_fusion.1
  205.1 4.3 %add_add_fusion.base_dn = f32[1024,1024]{1,0:T(8,128)} fusion(f32[1024,1024]{1,0:T(8,128)S(1)} %fusion.5, f32[1024,1024]{1,0:T(8,128)S(1)} %fusion.11, bf16[1024,3072]{1,0:T(8,128)(2,1)S(1)} %bitcast.73, bf16[2048,1024]{1,0:T(8,128)(2,1)S(1)} %copy-done.15), kind=kOutput, calls=%fused_computation.7 | convolution fusion | flops 2149580800 | bytes 16777216 | tf_op jit(solution)/shard_map/dot_general | solution.py:942
  209.4 0.0 collective-permute-done.returned
  209.4 29.3 %all-gather.5.cloned.1.call-done.w_back = bf16[4096,1024]{1,0:T(8,128)(2,1)} async-done(((bf16[256,1024]{1,0:T(8,128)(2,1)}), bf16[4096,1024]{1,0:T(8,128)(2,1)}) %all-gather.5.cloned.1.call-update) | async-done | bytes 8388624 | tf_op jit(solution)/shard_map/all_gather | solution.py:927
  238.7 145.9 %reduce.1 = (f32[64,3072]{1,0:T(8,128)}, f32[64,1024]{1,0:T(8,128)}, f32[64,4096]{1,0:T(8,128)}, f32[256,1024]{1,0:T(8,128)}, f32[8,1024]{1,0:T(8,128)}, /*index...) custom-call(bf16[8,2,64,1024]{3,2,1,0:T(8,128)(2,1)} %bitcast.75, bf16[8,2,64,1024]{3,2,1,0:T(8,128)(2,1)} %bitcast.78, ...), custom_call_target="tpu_custom_call" | custom-call | flops 99999997952 | bytes 104857600 | tf_op jit(solution)/shard_map/reduce/pallas_call | solution.py:861
  384.6 0.9 fusion.27
  385.4 0.8 slice_bitcast_fusion
  386.2 0.6 fusion.25
  386.8 0.6 fusion.23
  387.4 0.6 dynamic_slice.22
  388.0 3.2 copy.33
  391.3 0.0 copy-done.2
  391.3 2.0 copy.34
  393.3 0.9 copy.35
  394.2 0.7 copy.36
  394.9 0.0 copy-done.4
  394.9 1.0 copy.37
  395.8 1.0 copy.38
  (35 shorter events, 0.1 us)
Async XLA Ops:
  7.2 202.2 %all-gather.3.cloned.1.call-start = ((), (), s32[]{:S(2)}) async-start(), calls=%async_computation | async-start | bytes 8912896 | tf_op jit(solution)/shard_map/all_gather | solution.py:926
  8.4 79.7 %copy-start.9 = (s32[1,4]{1,0:T(1,128)S(1)}, s32[1,4]{1,0:T(1,128)}, u32[]{:S(2)}) copy-start(s32[1,4]{1,0:T(1,128)} %lengths.1) | copy-start | bytes 52
  8.4 79.7 %copy-start.13 = (pred[4,4]{1,0:T(4,128)(4,1)S(1)}, pred[4,4]{1,0:T(4,128)(4,1)}, u32[]{:S(2)}) copy-start(pred[4,4]{1,0:T(4,128)(4,1)} %constant.48.clone) | copy-start | bytes 52
  87.3 3.6 copy-start
  87.4 151.3 %all-gather.5.cloned.1.call-start = ((), (), s32[]{:S(2)}) async-start(), calls=%async_computation.1 | async-start | bytes 8912896 | tf_op jit(solution)/shard_map/all_gather | solution.py:927
  88.4 3.3 copy-start.8
  159.6 4.9 %copy-start.1 = (bf16[1024,1024]{1,0:T(8,128)(2,1)S(1)}, bf16[1024,1024]{1,0:T(8,128)(2,1)}, u32[]{:S(2)}) copy-start(bf16[1024,1024]{1,0:T(8,128)(2,1)} %get-tuple-element.56) | copy-start | bytes 6291460
  159.7 4.9 %copy-start.14 = (bf16[2048,1024]{1,0:T(8,128)(2,1)S(1)}, bf16[2048,1024]{1,0:T(8,128)(2,1)}, u32[]{:S(2)}) copy-start(bf16[2048,1024]{1,0:T(8,128)(2,1)} %get-tuple-element.45) | copy-start | bytes 12582916
  164.6 7.2 %copy-start.7 = (f32[8,1024]{1,0:T(8,128)S(1)}, f32[8,1024]{1,0:T(8,128)}, u32[]{:S(2)}) copy-start(f32[8,1024]{1,0:T(8,128)} %get-tuple-element.52) | copy-start | bytes 98308
  170.3 39.1 %collective-permute-start = (bf16[1024,1024]{1,0:T(8,128)(2,1)}, bf16[1024,1024]{1,0:T(8,128)(2,1)}, u32[]{:S(2)}, u32[]{:S(2)}) collective-permute-start(bf16[1024,1024]{1,0:T(8,128)(2,1)} %get-tuple-element.66), channel_id=1, source_target_pairs={{1,0},{3,2},{5,4},{7,6},{9,8},{11,10},{13,12},{15,14},{17,16},{19,... | collective-permute-start | bytes 6291464 | tf_op jit(solution)/shard_map/ppermute | solution.py:935
  173.6 4.7 %copy-start.15 = (bf16[2048,1024]{1,0:T(8,128)(2,1)S(1)}, bf16[2048,1024]{1,0:T(8,128)(2,1)}, u32[]{:S(2)}) copy-start(bf16[2048,1024]{1,0:T(8,128)(2,1)} %get-tuple-element.45) | copy-start | bytes 12582916
  173.6 4.8 %copy-start.18 = (bf16[1024,1024]{1,0:T(8,128)(2,1)S(1)}, bf16[1024,1024]{1,0:T(8,128)(2,1)}, u32[]{:S(2)}) copy-start(bf16[1024,1024]{1,0:T(8,128)(2,1)} %get-tuple-element.37.normed_t_hbm) | copy-start | bytes 6291460
  178.4 2.4 copy-start.16
  178.4 4.7 %slice-start = ((s8[6291456]{0:T(1024)(128)(4,1)}), s8[4194304]{0:T(1024)(128)(4,1)S(1)}, s32[]{:S(2)}) async-start(s8[6291456]{0:T(1024)(128)(4,1)} %bitcast.70), calls=%async_computation.2 | async-start | bytes 8388608
  180.8 2.4 slice-start.1
  180.8 2.6 copy-start.17
  185.7 3.7 copy-start.10
  185.7 3.7 copy-start.12
  185.7 3.7 copy-start.19
  189.4 4.4 %copy-start.21 = (bf16[1024,1024]{1,0:T(8,128)(2,1)S(1)}, bf16[1024,1024]{1,0:T(8,128)(2,1)}, u32[]{:S(2)}) copy-start(bf16[1024,1024]{1,0:T(8,128)(2,1)} %get-tuple-element.44) | copy-start | bytes 6291460
  193.8 3.9 copy-start.11
  193.8 3.9 copy-start.20
  388.0 3.2 copy-start.2
  391.3 2.0 copy-start.5
  391.3 2.9 copy-start.6
  393.3 1.6 copy-start.4
  393.3 2.6 copy-start.3
Sparse Core Ops, SparseCore 0:
  87.5 75.8 all-gather.2
  165.5 73.1 all-gather.4
